TPU v7x, 256 devices: a whole 4x4x8 slice. The times are simulated.
256 devices in a mesh: gx: 8 (over z), gy: 4 (over x), gz: 8 (over y, core).
Axes of the slice: x: 4, y: 4, z: 8, core: 2. Of those that a mesh axis runs over, the one named last changes fastest.
Arguments:
- rhs_boxes: float32 [8, 128, 32768], P('gz', ('gx', 'gy')), may hold values from -18 to 18
- a_boxes: float32 [8, 128, 32768], P('gz', ('gx', 'gy')), may hold values from 0.05 to 0.5
- b_boxes: float32 [8, 128, 32768], P('gz', ('gx', 'gy')), may hold values from 0.2 to 2
- new_place: int32 [8, 128], P('gz', ('gx', 'gy')), may hold values from 0 to 127, as said below
Outputs:
- solution: float32 [512, 128, 512], P('gx', 'gy', 'gz')
- residual: float32 [512, 128, 512], P('gx', 'gy', 'gz')
Inputs may be any that keep to these rules, and one draw needn't show every extreme that they name: `new_place`: each entry is p = t * 4 + q: the box goes to device t of its layer (counted in the order of the gx+gy axes) at box position q. The entries of one layer are a permutation of its positions. The boxes of one device go to 4 different devices.
All inputs are finite; a program needn't handle non-finite values.
Results may differ from a plain program's by a relative error of at most 0.000079.
Values sent between devices are 32-bit elements; how exact they have to be, the bound alone decides.
No kernel may reach another device: no remote copies, remote signals or barrier semaphores. Data moves between devices by JAX's collectives and lax.ppermute only.
A program may use at most 192 MiB of HBM per device.

v0:
```python
import jax
import jax.numpy as jnp
from jax import lax
from jax.sharding import PartitionSpec as P

BOX_EDGE = 32
BOXES_Z = 2
SWEEPS = 1
COARSE_SWEEPS = 4


def with_halo(cells, sides, width):
    for axis, dim in sides:
        count = lax.axis_size(axis)
        ends = count - 1
        head = lax.slice_in_dim(cells, 0, width, axis=dim)
        tail = lax.slice_in_dim(cells, cells.shape[dim] - width, cells.shape[dim], axis=dim)
        cells = jnp.concatenate(
            [
                lax.ppermute(tail, axis, [(i, (i + 1) % count) for i in range(ends)]),
                cells,
                lax.ppermute(head, axis, [((i + 1) % count, i) for i in range(ends)]),
            ],
            axis=dim,
        )
    return cells


def stencil_sum(padded, across_x, across_y, across_z):
    summed = across_x[:-1] * padded[:-2, 1:-1, 1:-1] + across_x[1:] * padded[2:, 1:-1, 1:-1]
    summed = (
        summed
        + across_y[:, :-1] * padded[1:-1, :-2, 1:-1]
        + across_y[:, 1:] * padded[1:-1, 2:, 1:-1]
    )
    summed = (
        summed
        + across_z[:, :, :-1] * padded[1:-1, 1:-1, :-2]
        + across_z[:, :, 1:] * padded[1:-1, 1:-1, 2:]
    )
    return summed


def face_total(across_x, across_y, across_z):
    return (
        across_x[:-1]
        + across_x[1:]
        + across_y[:, :-1]
        + across_y[:, 1:]
        + across_z[:, :, :-1]
        + across_z[:, :, 1:]
    )


def checker(extent):
    return (
        lax.broadcasted_iota(jnp.int32, extent, 0)
        + lax.broadcasted_iota(jnp.int32, extent, 1)
        + lax.broadcasted_iota(jnp.int32, extent, 2)
    ) % 2


def fine_pad(values):
    return with_halo(values, (("gx", 0), ("gy", 1), ("gz", 2)), 1)


def coarse_pad(values):
    return with_halo(values, (("gx", 0), ("gy", 1), ("gz", 2)), 1)


def colour_sweeps(solution, source, coeffs, sweeps, padder):
    diagonal, across_x, across_y, across_z, weight = coeffs
    colour = checker(solution.shape)
    for repeat in range(sweeps):
        for current in (0, 1):
            padded = padder(solution)
            updated = (
                source + weight * stencil_sum(padded, across_x, across_y, across_z)
            ) / diagonal
            solution = jnp.where(colour == current, updated, solution)
    return solution


def misfit(solution, source, coeffs):
    diagonal, across_x, across_y, across_z, weight = coeffs
    padded = fine_pad(solution)
    return source - (
        diagonal * solution - weight * stencil_sum(padded, across_x, across_y, across_z)
    )


def restrict(values):
    size_x, size_y, size_z = values.shape
    return values.reshape(size_x // 2, 2, size_y // 2, 2, size_z // 2, 2).mean(axis=(1, 3, 5))


def coarse_faces(across_x, across_y, across_z):
    size_x, size_y, size_z = (across_x.shape[0] - 1, across_x.shape[1], across_x.shape[2])
    coarse_x = (
        across_x[0::2].reshape(size_x // 2 + 1, size_y // 2, 2, size_z // 2, 2).mean(axis=(2, 4))
    )
    coarse_y = (
        across_y[:, 0::2].reshape(size_x // 2, 2, size_y // 2 + 1, size_z // 2, 2).mean(axis=(1, 4))
    )
    coarse_z = (
        across_z[:, :, 0::2]
        .reshape(size_x // 2, 2, size_y // 2, 2, size_z // 2 + 1)
        .mean(axis=(1, 3))
    )
    return (coarse_x, coarse_y, coarse_z)


def prolong(values):
    size_x, size_y, size_z = values.shape
    spread = jnp.broadcast_to(values[:, None, :, None, :, None], (size_x, 2, size_y, 2, size_z, 2))
    return spread.reshape(2 * size_x, 2 * size_y, 2 * size_z)


def to_brick(boxes):
    shaped = boxes.reshape(2, BOXES_Z, BOX_EDGE, BOX_EDGE, BOX_EDGE)
    return shaped.transpose(0, 2, 3, 1, 4).reshape(2 * BOX_EDGE, BOX_EDGE, BOXES_Z * BOX_EDGE)


def body(rhs_boxes, a_boxes, b_boxes, new_place):
    members = lax.axis_size(("gx", "gy"))
    box_count = new_place.shape[1]
    capacity = 1
    slot_count = members * capacity
    target = new_place[0] // box_count
    position = new_place[0] % box_count
    send_slot = target * capacity
    chosen = (
        lax.broadcasted_iota(jnp.int32, (slot_count, box_count), 0) == send_slot[None, :]
    ).astype(jnp.int32)
    source = jnp.sum(chosen * lax.broadcasted_iota(jnp.int32, (slot_count, box_count), 1), axis=1)
    filled = jnp.sum(chosen, axis=1) > 0
    send_rhs = jnp.where(filled[:, None], rhs_boxes[0][source], 0.0)
    send_a = jnp.where(filled[:, None], a_boxes[0][source], 0.0)
    send_b = jnp.where(filled[:, None], b_boxes[0][source], 0.0)
    send_position = jnp.where(filled, position[source], -1)
    got_rhs, got_a, got_b, got_position = (
        lax.all_to_all(send_rhs, ("gx", "gy"), split_axis=0, concat_axis=0, tiled=True),
        lax.all_to_all(send_a, ("gx", "gy"), split_axis=0, concat_axis=0, tiled=True),
        lax.all_to_all(send_b, ("gx", "gy"), split_axis=0, concat_axis=0, tiled=True),
        lax.all_to_all(send_position, ("gx", "gy"), split_axis=0, concat_axis=0, tiled=True),
    )
    wanted = (
        lax.broadcasted_iota(jnp.int32, (box_count, slot_count), 0) == got_position[None, :]
    ).astype(jnp.int32)
    picked = jnp.sum(wanted * lax.broadcasted_iota(jnp.int32, (box_count, slot_count), 1), axis=1)
    rhs = to_brick(got_rhs[picked])
    acoef = to_brick(got_a[picked])
    bcoef = to_brick(got_b[picked])
    padded_b = with_halo(bcoef, (("gx", 0), ("gy", 1), ("gz", 2)), 1)
    across_x = 0.5 * (padded_b[1:, 1:-1, 1:-1] + padded_b[:-1, 1:-1, 1:-1])
    across_y = 0.5 * (padded_b[1:-1, 1:, 1:-1] + padded_b[1:-1, :-1, 1:-1])
    across_z = 0.5 * (padded_b[1:-1, 1:-1, 1:] + padded_b[1:-1, 1:-1, :-1])
    diagonal = acoef + 1.0 * face_total(across_x, across_y, across_z)

    def smooth(solution):
        return colour_sweeps(
            solution, rhs, (diagonal, across_x, across_y, across_z, 1.0), SWEEPS, fine_pad
        )

    fine_level = (diagonal, across_x, across_y, across_z, 1.0)
    smoothed = smooth(jnp.zeros_like(rhs))
    coarse_rhs = restrict(misfit(smoothed, rhs, fine_level))
    coarse_x, coarse_y, coarse_z = coarse_faces(across_x, across_y, across_z)
    coarse = (
        restrict(acoef) + 0.25 * face_total(coarse_x, coarse_y, coarse_z),
        coarse_x,
        coarse_y,
        coarse_z,
        0.25,
    )
    correction = colour_sweeps(
        jnp.zeros_like(coarse_rhs), coarse_rhs, coarse, COARSE_SWEEPS, coarse_pad
    )
    solution = smooth(smoothed + prolong(correction))
    return (solution, misfit(solution, rhs, fine_level))


def solution(mesh):
    return jax.shard_map(
        body,
        mesh=mesh,
        in_specs=(
            P("gz", ("gx", "gy"), None),
            P("gz", ("gx", "gy"), None),
            P("gz", ("gx", "gy"), None),
            P("gz", ("gx", "gy")),
        ),
        out_specs=(P("gx", "gy", "gz"), P("gx", "gy", "gz")),
        check_vma=False,
    )
```

profile of v0, /device:TPU:41, one launch (start us, length us, event | category | flops | bytes accessed | tf_op | source)
XLA Modules:
  0.0 1055.7 jit_solution(9891542501992414026)
XLA Ops:
  6.1 10.6 %all-to-all-start.1 = ((s32[32,1,1]{2,1,0:T(1,128)}), s32[32,1,1]{2,1,0:T(1,128)S(1)}, u32[]{:S(2)}, u32[]{:S(2)}) async-start(s32[32,1,1]{2,1,0:T(1,128)} %copy.200), calls=%async_computation.1 | async-start | bytes 32768 | tf_op jit(solution)/shard_map/all_to_all | solution.py:145
  28.0 9.6 bitcast_select_fusion.1
  37.5 8.5 copy.202
  46.1 10.0 all-to-all-start.2
  56.1 8.5 copy.214
  64.6 82.9 %all-to-all-done.2 = f32[32,1,32768]{2,1,0:T(1,128)} async-done(((f32[32,1,32768]{2,1,0:T(1,128)}), f32[32,1,32768]{2,1,0:T(1,128)}, u32[]{:S(2)}, u32[]{:S(2)}) %all-to-all-start.2) | async-done | bytes 4194336 | tf_op jit(solution)/shard_map/all_to_all | solution.py:144
  147.5 9.1 all-to-all-start.3
  156.5 8.5 copy.199
  165.0 83.5 %all-to-all-done.3 = f32[32,1,32768]{2,1,0:T(1,128)} async-done(((f32[32,1,32768]{2,1,0:T(1,128)}), f32[32,1,32768]{2,1,0:T(1,128)}, u32[]{:S(2)}, u32[]{:S(2)}) %all-to-all-start.3) | async-done | bytes 4194336 | tf_op jit(solution)/shard_map/all_to_all | solution.py:143
  248.5 9.4 all-to-all-start
  269.3 77.3 %collective-permute-done.2 = f32[1,32,64]{2,1,0:T(8,128)S(1)} collective-permute-done((f32[1,32,64]{2,1,0:T(8,128)S(1)}, f32[1,32,64]{2,1,0:T(8,128)S(1)}, u32[]{:S(2)}, u32[]{:S(2)}) %collective-permute-start.2) | collective-permute-done | bytes 8224 | tf_op jit(solution)/shard_map/ppermute | solution.py:20
  352.4 6.6 copy.264
  379.9 4.7 collective-permute-start.1
  390.3 6.6 copy.263
  409.7 6.6 copy.265
  433.3 5.4 collective-permute-start.5
  454.7 5.3 fusion.77
  463.3 5.0 collective-permute-start.12
  505.2 21.8 %reshape_reshape.3 = f32[32,2,16,2,32,2]{3,2,5,4,1,0:T(8,128)} reshape(f32[2,32,32,2,32]{2,4,3,1,0:T(8,128)} %bitcast.66) | data formatting | bytes 1048576 | tf_op jit(solution)/shard_map/reshape;reshape | solution.py:94
  527.0 12.2 %reduce_sum.85 = f32[32,16,32]{1,2,0:T(8,128)S(1)} reduce(f32[32,2,16,2,32,2]{3,2,5,4,1,0:T(8,128)} %reshape_reshape.3, f32[]{:T(128)} %constant.81.clone.1), dimensions={1,3,5}, to_apply=%region_7.8 | reduce | flops 114688 | bytes 589828 | tf_op jit(solution)/shard_map/reduce_sum | solution.py:94
  540.1 10.0 slice.793
  552.4 13.3 %fusion.63 = f32[64,32,64]{0,2,1:T(8,128)S(1)} fusion(f32[64,32,64]{0,2,1:T(8,128)} %copy-done.26, f32[64,32,64]{0,2,1:T(8,128)} %reshape.171, f32[66,34,1]{0,2,1:T(1,128)S(1)} %collective-permute-done.17, f32[66,1,64]{0,2,1:T(8,128)S(1)} %collective-permute-done.15, f32[66,1,64]{0,2,1:T(8,128)S(1)} %collective-permute-done.14, f32[1,32,64]{0,2,1:T(8,128)} %copy.220, ...), kind=kLoop, calls=%fused_computation.167 | loop fusion | flops 6815744 | bytes 5311008 | tf_op jit(solution)/shard_map/jit(_where)/select_n | solution.py:80
  569.0 4.9 collective-permute-start.18
  615.2 10.7 %fusion.49 = f32[64,32,64]{0,2,1:T(8,128)} fusion(f32[64,32,64]{0,2,1:T(8,128)} %reshape.171, f32[66,34,1]{0,2,1:T(1,128)S(1)} %collective-permute-done.23, f32[66,1,64]{0,2,1:T(8,128)S(1)} %collective-permute-done.21, f32[66,1,64]{0,2,1:T(8,128)S(1)} %collective-permute-done.20, f32[1,32,64]{0,2,1:T(8,128)} %copy.226, f32[64,32,64]{0,2,1:T(8,128)S(1)} %copy-done.11, ...), kind=kLoop, calls=%fused_computation.135 | loop fusion | flops 4980736 | bytes 5311008 | tf_op jit(solution)/shard_map/sub | solution.py:87
  628.9 36.8 %reshape.176 = f32[32,2,16,2,32,2]{5,4,3,2,1,0:T(8,128)} reshape(f32[64,32,64]{2,1,0:T(8,128)} %copy.229) | data formatting | bytes 1048576 | tf_op jit(solution)/shard_map/reshape | solution.py:94
  665.6 12.2 %reduce_sum.81 = f32[32,16,32]{2,1,0:T(8,128)S(1)} reduce(f32[32,2,16,2,32,2]{5,4,3,2,1,0:T(8,128)} %reshape.176, f32[]{:T(128)} %constant.81.clone.1), dimensions={1,3,5}, to_apply=%region_3.4 | reduce | flops 114688 | bytes 589828 | tf_op jit(solution)/shard_map/reduce_sum | solution.py:94
  697.8 4.5 collective-permute-start.34
  707.3 4.4 collective-permute-done.35
  729.5 4.3 collective-permute-start.40
  738.8 4.4 collective-permute-done.41
  758.3 4.6 collective-permute-start.46
  767.9 4.4 collective-permute-done.47
  787.0 4.6 collective-permute-start.52
  796.6 4.4 collective-permute-done.53
  815.3 4.6 collective-permute-start.58
  824.9 4.4 collective-permute-done.59
  843.7 4.6 collective-permute-start.64
  853.2 4.4 collective-permute-done.65
  872.0 4.6 collective-permute-start.70
  881.5 4.4 collective-permute-done.71
  886.6 11.4 %broadcast_in_dim.53 = f32[32,2,16,2,32,2]{5,4,3,2,1,0:T(8,128)} broadcast(f32[32,16,32]{2,1,0:T(8,128)S(1)} %fusion.103), dimensions={0,2,4} | broadcast | bytes 589824 | tf_op jit(solution)/shard_map/broadcast_in_dim | solution.py:115
  898.0 28.6 %reshape.180 = f32[64,32,64]{2,1,0:T(8,128)} reshape(f32[32,2,16,2,32,2]{5,4,3,2,1,0:T(8,128)} %broadcast_in_dim.53) | data formatting | bytes 1048576 | tf_op jit(solution)/shard_map/reshape | solution.py:116
  953.5 4.6 collective-permute-start.76
  963.2 5.7 fusion.36
  991.4 4.8 collective-permute-start.82
  1001.3 5.7 fusion.22
  1028.4 4.8 collective-permute-start.88
  1038.4 14.1 %fusion.8 = f32[64,32,64]{0,2,1:T(8,128)} fusion(f32[64,32,64]{0,2,1:T(8,128)} %reshape.171, f32[66,34,1]{0,2,1:T(1,128)S(1)} %collective-permute-done.89, f32[66,1,64]{0,2,1:T(8,128)S(1)} %collective-permute-done.87, f32[66,1,64]{0,2,1:T(8,128)S(1)} %collective-permute-done.86, f32[1,32,64]{0,2,1:T(8,128)} %copy.251, f32[64,32,64]{0,2,1:T(8,128)} %copy-done.12, ...), kind=kLoop, calls=%fused_computation.40 | loop fusion | flops 4980736 | bytes 5311008 | tf_op jit(solution)/shard_map/sub | solution.py:87
  (393 shorter events, 430.5 us)
Async XLA Ops:
  6.1 40.0 %all-to-all-start.1 = ((s32[32,1,1]{2,1,0:T(1,128)}), s32[32,1,1]{2,1,0:T(1,128)S(1)}, u32[]{:S(2)}, u32[]{:S(2)}) async-start(s32[32,1,1]{2,1,0:T(1,128)} %copy.200), calls=%async_computation.1 | async-start | bytes 32768 | tf_op jit(solution)/shard_map/all_to_all | solution.py:145
  46.1 101.4 %all-to-all-start.2 = ((f32[32,1,32768]{2,1,0:T(1,128)}), f32[32,1,32768]{2,1,0:T(1,128)}, u32[]{:S(2)}, u32[]{:S(2)}) async-start(f32[32,1,32768]{2,1,0:T(1,128)} %copy.202), calls=%async_computation.2 | async-start | bytes 8388608 | tf_op jit(solution)/shard_map/all_to_all | solution.py:144
  147.5 101.1 %all-to-all-start.3 = ((f32[32,1,32768]{2,1,0:T(1,128)}), f32[32,1,32768]{2,1,0:T(1,128)}, u32[]{:S(2)}, u32[]{:S(2)}) async-start(f32[32,1,32768]{2,1,0:T(1,128)} %copy.214), calls=%async_computation.3 | async-start | bytes 8388608 | tf_op jit(solution)/shard_map/all_to_all | solution.py:143
  248.5 161.1 %all-to-all-start = ((f32[32,1,32768]{2,1,0:T(1,128)}), f32[32,1,32768]{2,1,0:T(1,128)}, u32[]{:S(2)}, u32[]{:S(2)}) async-start(f32[32,1,32768]{2,1,0:T(1,128)} %copy.199), calls=%async_computation | async-start | bytes 8388608 | tf_op jit(solution)/shard_map/all_to_all | solution.py:142
  257.9 88.7 %collective-permute-start.2 = (f32[1,32,64]{2,1,0:T(8,128)S(1)}, f32[1,32,64]{2,1,0:T(8,128)S(1)}, u32[]{:S(2)}, u32[]{:S(2)}) collective-permute-start(f32[1,32,64]{2,1,0:T(8,128)S(1)} %broadcast.216), channel_id=1, source_target_pairs={{0,32},{32,64},{64,96},{96,128},{128,160},{160,192},{192,224},{1,3... | collective-permute-start | bytes 24584 | tf_op jit(solution)/shard_map/ppermute | solution.py:20
  261.0 86.1 %collective-permute-start.3 = (f32[1,32,64]{2,1,0:T(8,128)S(1)}, f32[1,32,64]{2,1,0:T(8,128)S(1)}, u32[]{:S(2)}, u32[]{:S(2)}) collective-permute-start(f32[1,32,64]{2,1,0:T(8,128)S(1)} %broadcast.216), channel_id=1, source_target_pairs={{32,0},{64,32},{96,64},{128,96},{160,128},{192,160},{224,192},{33,... | collective-permute-start | bytes 24584 | tf_op jit(solution)/shard_map/ppermute | solution.py:22
  263.2 208.6 %collective-permute-start.24 = (f32[1,16,32]{2,1,0:T(8,128)S(1)}, f32[1,16,32]{2,1,0:T(8,128)S(1)}, u32[]{:S(2)}, u32[]{:S(2)}) collective-permute-start(f32[1,16,32]{2,1,0:T(8,128)S(1)} %broadcast.219), channel_id=1, source_target_pairs={{0,32},{32,64},{64,96},{96,128},{128,160},{160,192},{192,224},{1,3... | collective-permute-start | bytes 6152 | tf_op jit(solution)/shard_map/ppermute | solution.py:20
  266.3 205.5 %collective-permute-start.25 = (f32[1,16,32]{2,1,0:T(8,128)S(1)}, f32[1,16,32]{2,1,0:T(8,128)S(1)}, u32[]{:S(2)}, u32[]{:S(2)}) collective-permute-start(f32[1,16,32]{2,1,0:T(8,128)S(1)} %broadcast.219), channel_id=1, source_target_pairs={{32,0},{64,32},{96,64},{128,96},{160,128},{192,160},{224,192},{33,... | collective-permute-start | bytes 6152 | tf_op jit(solution)/shard_map/ppermute | solution.py:22
  348.8 31.1 %collective-permute-start.6 = (f32[66,1,64]{0,2,1:T(8,128)S(1)}, f32[66,1,64]{0,2,1:T(8,128)S(1)}, u32[]{:S(2)}, u32[]{:S(2)}) collective-permute-start(f32[66,1,64]{0,2,1:T(8,128)S(1)} %get-tuple-element.42), channel_id=1, source_target_pairs={{0,8},{8,16},{16,24},{1,9},{9,17},{17,25},{2,10},{10,18},{18,26},{... | collective-permute-start | bytes 50696 | tf_op jit(solution)/shard_map/ppermute | solution.py:20
  350.9 33.8 %collective-permute-start.7 = (f32[66,1,64]{0,2,1:T(8,128)S(1)}, f32[66,1,64]{0,2,1:T(8,128)S(1)}, u32[]{:S(2)}, u32[]{:S(2)}) collective-permute-start(f32[66,1,64]{0,2,1:T(8,128)S(1)} %get-tuple-element.43), channel_id=1, source_target_pairs={{8,0},{16,8},{24,16},{9,1},{17,9},{25,17},{10,2},{18,10},{26,18},{... | collective-permute-start | bytes 50696 | tf_op jit(solution)/shard_map/ppermute | solution.py:22
  374.3 54.8 %collective-permute-start = (f32[1,32,64]{2,1,0:T(8,128)S(1)}, f32[1,32,64]{2,1,0:T(8,128)S(1)}, u32[]{:S(2)}, u32[]{:S(2)}) collective-permute-start(f32[1,32,64]{2,1,0:T(8,128)S(1)} %copy.204), channel_id=1, source_target_pairs={{32,0},{64,32},{96,64},{128,96},{160,128},{192,160},{224,192},{33,... | collective-permute-start | bytes 24584 | tf_op jit(solution)/shard_map/ppermute | solution.py:22
  379.9 49.6 %collective-permute-start.1 = (f32[1,32,64]{2,1,0:T(8,128)S(1)}, f32[1,32,64]{2,1,0:T(8,128)S(1)}, u32[]{:S(2)}, u32[]{:S(2)}) collective-permute-start(f32[1,32,64]{2,1,0:T(8,128)S(1)} %copy.206), channel_id=1, source_target_pairs={{0,32},{32,64},{64,96},{96,128},{128,160},{160,192},{192,224},{1,3... | collective-permute-start | bytes 24584 | tf_op jit(solution)/shard_map/ppermute | solution.py:20
  386.0 66.9 %collective-permute-start.10 = (f32[66,34,1]{0,2,1:T(1,128)S(1)}, f32[66,34,1]{0,2,1:T(1,128)S(1)}, u32[]{:S(2)}, u32[]{:S(2)}) collective-permute-start(f32[66,34,1]{0,2,1:T(1,128)S(1)} %get-tuple-element.28), channel_id=1, source_target_pairs={{0,1},{1,2},{2,3},{3,4},{4,5},{5,6},{6,7},{8,9},{9,10},{10,11},{11... | collective-permute-start | bytes 26936 | tf_op jit(solution)/shard_map/ppermute | solution.py:20
  431.9 8.6 collective-permute-start.4
  433.3 7.3 collective-permute-start.5
  440.8 8.5 collective-permute-start.8
  442.7 8.8 collective-permute-start.9
  463.3 13.3 %collective-permute-start.12 = (f32[1,32,64]{2,1,0:T(8,128)S(1)}, f32[1,32,64]{2,1,0:T(8,128)S(1)}, u32[]{:S(2)}, u32[]{:S(2)}) collective-permute-start(f32[1,32,64]{2,1,0:T(8,128)S(1)} %copy.217), channel_id=1, source_target_pairs={{0,32},{32,64},{64,96},{96,128},{128,160},{160,192},{192,224},{1,3... | collective-permute-start | bytes 24584 | tf_op jit(solution)/shard_map/ppermute | solution.py:20
  469.8 8.1 collective-permute-start.13
  471.9 13.9 %collective-permute-start.26 = (f32[34,1,32]{2,1,0:T(1,128)S(1)}, f32[34,1,32]{2,1,0:T(1,128)S(1)}, u32[]{:S(2)}, u32[]{:S(2)}) collective-permute-start(f32[34,1,32]{2,1,0:T(1,128)S(1)} %get-tuple-element.86), channel_id=1, source_target_pairs={{0,8},{8,16},{16,24},{1,9},{9,17},{17,25},{2,10},{10,18},{18,26},{... | collective-permute-start | bytes 13064 | tf_op jit(solution)/shard_map/ppermute | solution.py:20
  475.2 10.5 collective-permute-start.27
  489.3 63.0 %collective-permute-start.16 = (f32[66,34,1]{0,2,1:T(1,128)S(1)}, f32[66,34,1]{0,2,1:T(1,128)S(1)}, u32[]{:S(2)}, u32[]{:S(2)}) collective-permute-start(f32[66,34,1]{0,2,1:T(1,128)S(1)} %get-tuple-element.24), channel_id=1, source_target_pairs={{0,1},{1,2},{2,3},{3,4},{4,5},{5,6},{6,7},{8,9},{9,10},{10,11},{11... | collective-permute-start | bytes 26936 | tf_op jit(solution)/shard_map/ppermute | solution.py:20
  493.5 58.8 %collective-permute-start.17 = (f32[66,34,1]{0,2,1:T(1,128)S(1)}, f32[66,34,1]{0,2,1:T(1,128)S(1)}, u32[]{:S(2)}, u32[]{:S(2)}) collective-permute-start(f32[66,34,1]{0,2,1:T(1,128)S(1)} %get-tuple-element.25), channel_id=1, source_target_pairs={{1,0},{2,1},{3,2},{4,3},{5,4},{6,5},{7,6},{9,8},{10,9},{11,10},{12... | collective-permute-start | bytes 26936 | tf_op jit(solution)/shard_map/ppermute | solution.py:22
  496.5 181.3 %collective-permute-start.28 = (f32[34,18,1]{2,1,0:T(8,128)}, f32[34,18,1]{2,1,0:T(8,128)}, u32[]{:S(2)}, u32[]{:S(2)}) collective-permute-start(f32[34,18,1]{2,1,0:T(8,128)} %get-tuple-element.70), channel_id=1, source_target_pairs={{0,1},{1,2},{2,3},{3,4},{4,5},{5,6},{6,7},{8,9},{9,10},{10,11},{11... | collective-permute-start | bytes 7352 | tf_op jit(solution)/shard_map/ppermute | solution.py:20
  500.2 177.7 %collective-permute-start.29 = (f32[34,18,1]{2,1,0:T(8,128)}, f32[34,18,1]{2,1,0:T(8,128)}, u32[]{:S(2)}, u32[]{:S(2)}) collective-permute-start(f32[34,18,1]{2,1,0:T(8,128)} %get-tuple-element.71), channel_id=1, source_target_pairs={{1,0},{2,1},{3,2},{4,3},{5,4},{6,5},{7,6},{9,8},{10,9},{11,10},{12... | collective-permute-start | bytes 7352 | tf_op jit(solution)/shard_map/ppermute | solution.py:22
  569.0 16.3 %collective-permute-start.18 = (f32[1,32,64]{2,1,0:T(8,128)S(1)}, f32[1,32,64]{2,1,0:T(8,128)}, u32[]{:S(2)}, u32[]{:S(2)}) collective-permute-start(f32[1,32,64]{2,1,0:T(8,128)S(1)} %copy.223), channel_id=1, source_target_pairs={{0,32},{32,64},{64,96},{96,128},{128,160},{160,192},{192,224},{1,3... | collective-permute-start | bytes 24584 | tf_op jit(solution)/shard_map/ppermute | solution.py:20
  576.0 11.3 %collective-permute-start.19 = (f32[1,32,64]{2,1,0:T(8,128)}, f32[1,32,64]{2,1,0:T(8,128)}, u32[]{:S(2)}, u32[]{:S(2)}) collective-permute-start(f32[1,32,64]{2,1,0:T(8,128)} %copy.225), channel_id=1, source_target_pairs={{32,0},{64,32},{96,64},{128,96},{160,128},{192,160},{224,192},{33,... | collective-permute-start | bytes 24584 | tf_op jit(solution)/shard_map/ppermute | solution.py:22
  590.5 13.9 %collective-permute-start.20 = (f32[66,1,64]{0,2,1:T(8,128)S(1)}, f32[66,1,64]{0,2,1:T(8,128)S(1)}, u32[]{:S(2)}, u32[]{:S(2)}) collective-permute-start(f32[66,1,64]{0,2,1:T(8,128)S(1)} %get-tuple-element.36), channel_id=1, source_target_pairs={{0,8},{8,16},{16,24},{1,9},{9,17},{17,25},{2,10},{10,18},{18,26},{... | collective-permute-start | bytes 50696 | tf_op jit(solution)/shard_map/ppermute | solution.py:20
  593.6 10.8 %collective-permute-start.21 = (f32[66,1,64]{0,2,1:T(8,128)S(1)}, f32[66,1,64]{0,2,1:T(8,128)S(1)}, u32[]{:S(2)}, u32[]{:S(2)}) collective-permute-start(f32[66,1,64]{0,2,1:T(8,128)S(1)} %get-tuple-element.37), channel_id=1, source_target_pairs={{8,0},{16,8},{24,16},{9,1},{17,9},{25,17},{10,2},{18,10},{26,18},{... | collective-permute-start | bytes 50696 | tf_op jit(solution)/shard_map/ppermute | solution.py:22
  697.8 9.5 collective-permute-start.34
  702.3 9.4 collective-permute-start.35
  729.5 9.3 collective-permute-start.40
  733.8 9.4 collective-permute-start.41
  758.3 9.6 collective-permute-start.46
  762.9 9.4 collective-permute-start.47
  787.0 9.6 collective-permute-start.52
  791.6 9.4 collective-permute-start.53
  815.3 9.6 collective-permute-start.58
  820.0 9.4 collective-permute-start.59
  843.7 9.6 collective-permute-start.64
  848.3 9.4 collective-permute-start.65
  872.0 9.6 collective-permute-start.70
  876.6 9.4 collective-permute-start.71
  934.3 6.9 collective-permute-start.72
  972.2 6.9 collective-permute-start.78
  991.4 6.7 collective-permute-start.82
  1010.3 6.9 collective-permute-start.84
  1028.4 9.9 collective-permute-start.88
  (93 other events, 725.9 us)
where the time goes:
time: 1070 us; the launch traced here: 1060 us
  waiting for transfers between devices  361 us (34%)
  local copies, waits for them, and re-layouts  282 us (26%)
  starting transfers between devices  280 us (26%)
  other arithmetic  129 us (12%)
    ppermute x45, starting transfers between devices, with_halo(): lax.ppermute(tail, axis, [(i, (i + 1) % count) for i in range(ends)])  156 us
    ppermute x45, waiting for transfers between devices, with_halo(): lax.ppermute(tail, axis, [(i, (i + 1) % count) for i in range(ends)])  98.7 us
    ppermute x45, waiting for transfers between devices, with_halo(): lax.ppermute(head, axis, [((i + 1) % count, i) for i in range(ends)])  96.4 us
    ppermute x45, starting transfers between devices, with_halo(): lax.ppermute(head, axis, [((i + 1) % count, i) for i in range(ends)])  85.1 us
    all_to_all x1, waiting for transfers between devices, body(): lax.all_to_all(send_a, ('gx', 'gy'), split_axis=0, concat_axis=0, tiled=T...  83.5 us
    all_to_all x1, waiting for transfers between devices, body(): lax.all_to_all(send_b, ('gx', 'gy'), split_axis=0, concat_axis=0, tiled=T...  82.9 us
    select_n x12, other arithmetic, colour_sweeps(): solution = jnp.where(colour == current, updated, solution)  36.8 us
    reshape x1, local copies, waits for them, and re-layouts, restrict(): values.reshape(size_x // 2, 2, size_y // 2, 2, size_z // 2, 2)  36.8 us
  transfers between devices with their start and end apart: 94, of which 42 were waited for; matrix products, arithmetic and copies ran while one was open for 29% of the time, Pallas kernels for 0%

commit v1 on v0

v1 whole, which is shorter than its diff:
```python
import functools

import jax
import jax.numpy as jnp
from jax import lax
from jax.experimental import pallas as pl
from jax.experimental.pallas import tpu as pltpu
from jax.sharding import PartitionSpec as P

LAYER = ("gx", "gy")
F32 = jnp.float32
YR = 40
FXN = 70
CXN = 50
FY0 = 4
CY0 = 12
Z0 = 32


def lane_of(rows):
    return lax.broadcasted_iota(jnp.int32, (rows, 128), 1)


def rl(v, shift):
    shift = shift % 128
    return v if shift == 0 else pltpu.roll(v, shift, 1)


def ry(v, shift):
    return pltpu.roll(v, shift % v.shape[0], 0)


def plane(index, rows=YR):
    if isinstance(index, int):
        return pl.ds(index * rows, rows)
    return pl.ds(pl.multiple_of(index * rows, 8), rows)


def every(start, count, stride):
    return pl.ds(start, count, stride=stride)


def own_lanes(v):
    lane = lane_of(v.shape[0])
    return jnp.where((lane >= Z0) & (lane < Z0 + 64), v, 0.0)


def call(kernel, outs, scratch=(), limit=40, smem=0):
    def run(*args):
        return pl.pallas_call(
            kernel,
            out_shape=[jax.ShapeDtypeStruct(s, F32) for s in outs],
            in_specs=[pl.BlockSpec(memory_space=pltpu.SMEM)] * smem
            + [pl.BlockSpec(memory_space=pltpu.VMEM)] * (len(args) - smem),
            out_specs=[pl.BlockSpec(memory_space=pltpu.VMEM)] * len(outs),
            scratch_shapes=[pltpu.VMEM(s, F32) for s in scratch],
            compiler_params=pltpu.CompilerParams(vmem_limit_bytes=limit << 20),
        )(*args)

    return run


def spread_kernel(place, rhs, a, b, out):
    lane = lane_of(8)
    mark = jnp.zeros((8, 128), F32)
    for k in range(4):
        mark = jnp.where(lane == k, place[0, k].astype(F32), mark)

    @pl.loop(0, 32)
    def _(j):
        for f, src in enumerate((rhs, a, b)):
            for m in range(8):
                col = pl.ds(pl.multiple_of(j * 1024 + m * 128, 128), 128)
                out[j, f * 32 + m * 4 : f * 32 + m * 4 + 4, :] = src[0, :, col]
        out[j, 96:104, :] = mark


def route_kernel(place, got, out):
    @pl.loop(0, 32)
    def _(s):
        for k in range(4):
            p = place[s, k]
            t = lax.shift_right_logical(p, 2)
            q = lax.bitwise_and(p, 3)
            for f in range(3):
                out[t, f * 4 + q] = got[s, every(f * 32 + k, 8, 4), :]


def brick_kernel(got, rh, aa, bb, ylo, yhi, xlo, xhi):
    lane8 = lane_of(8)
    bricks = (rh, aa, bb)
    for br in bricks:
        br[...] = jnp.zeros_like(br)

    @pl.loop(0, 32)
    def _(j):
        for f, br in enumerate(bricks):
            for qx in range(2):
                low = got[j, f * 4 + qx * 2]
                high = got[j, f * 4 + qx * 2 + 1]
                for c in range(4):
                    both = jnp.where(lane8 < 64, rl(low, 32 - 32 * c), rl(high, 64 - 32 * c))
                    start = (j + (qx * 32 + 3)) * YR + (FY0 + c)
                    br[every(start, 8, 4), :] = own_lanes(both)

    lane = lane_of(32)
    for f, br in enumerate(bricks):
        for r in range(3):
            at = pl.ds((f * 3 + r) * 32, 32)
            for dst, y in ((ylo, r), (yhi, 29 + r)):
                first = br[every(3 * YR + FY0 + y, 32, YR), :]
                second = br[every(35 * YR + FY0 + y, 32, YR), :]
                dst[at, :] = jnp.where(lane < 64, rl(first, -32), rl(second, 32))
        xlo[pl.ds(f * 3 * YR, 3 * YR), :] = br[pl.ds(3 * YR, 3 * YR), :]
        xhi[pl.ds(f * 3 * YR, 3 * YR), :] = br[pl.ds(64 * YR, 3 * YR), :]


def fine_x_kernel(xlo, xhi, ylo, yhi, slo, shi, tlo, thi):
    lane = lane_of(YR)
    for own, out, tmp, base, shift in ((xlo, slo, tlo, 0, 32), (xhi, shi, thi, 29, -32)):
        tmp[...] = own[...]
        for f in range(3):
            for r in range(3):
                at = pl.ds((f * 3 + r) * 32 + base, 3)
                tmp[every(f * 3 * YR + FY0 - 3 + r, 3, YR), :] = own_lanes(rl(ylo[at, :], shift))
                tmp[every(f * 3 * YR + FY0 + 32 + r, 3, YR), :] = own_lanes(rl(yhi[at, :], shift))
        for m in range(5):
            v = rl(tmp[plane(2 * m), :], -32)
            w = rl(tmp[plane(2 * m + 1), :], 32) if m < 4 else jnp.zeros_like(v)
            out[plane(m), :] = jnp.where(lane < 64, v, w)


def fine_z_kernel(rh0, aa0, bb0, ylo, yhi, xlo, xhi, rh, aa, bb, zlo, zhi):
    lane = lane_of(YR)
    bricks = (rh, aa, bb)
    for f, (br0, br) in enumerate(zip((rh0, aa0, bb0), bricks)):
        br[...] = br0[...]
        for r in range(3):
            at = pl.ds((f * 3 + r) * 32, 32)
            for src, row in ((ylo, FY0 - 3 + r), (yhi, FY0 + 32 + r)):
                v = src[at, :]
                br[every(3 * YR + row, 32, YR), :] = own_lanes(rl(v, 32))
                br[every(35 * YR + row, 32, YR), :] = own_lanes(rl(v, -32))
        for i in range(3):
            n = f * 3 + i
            shift = 32 if n % 2 == 0 else -32
            br[plane(i), :] = own_lanes(rl(xlo[plane(n // 2), :], shift))
            br[plane(67 + i), :] = own_lanes(rl(xhi[plane(n // 2), :], shift))
    for group in range(5):
        lo = jnp.zeros((YR, 128), F32)
        hi = lo
        for slot in range(14):
            for f, br in enumerate(bricks):
                v = br[plane(group * 14 + slot), :]
                at = 9 * slot + 3 * f
                here = (lane >= at) & (lane < at + 3)
                lo = jnp.where(here, rl(v, at - Z0), lo)
                hi = jnp.where(here, rl(v, at - Z0 - 61), hi)
        zlo[plane(group), :] = lo
        zhi[plane(group), :] = hi


def nb_sum(fxp, fxm, fy, fz, vm, v, vp, step):
    total = fxp * vp + fxm * vm
    total = total + (fy * ry(v, -1) + ry(fy * v, 1))
    return total + (fz * rl(v, -step) + rl(fz * v, step))


def fine_nb(x, fx, fy, fz, v):
    return nb_sum(
        fx[plane(x), :],
        fx[plane(x - 1), :],
        fy[plane(x), :],
        fz[plane(x), :],
        v[plane(x - 1), :],
        v[plane(x), :],
        v[plane(x + 1), :],
        1,
    )


def fine_colour():
    return (lax.broadcasted_iota(jnp.int32, (YR, 128), 0) + lane_of(YR) + 1) % 2


def fine_update(x, colour, base, f, fx, fy, fz, inv, v):
    new = (f[plane(x), :] + fine_nb(x, fx, fy, fz, v)) * inv[plane(x), :]
    v[plane(x), :] = jnp.where((colour + x) % 2 == base, new, v[plane(x), :])


def presmooth_kernel(
    rh0, aa0, bb0, zlo, zhi, f, fx, fy, fz, inv, dg, v, c1, rc, slo, shi, a, b, tmp
):
    lane = lane_of(YR)
    even = lane % 2 == 0
    colour = fine_colour()
    for x in range(FXN):
        for n, (src, dst) in enumerate(((rh0, f), (aa0, a), (bb0, b))):
            at = 9 * (x % 14) + 3 * n
            w = src[plane(x), :]
            lo = rl(zlo[plane(x // 14), :], Z0 - 3 - at)
            hi = rl(zhi[plane(x // 14), :], Z0 + 64 - at)
            w = jnp.where((lane >= Z0 - 3) & (lane < Z0), lo, w)
            dst[plane(x), :] = jnp.where((lane >= Z0 + 64) & (lane < Z0 + 67), hi, w)

    @pl.loop(0, FXN - 1)
    def _(x):
        here = b[plane(x), :]
        fx[plane(x), :] = 0.5 * (here + b[plane(x + 1), :])
        fy[plane(x), :] = 0.5 * (here + ry(here, -1))
        fz[plane(x), :] = 0.5 * (here + rl(here, -1))

    for ref in (fx, fy, fz):
        ref[plane(FXN - 1), :] = jnp.zeros((YR, 128), F32)
    for ref in (inv, dg, v):
        ref[plane(0), :] = jnp.zeros((YR, 128), F32)
        ref[plane(FXN - 1), :] = jnp.zeros((YR, 128), F32)

    @pl.loop(1, FXN - 1)
    def _(x):
        py = fy[plane(x), :]
        pz = fz[plane(x), :]
        ax = a[plane(x), :]
        total = fx[plane(x), :] + fx[plane(x - 1), :] + py + ry(py, 1) + pz + rl(pz, 1)
        diag = ax + total
        inside = ax > 0.0
        one = jnp.where(inside, 1.0 / jnp.where(inside, diag, 1.0), 0.0)
        dg[plane(x), :] = diag
        inv[plane(x), :] = one
        v[plane(x), :] = jnp.where((colour + x) % 2 == 0, f[plane(x), :] * one, 0.0)

    @pl.loop(2, FXN - 2)
    def _(x):
        fine_update(x, colour, 1, f, fx, fy, fz, inv, v)

    even16 = lane_of(16) % 2 == 0
    lane16 = lane_of(16)

    def zpair(s):
        return s + jnp.where(even, rl(s, -1), rl(s, 1))

    def rows(slot, first):
        return tmp[every(slot * YR + first, 16, 2), :]

    def ypair(slot):
        return rows(slot, FY0) + rows(slot, FY0 + 1)

    def miss(x):
        return f[plane(x), :] - (dg[plane(x), :] * v[plane(x), :] - fine_nb(x, fx, fy, fz, v))

    @pl.loop(0, 32)
    def _(i):
        x0 = 2 * i + 3
        x1 = x0 + 1
        tmp[plane(0), :] = zpair(miss(x0) + miss(x1))
        tmp[plane(1), :] = zpair(a[plane(x0), :] + a[plane(x1), :])
        tmp[plane(2), :] = zpair(fx[plane(x1), :])
        tmp[plane(3), :] = zpair(fx[plane(x0 - 1), :])
        tmp[plane(4), :] = zpair(fy[plane(x0), :] + fy[plane(x1), :])
        tmp[plane(5), :] = fz[plane(x0), :] + fz[plane(x1), :]
        rhs = 0.125 * ypair(0)
        acoef = 0.125 * ypair(1)
        fxp = 0.25 * ypair(2)
        fxm = 0.25 * ypair(3)
        fyp = 0.25 * rows(4, FY0 + 1)
        fym = 0.25 * rows(4, FY0 - 1)
        s = 0.25 * ypair(5)
        fzp = jnp.where(even16, rl(s, -1), s)
        fzm = jnp.where(even16, rl(s, 1), rl(s, 2))
        diag = acoef + 0.25 * (fxp + fxm + fyp + fym + fzp + fzm)
        pa = jnp.where(even16, fxp, fyp)
        pb = jnp.where(even16, fzp, diag)
        c1[plane(i, 16), :] = jnp.where(lane16 < 64, rl(pa, -32), rl(pb, 32))
        rc[plane(i, 16), :] = jnp.where(lane16 < 64, rl(rhs, -32), 0.0)

    lane32 = lane_of(32)
    for dst, y0, fine0 in ((slo, 0, 0), (shi, 7, 29)):
        for r in range(9):
            dst[plane(r, 32), :] = c1[every(y0 + r, 32, 16), :]
            w = rc[every(y0 + r, 32, 16), :]
            if r < 6:
                start = (3 + 32 * (r // 3)) * YR + FY0 + fine0 + r % 3
                w = jnp.where(lane32 < 64, w, rl(v[every(start, 32, YR), :], 32))
            dst[plane(9 + r, 32), :] = w


def coarse_x_kernel(c1, rc, v, ylo, yhi, ec, er, vs, slo, shi):
    lane = lane_of(YR)
    ec[...] = jnp.zeros_like(ec)
    er[...] = jnp.zeros_like(er)
    vs[...] = v[...]
    for i in range(32):
        ec[pl.ds((i + 9) * YR + CY0, 16), :] = c1[plane(i, 16), :]
        er[pl.ds((i + 9) * YR + CY0, 16), :] = rc[plane(i, 16), :]
    for src, crow, frow in ((ylo, CY0 - 9, FY0 - 3), (yhi, CY0 + 16, FY0 + 32)):
        for r in range(9):
            ec[every(9 * YR + crow + r, 32, YR), :] = src[plane(r, 32), :]
            w = src[plane(9 + r, 32), :]
            er[every(9 * YR + crow + r, 32, YR), :] = w
            if r < 6:
                start = (3 + 32 * (r // 3)) * YR + frow + r % 3
                vs[every(start, 32, YR), :] = own_lanes(rl(w, -32))
    for dst, first, fine in ((slo, 9, 3), (shi, 32, 64)):
        for i in range(9):
            dst[plane(i), :] = ec[plane(first + i), :]
            w = er[plane(first + i), :]
            if i < 3:
                w = jnp.where(lane < 64, w, rl(own_lanes(vs[plane(fine + i), :]), 32))
            dst[plane(9 + i), :] = w


def slots():
    for n in range(150):
        yield n, n // 50, n % 50, n // 6, 21 * (n % 6)


def coarse_z_kernel(ec0, er0, vs0, xlo, xhi, ec, er, vs, zlo, zhi):
    lane = lane_of(YR)
    ec[...] = ec0[...]
    er[...] = er0[...]
    vs[...] = vs0[...]
    for src, first, fine in ((xlo, 0, 0), (xhi, 41, 67)):
        for i in range(9):
            ec[plane(first + i), :] = src[plane(i), :]
            w = src[plane(9 + i), :]
            er[plane(first + i), :] = w
            if i < 3:
                vs[plane(fine + i), :] = own_lanes(rl(w, -32))
    lo = hi = None
    for n, which, x, group, at in slots():
        if n % 6 == 0:
            lo = jnp.zeros((YR, 128), F32)
            hi = lo
        w = (ec, ec, er)[which][plane(x), :]
        base = 64 if which == 1 else 0
        here = (lane >= at) & (lane < at + 18)
        lo = jnp.where(here, rl(w, at - base), lo)
        hi = jnp.where(here, rl(w, at - base - 46), hi)
        if n < FXN:
            w = vs[plane(n), :]
            here = (lane >= at + 18) & (lane < at + 21)
            lo = jnp.where(here, rl(w, at + 18 - Z0), lo)
            hi = jnp.where(here, rl(w, at + 18 - Z0 - 61), hi)
        if n % 6 == 5:
            zlo[plane(group), :] = lo
            zhi[plane(group), :] = hi


def finish_kernel(
    ec, er, vs, zlo, zhi, f, fx, fy, fz, inv, dg, out, res, cx, cy, cz, ci, cf, cv, v, tmp
):
    lane = lane_of(YR)
    even = lane % 2 == 0
    own = (lane >= Z0) & (lane < Z0 + 64)
    below = (lane >= Z0 - 18) & (lane < Z0)
    above = (lane >= Z0 + 64) & (lane < Z0 + 82)
    for n, which, x, group, at in slots():
        w = (ec, ec, er)[which][plane(x), :]
        w = jnp.where(own, rl(w, -32 if which == 1 else 32), 0.0)
        w = jnp.where(below, rl(zlo[plane(group), :], Z0 - 18 - at), w)
        w = jnp.where(above, rl(zhi[plane(group), :], Z0 + 64 - at), w)
        if which == 0:
            cx[plane(x), :] = 0.25 * jnp.where(even, w, rl(w, 1))
            cy[plane(x), :] = 0.25 * jnp.where(even, rl(w, -1), w)
        elif which == 1:
            cz[plane(x), :] = 0.25 * jnp.where(even, w, rl(w, 1))
            diag = jnp.where(even, rl(w, -1), w)
            inside = diag > 0.0
            ci[plane(x), :] = jnp.where(inside, 1.0 / jnp.where(inside, diag, 1.0), 0.0)
        else:
            cf[plane(x), :] = w
        if n < FXN:
            w = own_lanes(vs[plane(n), :])
            low = rl(zlo[plane(group), :], Z0 - 3 - at - 18)
            high = rl(zhi[plane(group), :], Z0 + 64 - at - 18)
            w = jnp.where((lane >= Z0 - 3) & (lane < Z0), low, w)
            v[plane(n), :] = jnp.where((lane >= Z0 + 64) & (lane < Z0 + 67), high, w)

    row = lax.broadcasted_iota(jnp.int32, (YR, 128), 0)
    colour = (row + lane // 2 + 1) % 2

    @pl.loop(0, CXN)
    def _(x):
        cv[plane(x), :] = jnp.where((colour + x) % 2 == 0, cf[plane(x), :] * ci[plane(x), :], 0.0)

    for half in range(1, 8):

        @pl.loop(half, CXN - half)
        def _(x):
            nb = nb_sum(
                cx[plane(x), :],
                cx[plane(x - 1), :],
                cy[plane(x), :],
                cz[plane(x), :],
                cv[plane(x - 1), :],
                cv[plane(x), :],
                cv[plane(x + 1), :],
                2,
            )
            new = (cf[plane(x), :] + nb) * ci[plane(x), :]
            cv[plane(x), :] = jnp.where((colour + x) % 2 == half % 2, new, cv[plane(x), :])

    for i in range(-2, 34):
        c = cv[pl.ds((i + 9) * YR + CY0 - 2, 20), :]
        slot = (i % 2) * YR
        tmp[every(slot, 20, 2), :] = c
        tmp[every(slot + 1, 20, 2), :] = c
        spread = tmp[pl.ds(slot, YR), :]
        for x in (2 * i + 3, 2 * i + 4):
            if 0 <= x < FXN:
                v[plane(x), :] = v[plane(x), :] + spread

    shade = fine_colour()

    @pl.loop(1, FXN - 1)
    def _(x):
        fine_update(x, shade, 0, f, fx, fy, fz, inv, v)

    @pl.loop(2, FXN - 2)
    def _(x):
        fine_update(x, shade, 1, f, fx, fy, fz, inv, v)

    @pl.loop(0, 64)
    def _(i):
        x = i + 3
        w = v[plane(x), :]
        r = f[plane(x), :] - (dg[plane(x), :] * w - fine_nb(x, fx, fy, fz, v))
        out[i] = rl(w, -32)[FY0 : FY0 + 32, :64]
        res[i] = rl(r, -32)[FY0 : FY0 + 32, :64]


def swap(low, high, axis):
    count = lax.axis_size(axis)
    up = [(i, i + 1) for i in range(count - 1)]
    down = [(i + 1, i) for i in range(count - 1)]
    return lax.ppermute(high, axis, up), lax.ppermute(low, axis, down)


def body(rhs_boxes, a_boxes, b_boxes, new_place):
    exchange = functools.partial(
        lax.all_to_all, axis_name=LAYER, split_axis=0, concat_axis=0, tiled=True
    )
    (spread,) = call(spread_kernel, [(32, 104, 128)], smem=1)(
        new_place, rhs_boxes, a_boxes, b_boxes
    )
    got = exchange(spread)
    place = got[:, 96, :4].astype(jnp.int32)
    (routed,) = call(route_kernel, [(32, 12, 8, 128)], smem=1)(place, got)
    got = exchange(routed)

    fine = (FXN * YR, 128)
    coarse = (CXN * YR, 128)
    rh, aa, bb, ylo, yhi, xlo, xhi = call(
        brick_kernel, [fine] * 3 + [(288, 128)] * 2 + [(9 * YR, 128)] * 2
    )(got)
    ylo, yhi = swap(ylo, yhi, "gy")
    xlo, xhi = call(fine_x_kernel, [(5 * YR, 128)] * 2, [(9 * YR, 128)] * 2)(xlo, xhi, ylo, yhi)
    xlo, xhi = swap(xlo, xhi, "gx")
    rh, aa, bb, zlo, zhi = call(fine_z_kernel, [fine] * 3 + [(5 * YR, 128)] * 2)(
        rh, aa, bb, ylo, yhi, xlo, xhi
    )
    zlo, zhi = swap(zlo, zhi, "gz")
    f, fx, fy, fz, inv, dg, v, c1, rc, ylo, yhi = call(
        presmooth_kernel,
        [fine] * 7 + [(512, 128)] * 2 + [(18 * 32, 128)] * 2,
        [fine, fine, (6 * YR, 128)],
    )(rh, aa, bb, zlo, zhi)
    ylo, yhi = swap(ylo, yhi, "gy")
    ec, er, vs, xlo, xhi = call(coarse_x_kernel, [coarse, coarse, fine] + [(18 * YR, 128)] * 2)(
        c1, rc, v, ylo, yhi
    )
    xlo, xhi = swap(xlo, xhi, "gx")
    ec, er, vs, zlo, zhi = call(coarse_z_kernel, [coarse, coarse, fine] + [(25 * YR, 128)] * 2)(
        ec, er, vs, xlo, xhi
    )
    zlo, zhi = swap(zlo, zhi, "gz")
    return tuple(
        call(
            finish_kernel,
            [(64, 32, 64)] * 2,
            [coarse] * 6 + [fine, (2 * YR, 128)],
        )(ec, er, vs, zlo, zhi, f, fx, fy, fz, inv, dg)
    )


def solution(mesh):
    return jax.shard_map(
        body,
        mesh=mesh,
        in_specs=(
            P("gz", ("gx", "gy"), None),
            P("gz", ("gx", "gy"), None),
            P("gz", ("gx", "gy"), None),
            P("gz", ("gx", "gy")),
        ),
        out_specs=(P("gx", "gy", "gz"), P("gx", "gy", "gz")),
        check_vma=False,
    )
```

time: 1070 us -> 275 us (0.26); the launches traced: 1060 us -> 273 us
  waiting for transfers between devices: 361 us -> 37.6 us
  local copies, waits for them, and re-layouts: 282 us -> 4.89 us
  starting transfers between devices: 280 us -> 36.3 us
  other arithmetic: 129 us -> 0.01 us
  Pallas kernels: 0 us -> 99.5 us
  blocking collectives: 0 us -> 93.6 us
    ppermute x90 -> x12, starting transfers between devices: 241 us -> 36.3 us  [swap(): return (lax.ppermute(high, axis, up), lax.ppermute(low, axis, down))]
    all_to_all x4 -> x0, waiting for transfers between devices: 166 us -> none  [the longest x1 83.5 us: body(): lax.all_to_all(send_a, ('gx', 'gy'), split_axis=0, concat_axis=0, tiled=T...]
    ppermute x90 -> x12, waiting for transfers between devices: 195 us -> 37.6 us  [swap(): return (lax.ppermute(high, axis, up), lax.ppermute(low, axis, down))]
    pallas_call x0 -> x9, Pallas kernels: none -> 99.5 us  [run(): pl.pallas_call(kernel, out_shape=[jax.ShapeDtypeStruct(s, F32) for s in o...]
    all_to_all x0 -> x2, blocking collectives: none -> 93.6 us  [the longest x1 50.7 us: body(): got = exchange(spread)]
    reshape x10 -> x0, local copies, waits for them, and re-layouts: 86.4 us -> none  [the longest x1 36.8 us: restrict(): values.reshape(size_x // 2, 2, size_y // 2, 2, size_z // 2, 2)]
    slice x38 -> x0, local copies, waits for them, and re-layouts: 52.1 us -> none  [the longest x27 22 us: with_halo(): lax.slice_in_dim(cells, cells.shape[dim] - width, cells.shape[dim], axis=...]
    select_n x17 -> x0, other arithmetic: 49.7 us -> none  [the longest x12 36.8 us: colour_sweeps(): solution = jnp.where(colour == current, updated, solution)]
  transfers between devices with their start and end apart: 94 -> 12, of which waited for: 42 -> 11; matrix products, arithmetic and copies ran while one was open for 29% -> 0% of each run, Pallas kernels for 0% -> 0%
where the time goes in v1:
time: 275 us; the launch traced here: 273 us
  Pallas kernels  99.5 us (36%)
  blocking collectives  93.6 us (34%)
  waiting for transfers between devices  37.6 us (14%)
  starting transfers between devices  36.3 us (13%)
  local copies, waits for them, and re-layouts  4.89 us (2%)
    pallas_call x9, Pallas kernels, run(): pl.pallas_call(kernel, out_shape=[jax.ShapeDtypeStruct(s, F32) for s in o...  99.5 us
    all_to_all x1, blocking collectives, body(): got = exchange(spread)  50.7 us
    all_to_all x1, blocking collectives, body(): got = exchange(routed)  42.9 us
    ppermute x12, waiting for transfers between devices, swap(): return (lax.ppermute(high, axis, up), lax.ppermute(low, axis, down))  37.6 us
    ppermute x12, starting transfers between devices, swap(): return (lax.ppermute(high, axis, up), lax.ppermute(low, axis, down))  36.3 us
  transfers between devices with their start and end apart: 12, of which 11 were waited for; matrix products, arithmetic and copies ran while one was open for 0% of the time, Pallas kernels for 0%

profile of v1, /device:TPU:41, one launch (start us, length us, event | category | flops | bytes accessed | tf_op | source)
XLA Modules:
  0.0 272.8 jit_solution(17140312628237333376)
XLA Ops:
  0.6 0.0 copy-start.1
  0.6 1.0 copy-done.1
  1.7 0.0 copy-start.2
  1.7 1.0 copy-done.2
  2.7 0.0 copy-start.3
  2.7 1.0 copy-done.3
  3.8 0.0 copy-start.4
  3.8 0.7 copy-done.4
  4.4 1.1 shard_map.59
  5.6 50.7 %all_to_all.10.got = f32[32,104,128]{2,1,0:T(8,128)S(1)} all-to-all(f32[32,104,128]{2,1,0:T(8,128)S(1)} %shard_map.59), channel_id=1, replica_groups=mesh['gx'=8,'gy'=4,'gz'=8] {'gx','gy'}, dimensions={0} | all-to-all | bytes 3407872 | tf_op jit(solution)/shard_map/all_to_all | solution.py:446
  56.2 1.3 shard_map.60
  57.5 42.9 %all_to_all.11.got = f32[32,12,8,128]{3,2,1,0:T(8,128)S(1)} all-to-all(f32[32,12,8,128]{3,2,1,0:T(8,128)S(1)} %shard_map.60), channel_id=1, replica_groups=mesh['gx'=8,'gy'=4,'gz'=8] {'gx','gy'}, dimensions={0} | all-to-all | bytes 3145728 | tf_op jit(solution)/shard_map/all_to_all | solution.py:449
  100.5 3.9 %shard_map.61 = (f32[2800,128]{1,0:T(8,128)S(1)}, f32[2800,128]{1,0:T(8,128)S(1)}, f32[2800,128]{1,0:T(8,128)S(1)}, f32[288,128]{1,0:T(8,128)S(1)}, f32[288,128]...) custom-call(f32[32,12,8,128]{3,2,1,0:T(8,128)S(1)} %all_to_all.11.got), custom_call_target="tpu_custom_call" | custom-call | tf_op jit(solution)/shard_map/pallas_call | solution.py:50
  104.4 2.6 collective-permute-start
  107.0 1.3 collective-permute-start.1
  108.3 0.8 collective-permute-done.ylo
  109.1 3.8 %collective-permute-done.1.yhi = f32[288,128]{1,0:T(8,128)S(1)} collective-permute-done((f32[288,128]{1,0:T(8,128)S(1)}, f32[288,128]{1,0:T(8,128)S(1)}, u32[]{:S(2)}, u32[]{:S(2)}) %collective-permute-start.1) | collective-permute-done | bytes 147488 | tf_op jit(solution)/shard_map/ppermute | solution.py:436
  112.9 0.3 shard_map.62
  113.1 2.2 collective-permute-start.2
  115.4 3.1 %collective-permute-start.3 = (f32[200,128]{1,0:T(8,128)S(1)}, f32[200,128]{1,0:T(8,128)S(1)}, u32[]{:S(2)}, u32[]{:S(2)}) collective-permute-start(f32[200,128]{1,0:T(8,128)S(1)} %get-tuple-element.45), channel_id=1, source_target_pairs={{32,0},{64,32},{96,64},{128,96},{160,128},{192,160},{224,192},{33,... | collective-permute-start | bytes 307208 | tf_op jit(solution)/shard_map/ppermute | solution.py:436
  118.4 0.1 collective-permute-done.2.xlo
  118.5 2.2 collective-permute-done.3.xhi
  120.8 2.7 shard_map.63
  123.5 0.0 copy-start
  123.5 1.1 copy-done
  124.6 9.5 %collective-permute-start.4 = (f32[200,128]{1,0:T(8,128)S(1)}, f32[200,128]{1,0:T(8,128)S(1)}, u32[]{:S(2)}, u32[]{:S(2)}) collective-permute-start(f32[200,128]{1,0:T(8,128)S(1)} %get-tuple-element.49), channel_id=1, source_target_pairs={{0,1},{1,2},{2,3},{3,4},{4,5},{5,6},{6,7},{8,9},{9,10},{10,11},{11... | collective-permute-start | bytes 307208 | tf_op jit(solution)/shard_map/ppermute | solution.py:436
  134.1 1.9 collective-permute-start.5
  136.1 0.0 collective-permute-done.4.zlo
  136.1 4.0 %collective-permute-done.5.zhi = f32[200,128]{1,0:T(8,128)S(1)} collective-permute-done((f32[200,128]{1,0:T(8,128)S(1)}, f32[200,128]{1,0:T(8,128)S(1)}, u32[]{:S(2)}, u32[]{:S(2)}) %collective-permute-start.5) | collective-permute-done | bytes 102432 | tf_op jit(solution)/shard_map/ppermute | solution.py:436
  140.1 28.5 %shard_map.64 = (f32[2800,128]{1,0:T(8,128)S(1)}, f32[2800,128]{1,0:T(8,128)S(1)}, f32[2800,128]{1,0:T(8,128)S(1)}, f32[2800,128]{1,0:T(8,128)S(1)}, f32[2800,12...) custom-call(f32[2800,128]{1,0:T(8,128)S(1)} %get-tuple-element.46.rh, ...), custom_call_target="tpu_custom_call" | custom-call | tf_op jit(solution)/shard_map/pallas_call | solution.py:50
  168.6 2.8 %collective-permute-start.6 = (f32[576,128]{1,0:T(8,128)S(1)}, f32[576,128]{1,0:T(8,128)S(1)}, u32[]{:S(2)}, u32[]{:S(2)}) collective-permute-start(f32[576,128]{1,0:T(8,128)S(1)} %get-tuple-element.54), channel_id=1, source_target_pairs={{0,8},{8,16},{16,24},{1,9},{9,17},{17,25},{2,10},{10,18},{18,26},{... | collective-permute-start | bytes 884744 | tf_op jit(solution)/shard_map/ppermute | solution.py:436
  171.4 1.3 collective-permute-start.7
  172.7 4.7 %collective-permute-done.6.ylo = f32[576,128]{1,0:T(8,128)S(1)} collective-permute-done((f32[576,128]{1,0:T(8,128)S(1)}, f32[576,128]{1,0:T(8,128)S(1)}, u32[]{:S(2)}, u32[]{:S(2)}) %collective-permute-start.6) | collective-permute-done | bytes 294944 | tf_op jit(solution)/shard_map/ppermute | solution.py:436
  177.4 4.1 %collective-permute-done.7.yhi = f32[576,128]{1,0:T(8,128)S(1)} collective-permute-done((f32[576,128]{1,0:T(8,128)S(1)}, f32[576,128]{1,0:T(8,128)S(1)}, u32[]{:S(2)}, u32[]{:S(2)}) %collective-permute-start.7) | collective-permute-done | bytes 294944 | tf_op jit(solution)/shard_map/ppermute | solution.py:436
  181.5 0.4 shard_map.65
  182.0 2.3 collective-permute-start.8
  184.2 3.0 %collective-permute-start.9 = (f32[720,128]{1,0:T(8,128)S(1)}, f32[720,128]{1,0:T(8,128)S(1)}, u32[]{:S(2)}, u32[]{:S(2)}) collective-permute-start(f32[720,128]{1,0:T(8,128)S(1)} %get-tuple-element.60), channel_id=1, source_target_pairs={{32,0},{64,32},{96,64},{128,96},{160,128},{192,160},{224,192},{33,... | collective-permute-start | bytes 1105928 | tf_op jit(solution)/shard_map/ppermute | solution.py:436
  187.3 6.5 %collective-permute-done.8.xlo = f32[720,128]{1,0:T(8,128)S(1)} collective-permute-done((f32[720,128]{1,0:T(8,128)S(1)}, f32[720,128]{1,0:T(8,128)S(1)}, u32[]{:S(2)}, u32[]{:S(2)}) %collective-permute-start.8) | collective-permute-done | bytes 368672 | tf_op jit(solution)/shard_map/ppermute | solution.py:436
  193.8 3.1 %collective-permute-done.9.xhi = f32[720,128]{1,0:T(8,128)S(1)} collective-permute-done((f32[720,128]{1,0:T(8,128)S(1)}, f32[720,128]{1,0:T(8,128)S(1)}, u32[]{:S(2)}, u32[]{:S(2)}) %collective-permute-start.9) | collective-permute-done | bytes 368672 | tf_op jit(solution)/shard_map/ppermute | solution.py:436
  196.9 2.4 shard_map.66
  199.3 4.2 %collective-permute-start.10 = (f32[1000,128]{1,0:T(8,128)S(1)}, f32[1000,128]{1,0:T(8,128)S(1)}, u32[]{:S(2)}, u32[]{:S(2)}) collective-permute-start(f32[1000,128]{1,0:T(8,128)S(1)} %get-tuple-element.64), channel_id=1, source_target_pairs={{0,1},{1,2},{2,3},{3,4},{4,5},{5,6},{6,7},{8,9},{9,10},{10,11},{11... | collective-permute-start | bytes 1536008 | tf_op jit(solution)/shard_map/ppermute | solution.py:436
  203.5 2.1 collective-permute-start.11
  205.6 3.9 %collective-permute-done.10.zlo = f32[1000,128]{1,0:T(8,128)S(1)} collective-permute-done((f32[1000,128]{1,0:T(8,128)S(1)}, f32[1000,128]{1,0:T(8,128)S(1)}, u32[]{:S(2)}, u32[]{:S(2)}) %collective-permute-start.10) | collective-permute-done | bytes 512032 | tf_op jit(solution)/shard_map/ppermute | solution.py:436
  209.4 4.4 %collective-permute-done.11.zhi = f32[1000,128]{1,0:T(8,128)S(1)} collective-permute-done((f32[1000,128]{1,0:T(8,128)S(1)}, f32[1000,128]{1,0:T(8,128)S(1)}, u32[]{:S(2)}, u32[]{:S(2)}) %collective-permute-start.11) | collective-permute-done | bytes 512032 | tf_op jit(solution)/shard_map/ppermute | solution.py:436
  213.8 58.9 %shard_map.67 = (f32[64,32,64]{2,1,0:T(8,128)}, f32[64,32,64]{2,1,0:T(8,128)}) custom-call(f32[2000,128]{1,0:T(8,128)S(1)} %get-tuple-element.61.ec, f32[2000,128]{1,0:T(8,128)S(1)} %get-tuple-element.62.er, f32[2800,128]{1,0:T(8,128)S(1)} %get-tuple-element.63.vs, f32[1000,128]{1,0:T(8,128)S(1)} %collective-permute-done.10.zlo, ...), custom_call_target="tpu_custom_call" | custom-call | tf_op jit(solution)/shard_map/pallas_call | solution.py:50
  (1 shorter events, 0.0 us)
Async XLA Ops:
  0.6 1.0 copy-start.1
  1.7 1.0 copy-start.2
  2.7 1.0 copy-start.3
  3.8 0.7 copy-start.4
  104.4 4.7 %collective-permute-start = (f32[288,128]{1,0:T(8,128)S(1)}, f32[288,128]{1,0:T(8,128)S(1)}, u32[]{:S(2)}, u32[]{:S(2)}) collective-permute-start(f32[288,128]{1,0:T(8,128)S(1)} %get-tuple-element.40), channel_id=1, source_target_pairs={{0,8},{8,16},{16,24},{1,9},{9,17},{17,25},{2,10},{10,18},{18,26},{... | collective-permute-start | bytes 442376 | tf_op jit(solution)/shard_map/ppermute | solution.py:436
  107.0 5.9 %collective-permute-start.1 = (f32[288,128]{1,0:T(8,128)S(1)}, f32[288,128]{1,0:T(8,128)S(1)}, u32[]{:S(2)}, u32[]{:S(2)}) collective-permute-start(f32[288,128]{1,0:T(8,128)S(1)} %get-tuple-element.41), channel_id=1, source_target_pairs={{8,0},{16,8},{24,16},{9,1},{17,9},{25,17},{10,2},{18,10},{26,18},{... | collective-permute-start | bytes 442376 | tf_op jit(solution)/shard_map/ppermute | solution.py:436
  113.1 5.4 %collective-permute-start.2 = (f32[200,128]{1,0:T(8,128)S(1)}, f32[200,128]{1,0:T(8,128)S(1)}, u32[]{:S(2)}, u32[]{:S(2)}) collective-permute-start(f32[200,128]{1,0:T(8,128)S(1)} %get-tuple-element.44), channel_id=1, source_target_pairs={{0,32},{32,64},{64,96},{96,128},{128,160},{160,192},{192,224},{1,3... | collective-permute-start | bytes 307208 | tf_op jit(solution)/shard_map/ppermute | solution.py:436
  115.4 5.4 %collective-permute-start.3 = (f32[200,128]{1,0:T(8,128)S(1)}, f32[200,128]{1,0:T(8,128)S(1)}, u32[]{:S(2)}, u32[]{:S(2)}) collective-permute-start(f32[200,128]{1,0:T(8,128)S(1)} %get-tuple-element.45), channel_id=1, source_target_pairs={{32,0},{64,32},{96,64},{128,96},{160,128},{192,160},{224,192},{33,... | collective-permute-start | bytes 307208 | tf_op jit(solution)/shard_map/ppermute | solution.py:436
  123.5 1.1 copy-start
  124.6 11.5 %collective-permute-start.4 = (f32[200,128]{1,0:T(8,128)S(1)}, f32[200,128]{1,0:T(8,128)S(1)}, u32[]{:S(2)}, u32[]{:S(2)}) collective-permute-start(f32[200,128]{1,0:T(8,128)S(1)} %get-tuple-element.49), channel_id=1, source_target_pairs={{0,1},{1,2},{2,3},{3,4},{4,5},{5,6},{6,7},{8,9},{9,10},{10,11},{11... | collective-permute-start | bytes 307208 | tf_op jit(solution)/shard_map/ppermute | solution.py:436
  134.1 6.0 %collective-permute-start.5 = (f32[200,128]{1,0:T(8,128)S(1)}, f32[200,128]{1,0:T(8,128)S(1)}, u32[]{:S(2)}, u32[]{:S(2)}) collective-permute-start(f32[200,128]{1,0:T(8,128)S(1)} %get-tuple-element.50), channel_id=1, source_target_pairs={{1,0},{2,1},{3,2},{4,3},{5,4},{6,5},{7,6},{9,8},{10,9},{11,10},{12... | collective-permute-start | bytes 307208 | tf_op jit(solution)/shard_map/ppermute | solution.py:436
  168.6 8.8 %collective-permute-start.6 = (f32[576,128]{1,0:T(8,128)S(1)}, f32[576,128]{1,0:T(8,128)S(1)}, u32[]{:S(2)}, u32[]{:S(2)}) collective-permute-start(f32[576,128]{1,0:T(8,128)S(1)} %get-tuple-element.54), channel_id=1, source_target_pairs={{0,8},{8,16},{16,24},{1,9},{9,17},{17,25},{2,10},{10,18},{18,26},{... | collective-permute-start | bytes 884744 | tf_op jit(solution)/shard_map/ppermute | solution.py:436
  171.4 10.1 %collective-permute-start.7 = (f32[576,128]{1,0:T(8,128)S(1)}, f32[576,128]{1,0:T(8,128)S(1)}, u32[]{:S(2)}, u32[]{:S(2)}) collective-permute-start(f32[576,128]{1,0:T(8,128)S(1)} %get-tuple-element.55), channel_id=1, source_target_pairs={{8,0},{16,8},{24,16},{9,1},{17,9},{25,17},{10,2},{18,10},{26,18},{... | collective-permute-start | bytes 884744 | tf_op jit(solution)/shard_map/ppermute | solution.py:436
  182.0 11.9 %collective-permute-start.8 = (f32[720,128]{1,0:T(8,128)S(1)}, f32[720,128]{1,0:T(8,128)S(1)}, u32[]{:S(2)}, u32[]{:S(2)}) collective-permute-start(f32[720,128]{1,0:T(8,128)S(1)} %get-tuple-element.59), channel_id=1, source_target_pairs={{0,32},{32,64},{64,96},{96,128},{128,160},{160,192},{192,224},{1,3... | collective-permute-start | bytes 1105928 | tf_op jit(solution)/shard_map/ppermute | solution.py:436
  184.2 12.6 %collective-permute-start.9 = (f32[720,128]{1,0:T(8,128)S(1)}, f32[720,128]{1,0:T(8,128)S(1)}, u32[]{:S(2)}, u32[]{:S(2)}) collective-permute-start(f32[720,128]{1,0:T(8,128)S(1)} %get-tuple-element.60), channel_id=1, source_target_pairs={{32,0},{64,32},{96,64},{128,96},{160,128},{192,160},{224,192},{33,... | collective-permute-start | bytes 1105928 | tf_op jit(solution)/shard_map/ppermute | solution.py:436
  199.3 10.2 %collective-permute-start.10 = (f32[1000,128]{1,0:T(8,128)S(1)}, f32[1000,128]{1,0:T(8,128)S(1)}, u32[]{:S(2)}, u32[]{:S(2)}) collective-permute-start(f32[1000,128]{1,0:T(8,128)S(1)} %get-tuple-element.64), channel_id=1, source_target_pairs={{0,1},{1,2},{2,3},{3,4},{4,5},{5,6},{6,7},{8,9},{9,10},{10,11},{11... | collective-permute-start | bytes 1536008 | tf_op jit(solution)/shard_map/ppermute | solution.py:436
  203.5 10.4 %collective-permute-start.11 = (f32[1000,128]{1,0:T(8,128)S(1)}, f32[1000,128]{1,0:T(8,128)S(1)}, u32[]{:S(2)}, u32[]{:S(2)}) collective-permute-start(f32[1000,128]{1,0:T(8,128)S(1)} %get-tuple-element.65), channel_id=1, source_target_pairs={{1,0},{2,1},{3,2},{4,3},{5,4},{6,5},{7,6},{9,8},{10,9},{11,10},{12... | collective-permute-start | bytes 1536008 | tf_op jit(solution)/shard_map/ppermute | solution.py:436

commit v2 on v1

v2 whole, which is shorter than its diff:
```python
import functools

import jax
import jax.numpy as jnp
from jax import lax
from jax.experimental import pallas as pl
from jax.experimental.pallas import tpu as pltpu
from jax.sharding import PartitionSpec as P

LAYER = ("gx", "gy")
F32 = jnp.float32
YR = 40
FXN = 70
CXN = 50
FY0 = 4
CY0 = 12
Z0 = 32


def lane_of(rows):
    return lax.broadcasted_iota(jnp.int32, (rows, 128), 1)


def rl(v, shift):
    shift = shift % 128
    return v if shift == 0 else pltpu.roll(v, shift, 1)


def ry(v, shift):
    return pltpu.roll(v, shift % v.shape[0], 0)


def plane(index, rows=YR):
    if isinstance(index, int):
        return pl.ds(index * rows, rows)
    return pl.ds(pl.multiple_of(index * rows, 8), rows)


def every(start, count, stride):
    return pl.ds(start, count, stride=stride)


def own_lanes(v):
    lane = lane_of(v.shape[0])
    return jnp.where((lane >= Z0) & (lane < Z0 + 64), v, 0.0)


def call(kernel, outs, scratch=(), limit=24, smem=0, us=2):
    def run(*args):
        return pl.pallas_call(
            kernel,
            out_shape=[jax.ShapeDtypeStruct(s, F32) for s in outs],
            in_specs=[pl.BlockSpec(memory_space=pltpu.SMEM)] * smem
            + [pl.BlockSpec(memory_space=pltpu.VMEM)] * (len(args) - smem),
            out_specs=[pl.BlockSpec(memory_space=pltpu.VMEM)] * len(outs),
            scratch_shapes=[pltpu.VMEM(s, F32) for s in scratch],
            cost_estimate=pl.CostEstimate(
                flops=0, transcendentals=0, bytes_accessed=us * 3_000_000
            ),
            compiler_params=pltpu.CompilerParams(vmem_limit_bytes=limit << 20),
        )(*args)

    return run


def spread_kernel(place, rhs, a, b, out):
    lane = lane_of(8)
    mark = jnp.zeros((8, 128), F32)
    for k in range(4):
        mark = jnp.where(lane == k, place[0, k].astype(F32), mark)

    @pl.loop(0, 32)
    def _(j):
        for f, src in enumerate((rhs, a, b)):
            for m in range(8):
                col = pl.ds(pl.multiple_of(j * 1024 + m * 128, 128), 128)
                out[j, f * 32 + m * 4 : f * 32 + m * 4 + 4, :] = src[0, :, col]
        out[j, 96:104, :] = mark


def route_kernel(place, got, out):
    @pl.loop(0, 32)
    def _(s):
        for k in range(4):
            p = place[s, k]
            t = lax.shift_right_logical(p, 2)
            q = lax.bitwise_and(p, 3)
            for f in range(3):
                out[t, f * 4 + q] = got[s, every(f * 32 + k, 8, 4), :]


def brick_kernel(got, rh, aa, bb, ylo, yhi, xlo, xhi):
    lane8 = lane_of(8)
    bricks = (rh, aa, bb)
    for br in bricks:
        br[...] = jnp.zeros_like(br)

    @pl.loop(0, 32)
    def _(j):
        for f, br in enumerate(bricks):
            for qx in range(2):
                low = got[j, f * 4 + qx * 2]
                high = got[j, f * 4 + qx * 2 + 1]
                for c in range(4):
                    both = jnp.where(lane8 < 64, rl(low, 32 - 32 * c), rl(high, 64 - 32 * c))
                    start = (j + (qx * 32 + 3)) * YR + (FY0 + c)
                    br[every(start, 8, 4), :] = own_lanes(both)

    lane = lane_of(32)
    for f, br in enumerate(bricks):
        for r in range(3):
            at = pl.ds((f * 3 + r) * 32, 32)
            for dst, y in ((ylo, r), (yhi, 29 + r)):
                first = br[every(3 * YR + FY0 + y, 32, YR), :]
                second = br[every(35 * YR + FY0 + y, 32, YR), :]
                dst[at, :] = jnp.where(lane < 64, rl(first, -32), rl(second, 32))
        xlo[pl.ds(f * 3 * YR, 3 * YR), :] = br[pl.ds(3 * YR, 3 * YR), :]
        xhi[pl.ds(f * 3 * YR, 3 * YR), :] = br[pl.ds(64 * YR, 3 * YR), :]


def fine_x_kernel(xlo, xhi, ylo, yhi, slo, shi, tlo, thi):
    lane = lane_of(YR)
    for own, out, tmp, base, shift in ((xlo, slo, tlo, 0, 32), (xhi, shi, thi, 29, -32)):
        tmp[...] = own[...]
        for f in range(3):
            for r in range(3):
                at = pl.ds((f * 3 + r) * 32 + base, 3)
                tmp[every(f * 3 * YR + FY0 - 3 + r, 3, YR), :] = own_lanes(rl(ylo[at, :], shift))
                tmp[every(f * 3 * YR + FY0 + 32 + r, 3, YR), :] = own_lanes(rl(yhi[at, :], shift))
        for m in range(5):
            v = rl(tmp[plane(2 * m), :], -32)
            w = rl(tmp[plane(2 * m + 1), :], 32) if m < 4 else jnp.zeros_like(v)
            out[plane(m), :] = jnp.where(lane < 64, v, w)


def fine_z_kernel(rh0, aa0, bb0, ylo, yhi, xlo, xhi, rh, aa, bb, zlo, zhi):
    lane = lane_of(YR)
    bricks = (rh, aa, bb)
    for f, (br0, br) in enumerate(zip((rh0, aa0, bb0), bricks)):
        br[...] = br0[...]
        for r in range(3):
            at = pl.ds((f * 3 + r) * 32, 32)
            for src, row in ((ylo, FY0 - 3 + r), (yhi, FY0 + 32 + r)):
                v = src[at, :]
                br[every(3 * YR + row, 32, YR), :] = own_lanes(rl(v, 32))
                br[every(35 * YR + row, 32, YR), :] = own_lanes(rl(v, -32))
        for i in range(3):
            n = f * 3 + i
            shift = 32 if n % 2 == 0 else -32
            br[plane(i), :] = own_lanes(rl(xlo[plane(n // 2), :], shift))
            br[plane(67 + i), :] = own_lanes(rl(xhi[plane(n // 2), :], shift))
    for group in range(5):
        lo = jnp.zeros((YR, 128), F32)
        hi = lo
        for slot in range(14):
            for f, br in enumerate(bricks):
                v = br[plane(group * 14 + slot), :]
                at = 9 * slot + 3 * f
                here = (lane >= at) & (lane < at + 3)
                lo = jnp.where(here, rl(v, at - Z0), lo)
                hi = jnp.where(here, rl(v, at - Z0 - 61), hi)
        zlo[plane(group), :] = lo
        zhi[plane(group), :] = hi


def span(x, count):
    if isinstance(x, int):
        return pl.ds(x * YR, count * YR)
    return pl.ds(pl.multiple_of(x * YR, 8), count * YR)


def nb_sum(x, count, cx, cy_ref, cz, v, step):
    at = span(x, count)
    here = v[at, :]
    cz = cz[span(x, count), :]
    total = cx[span(x, count), :] * v[span(x + 1, count), :]
    total = total + cx[span(x - 1, count), :] * v[span(x - 1, count), :]
    cy = cy_ref[at, :]
    total = total + (cy * ry(here, -1) + ry(cy * here, 1))
    return total + (cz * rl(here, -step) + rl(cz * here, step))


def steps(count):
    def run(step):
        for k in range(count):
            step(k)

    return run


def red_rows(rows, odd):
    row = lax.broadcasted_iota(jnp.int32, (rows, 128), 0)
    return (row + row // YR + lane_of(rows) + odd) % 2 == 0


FC = 4
FS = 4
STEPS = 68 // FS


def zpair(s):
    return s + jnp.where(lane_of(s.shape[0]) % 2 == 0, rl(s, -1), rl(s, 1))


def halves(w):
    w = w.reshape(FC // 2, 2, YR, 128)
    return w[:, 0].reshape(FC // 2 * YR, 128), w[:, 1].reshape(FC // 2 * YR, 128)


def both(w):
    first, second = halves(w)
    return first + second


def coefficient_kernel(
    rh0, aa0, bb0, zlo, zhi, f, fx, fy, fz, ir, ib, dg, v, c1, slo, shi, a, b, ta, tx, ty, tz
):
    lane = lane_of(YR)
    for x in range(FXN):
        for n, (src, dst) in enumerate(((rh0, f), (aa0, a), (bb0, b))):
            at = 9 * (x % 14) + 3 * n
            w = src[plane(x), :]
            lo = rl(zlo[plane(x // 14), :], Z0 - 3 - at)
            hi = rl(zhi[plane(x // 14), :], Z0 + 64 - at)
            w = jnp.where((lane >= Z0 - 3) & (lane < Z0), lo, w)
            dst[plane(x), :] = jnp.where((lane >= Z0 + 64) & (lane < Z0 + 67), hi, w)

    def faces(x, count):
        here = b[span(x, count), :]
        fx[span(x, count), :] = 0.5 * (here + b[span(x + 1, count), :])
        fy[span(x, count), :] = 0.5 * (here + ry(here, -1))
        fz[span(x, count), :] = 0.5 * (here + rl(here, -1))

    faces(0, 1)

    @steps(STEPS)
    def _(k):
        faces(1 + k * FS, FS)

    nothing = jnp.zeros((YR, 128), F32)
    for ref in (fx, fy, fz):
        ref[plane(FXN - 1), :] = nothing
    for ref in (ir, ib, dg, v):
        ref[plane(0), :] = nothing
        ref[plane(FXN - 1), :] = nothing

    @steps(STEPS)
    def _(k):
        x = 1 + k * FS
        at = span(x, FS)
        py = fy[at, :]
        pz = fz[at, :]
        ax = a[at, :]
        total = fx[at, :] + fx[span(x - 1, FS), :] + py + ry(py, 1) + pz + rl(pz, 1)
        diag = ax + total
        inside = ax > 0.0
        one = jnp.where(inside, 1.0 / jnp.where(inside, diag, 1.0), 0.0)
        red = red_rows(FS * YR, 0)
        dg[at, :] = diag
        ir[at, :] = jnp.where(red, one, 0.0)
        ib[at, :] = jnp.where(red, 0.0, one)
        v[at, :] = jnp.where(red, f[at, :] * one, 0.0)

    edge = fx[plane(2), :]
    edge = edge + jnp.where(lane % 2 == 0, rl(edge, -1), rl(edge, 1))
    tx[plane(0), :] = edge

    @steps(64 // FC)
    def _(k):
        at = span(3 + k * FC, FC)
        to = span(k * (FC // 2), FC // 2)
        ta[to, :] = zpair(both(a[at, :]))
        tx[span(k * (FC // 2) + 1, FC // 2), :] = zpair(halves(fx[at, :])[1])
        ty[to, :] = zpair(both(fy[at, :]))
        tz[to, :] = both(fz[at, :])

    @steps(8)
    def _(k):
        base = k * 4 * YR
        even = lane_of(80) % 2 == 0

        def rows(ref, first, planes=0):
            return ref[every(base + planes * YR + first, 80, 2), :]

        acoef = 0.125 * (rows(ta, 0) + rows(ta, 1))
        fxp = 0.25 * (rows(tx, 0, 1) + rows(tx, 1, 1))
        fxm = 0.25 * (rows(tx, 0) + rows(tx, 1))
        fyp = 0.25 * rows(ty, 1)
        s = 0.25 * (rows(tz, 0) + rows(tz, 1))
        fzp = jnp.where(even, rl(s, -1), s)
        diag = acoef + 0.25 * (fxp + fxm + fyp + ry(fyp, 1) + fzp + rl(fzp, 2))
        pa = jnp.where(even, fxp, fyp)
        pb = jnp.where(even, fzp, diag)
        c1[pl.ds(k * 80, 80), :] = jnp.where(lane_of(80) < 64, rl(pa, -32), rl(pb, 32))

    for dst, y0 in ((slo, 2), (shi, 9)):
        for r in range(9):
            dst[plane(r, 32), :] = c1[every(y0 + r, 32, 20), :]


def presmooth_kernel(f, fx, fy, fz, ib, dg, v0, v, rc, slo, shi, tr):
    for x in (0, FXN - 1):
        v[plane(x), :] = v0[plane(x), :]

    @steps(STEPS)
    def _(k):
        x = 1 + k * FS
        at = span(x, FS)
        new = (f[at, :] + nb_sum(x, FS, fx, fy, fz, v0, 1)) * ib[at, :]
        v[at, :] = v0[at, :] + new

    @steps(64 // FC)
    def _(k):
        x = 3 + k * FC
        at = span(x, FC)
        miss = f[at, :] - (dg[at, :] * v[at, :] - nb_sum(x, FC, fx, fy, fz, v, 1))
        tr[span(k * (FC // 2), FC // 2), :] = zpair(both(miss))

    @steps(8)
    def _(k):
        base = k * 4 * YR
        rhs = tr[every(base, 80, 2), :] + tr[every(base + 1, 80, 2), :]
        rc[pl.ds(k * 80, 80), :] = jnp.where(lane_of(80) < 64, rl(0.125 * rhs, -32), 0.0)

    lane32 = lane_of(32)
    for dst, y0, fine0 in ((slo, 2, 0), (shi, 9, 29)):
        for r in range(9):
            w = rc[every(y0 + r, 32, 20), :]
            if r < 6:
                start = (3 + 32 * (r // 3)) * YR + FY0 + fine0 + r % 3
                w = jnp.where(lane32 < 64, w, rl(v[every(start, 32, YR), :], 32))
            dst[plane(r, 32), :] = w


def coarse_own(dst, src):
    dst[...] = jnp.zeros_like(dst)
    for i in range(32):
        dst[pl.ds((i + 9) * YR + CY0, 16), :] = src[pl.ds(i * 20 + 2, 16), :]


def coef_x_kernel(c1, ylo, yhi, ec, slo, shi):
    coarse_own(ec, c1)
    for src, crow in ((ylo, CY0 - 9), (yhi, CY0 + 16)):
        for r in range(9):
            ec[every(9 * YR + crow + r, 32, YR), :] = src[plane(r, 32), :]
    slo[...] = ec[pl.ds(9 * YR, 9 * YR), :]
    shi[...] = ec[pl.ds(32 * YR, 9 * YR), :]


def rhs_x_kernel(rc, v, ylo, yhi, er, vs, slo, shi):
    lane = lane_of(YR)
    coarse_own(er, rc)
    vs[...] = v[...]
    for src, crow, frow in ((ylo, CY0 - 9, FY0 - 3), (yhi, CY0 + 16, FY0 + 32)):
        for r in range(9):
            w = src[plane(r, 32), :]
            er[every(9 * YR + crow + r, 32, YR), :] = w
            if r < 6:
                start = (3 + 32 * (r // 3)) * YR + frow + r % 3
                vs[every(start, 32, YR), :] = own_lanes(rl(w, -32))
    for dst, first, fine in ((slo, 9, 3), (shi, 32, 64)):
        for i in range(9):
            w = er[plane(first + i), :]
            if i < 3:
                w = jnp.where(lane < 64, w, rl(own_lanes(vs[plane(fine + i), :]), 32))
            dst[plane(i), :] = w


def coef_slot(which, x):
    n = which * 50 + x
    return plane(n // 7), 18 * (n % 7)


def coef_z_kernel(ec0, xlo, xhi, ec, zlo, zhi):
    lane = lane_of(YR)
    ec[...] = ec0[...]
    ec[pl.ds(0, 9 * YR), :] = xlo[...]
    ec[pl.ds(41 * YR, 9 * YR), :] = xhi[...]
    lo = hi = None
    for n in range(100):
        at = 18 * (n % 7)
        if at == 0:
            lo = jnp.zeros((YR, 128), F32)
            hi = lo
        w = ec[plane(n % 50), :]
        base = 64 * (n // 50)
        here = (lane >= at) & (lane < at + 18)
        lo = jnp.where(here, rl(w, at - base), lo)
        hi = jnp.where(here, rl(w, at - base - 46), hi)
        if at == 108 or n == 99:
            zlo[plane(n // 7), :] = lo
            zhi[plane(n // 7), :] = hi


def rhs_z_kernel(er, vs0, xlo, xhi, rm, vs, zlo, zhi):
    lane = lane_of(YR)
    even = lane % 2 == 0
    own = (lane >= Z0) & (lane < Z0 + 64)
    vs[...] = vs0[...]
    for src, fine in ((xlo, 0), (xhi, 67)):
        for i in range(3):
            vs[plane(fine + i), :] = own_lanes(rl(src[plane(i), :], -32))
    lo = hi = None
    for n in range(25):
        at = 27 * (n % 4)
        if at == 0:
            lo = jnp.zeros((YR, 128), F32)
            hi = lo
        first = xlo[plane(n), :] if n < 9 else er[plane(n), :]
        second = xhi[plane(n - 16), :] if n >= 16 else er[plane(n + 25), :]
        w = rl(jnp.where(even, first, second), 32)
        rm[plane(n), :] = jnp.where(own, w, 0.0)
        here = (lane >= at) & (lane < at + 18)
        lo = jnp.where(here, rl(w, at - Z0), lo)
        hi = jnp.where(here, rl(w, at - Z0 - 46), hi)
        for i in range(3):
            if 3 * n + i < FXN:
                w = vs[plane(3 * n + i), :]
                to = at + 18 + 3 * i
                here = (lane >= to) & (lane < to + 3)
                lo = jnp.where(here, rl(w, to - Z0), lo)
                hi = jnp.where(here, rl(w, to - Z0 - 61), hi)
        if at == 81 or n == 24:
            zlo[plane(n // 4), :] = lo
            zhi[plane(n // 4), :] = hi


MXN = 28
CC = 1


def merge_kernel(ec, zlo, zhi, cx, cy, cz, jr, jb):
    lane = lane_of(YR)
    even = lane % 2 == 0
    own = (lane >= Z0) & (lane < Z0 + 64)
    below = (lane >= Z0 - 18) & (lane < Z0)
    above = (lane >= Z0 + 64) & (lane < Z0 + 82)
    nothing = jnp.zeros((YR, 128), F32)
    row = lax.broadcasted_iota(jnp.int32, (YR, 128), 0)
    colour = (row + lane // 2 + 1) % 2

    def load(which, x):
        if not 0 <= x < CXN:
            return nothing
        group, at = coef_slot(which, x)
        w = jnp.where(own, rl(ec[plane(x), :], 32 - 64 * which), 0.0)
        w = jnp.where(below, rl(zlo[group, :], Z0 - 18 - at), w)
        return jnp.where(above, rl(zhi[group, :], Z0 + 64 - at), w)

    for p in range(27):
        first, second = load(0, p - 1), load(0, p + 24)
        cx[plane(p), :] = 0.25 * jnp.where(even, first, rl(second, 1))
        cy[plane(p), :] = 0.25 * jnp.where(even, rl(first, -1), second)
        first, second = load(1, p - 1), load(1, p + 24)
        cz[plane(p), :] = 0.25 * jnp.where(even, first, rl(second, 1))
        diag = jnp.where(even, rl(first, -1), second)
        inside = diag > 0.0
        one = jnp.where(inside, 1.0 / jnp.where(inside, diag, 1.0), 0.0)
        isred = jnp.where(even, colour + p - 1, colour + p + 24) % 2 == 0
        jr[plane(p), :] = jnp.where(isred, one, 0.0)
        jb[plane(p), :] = jnp.where(isred, 0.0, one)
    for ref in (cx, cy, cz, jr, jb):
        ref[plane(27), :] = nothing


def finish_kernel(
    rm, vs, zlo, zhi, cx, cy, cz, jr, jb, f, fx, fy, fz, ir, ib, dg, out, res, cf, red, blk, v, w0, tmp
):
    lane = lane_of(YR)
    even = lane % 2 == 0
    below = (lane >= Z0 - 18) & (lane < Z0)
    above = (lane >= Z0 + 64) & (lane < Z0 + 82)
    nothing = jnp.zeros((YR, 128), F32)
    for ref in (cf, red, blk):
        for p in (0, 26, 27):
            ref[plane(p), :] = nothing
    for n in range(25):
        at = 27 * (n % 4)
        w = jnp.where(below, rl(zlo[plane(n // 4), :], Z0 - 18 - at), rm[plane(n), :])
        w = jnp.where(above, rl(zhi[plane(n // 4), :], Z0 + 64 - at), w)
        cf[plane(n + 1), :] = w
        red[plane(n + 1), :] = w * jr[plane(n + 1), :]
    for n in range(FXN):
        at = 27 * (n // 3 % 4) + 18 + 3 * (n % 3)
        group = plane(n // 12)
        w = own_lanes(vs[plane(n), :])
        low = rl(zlo[group, :], Z0 - 3 - at)
        high = rl(zhi[group, :], Z0 + 64 - at)
        w = jnp.where((lane >= Z0 - 3) & (lane < Z0), low, w)
        v[plane(n), :] = jnp.where((lane >= Z0 + 64) & (lane < Z0 + 67), high, w)

    def seam(ref):
        ref[plane(26), :] = jnp.where(even, rl(ref[plane(1), :], -1), 0.0)
        ref[plane(0), :] = jnp.where(even, 0.0, rl(ref[plane(25), :], 1))

    seam(red)

    for half in range(1, 8):
        src, dst, inv = (red, blk, jb) if half % 2 else (blk, red, jr)

        @steps(26 // CC)
        def _(k):
            x = 1 + k * CC
            at = span(x, CC)
            dst[at, :] = (cf[at, :] + nb_sum(x, CC, cx, cy, cz, src, 2)) * inv[at, :]

        seam(dst)

    for i in range(-2, 34):
        p = i + 10 if i + 9 < 25 else i + 9 - 24
        c = red[plane(p), :] + blk[plane(p), :]
        c = jnp.where(even, c, rl(c, 1)) if i + 9 < 25 else jnp.where(even, rl(c, -1), c)
        c = c[CY0 - 2 : CY0 + 18]
        slot = (i % 8) * YR
        tmp[every(slot, 20, 2), :] = c
        tmp[every(slot + 1, 20, 2), :] = c
        spread = tmp[pl.ds(slot, YR), :]
        for x in (2 * i + 3, 2 * i + 4):
            if 0 <= x < FXN:
                v[plane(x), :] = v[plane(x), :] + spread

    w0[plane(0), :] = nothing
    w0[plane(FXN - 1), :] = nothing

    @steps(STEPS)
    def _(k):
        x = 1 + k * FS
        at = span(x, FS)
        w0[at, :] = (f[at, :] + nb_sum(x, FS, fx, fy, fz, v, 1)) * ir[at, :]

    @steps(STEPS)
    def _(k):
        x = 1 + k * FS
        at = span(x, FS)
        new = (f[at, :] + nb_sum(x, FS, fx, fy, fz, w0, 1)) * ib[at, :]
        v[at, :] = new + w0[at, :]

    def crop(w):
        return rl(w, -32).reshape(FC, YR, 128)[:, FY0 : FY0 + 32, :64]

    @steps(64 // FC)
    def _(k):
        x = 3 + k * FC
        at = span(x, FC)
        w = v[at, :]
        r = f[at, :] - (dg[at, :] * w - nb_sum(x, FC, fx, fy, fz, v, 1))
        out[pl.ds(k * FC, FC)] = crop(w)
        res[pl.ds(k * FC, FC)] = crop(r)


def swap(low, high, axis):
    count = lax.axis_size(axis)
    up = [(i, i + 1) for i in range(count - 1)]
    down = [(i + 1, i) for i in range(count - 1)]
    return lax.ppermute(high, axis, up), lax.ppermute(low, axis, down)


def body(rhs_boxes, a_boxes, b_boxes, new_place):
    exchange = functools.partial(
        lax.all_to_all, axis_name=LAYER, split_axis=0, concat_axis=0, tiled=True
    )
    (spread,) = call(spread_kernel, [(32, 104, 128)], smem=1)(
        new_place, rhs_boxes, a_boxes, b_boxes
    )
    got = exchange(spread)
    place = got[:, 96, :4].astype(jnp.int32)
    (routed,) = call(route_kernel, [(32, 12, 8, 128)], smem=1)(place, got)
    got = exchange(routed)

    fine = (FXN * YR, 128)
    coarse = (CXN * YR, 128)
    rh, aa, bb, ylo, yhi, xlo, xhi = call(
        brick_kernel, [fine] * 3 + [(288, 128)] * 2 + [(9 * YR, 128)] * 2
    )(got)
    ylo, yhi = swap(ylo, yhi, "gy")
    xlo, xhi = call(fine_x_kernel, [(5 * YR, 128)] * 2, [(9 * YR, 128)] * 2)(xlo, xhi, ylo, yhi)
    xlo, xhi = swap(xlo, xhi, "gx")
    rh, aa, bb, zlo, zhi = call(fine_z_kernel, [fine] * 3 + [(5 * YR, 128)] * 2)(
        rh, aa, bb, ylo, yhi, xlo, xhi
    )
    zlo, zhi = swap(zlo, zhi, "gz")
    f, fx, fy, fz, ir, ib, dg, v, c1, cylo, cyhi = call(
        coefficient_kernel,
        [fine] * 8 + [(640, 128)] + [(9 * 32, 128)] * 2,
        [fine, fine] + [(33 * YR, 128)] * 4,
        us=8,
    )(rh, aa, bb, zlo, zhi)
    cylo, cyhi = swap(cylo, cyhi, "gy")
    v, rc, ylo, yhi = call(
        presmooth_kernel,
        [fine, (640, 128)] + [(9 * 32, 128)] * 2,
        [(32 * YR, 128)],
        us=6,
    )(f, fx, fy, fz, ib, dg, v)
    cylo, cyhi, rc = lax.optimization_barrier((cylo, cyhi, rc))
    ylo, yhi = swap(ylo, yhi, "gy")
    ec, cxlo, cxhi = call(coef_x_kernel, [coarse] + [(9 * YR, 128)] * 2, us=1)(c1, cylo, cyhi)
    cxlo, cxhi = swap(cxlo, cxhi, "gx")
    er, vs, xlo, xhi = call(rhs_x_kernel, [coarse, fine] + [(9 * YR, 128)] * 2, us=1)(
        rc, v, ylo, yhi
    )
    xlo, xhi = swap(xlo, xhi, "gx")
    ec, czlo, czhi = call(coef_z_kernel, [coarse] + [(15 * YR, 128)] * 2)(ec, cxlo, cxhi)
    czlo, czhi = swap(czlo, czhi, "gz")
    rm, vs, zlo, zhi = call(
        rhs_z_kernel, [(25 * YR, 128), fine] + [(7 * YR, 128)] * 2
    )(er, vs, xlo, xhi)
    zlo, zhi = swap(zlo, zhi, "gz")
    merged = (MXN * YR, 128)
    coefs = call(merge_kernel, [merged] * 5, us=5)(ec, czlo, czhi)
    return tuple(
        call(
            finish_kernel,
            [(64, 32, 64)] * 2,
            [merged] * 3 + [fine, fine, (8 * YR, 128)],
            us=8,
        )(rm, vs, zlo, zhi, *coefs, f, fx, fy, fz, ir, ib, dg)
    )


def solution(mesh):
    return jax.shard_map(
        body,
        mesh=mesh,
        in_specs=(
            P("gz", ("gx", "gy"), None),
            P("gz", ("gx", "gy"), None),
            P("gz", ("gx", "gy"), None),
            P("gz", ("gx", "gy")),
        ),
        out_specs=(P("gx", "gy", "gz"), P("gx", "gy", "gz")),
        check_vma=False,
    )
```

time: 275 us -> 207 us (0.75)
  Pallas kernels: 99.5 us -> 36.5 us
  waiting for transfers between devices: 37.6 us -> 17.7 us
  starting transfers between devices: 36.3 us -> 53.5 us
    pallas_call x9 -> x13, Pallas kernels: 99.5 us -> 36.5 us  [run(): pl.pallas_call(kernel, out_shape=[jax.ShapeDtypeStruct(s, F32) for s in o...]
    ppermute x12 -> x18, waiting for transfers between devices: 37.6 us -> 17.7 us  [swap(): return (lax.ppermute(high, axis, up), lax.ppermute(low, axis, down))]
    ppermute x12 -> x18, starting transfers between devices: 36.3 us -> 53.5 us  [swap(): return (lax.ppermute(high, axis, up), lax.ppermute(low, axis, down))]
  transfers between devices with their start and end apart: 12 -> 18, of which waited for: 11 -> 8; matrix products, arithmetic and copies ran while one was open for 0% -> 0% of each run, Pallas kernels for 0% -> 6%
where the time goes in v2:
time: 207 us; the launch traced here: 206 us
  blocking collectives  93.6 us (45%)
  starting transfers between devices  53.5 us (26%)
  Pallas kernels  36.5 us (18%)
  waiting for transfers between devices  17.7 us (9%)
  local copies, waits for them, and re-layouts  3.77 us (2%)
    ppermute x18, starting transfers between devices, swap(): return (lax.ppermute(high, axis, up), lax.ppermute(low, axis, down))  53.5 us
    all_to_all x1, blocking collectives, body(): got = exchange(spread)  50.7 us
    all_to_all x1, blocking collectives, body(): got = exchange(routed)  42.9 us
    pallas_call x13, Pallas kernels, run(): pl.pallas_call(kernel, out_shape=[jax.ShapeDtypeStruct(s, F32) for s in o...  36.5 us
    ppermute x18, waiting for transfers between devices, swap(): return (lax.ppermute(high, axis, up), lax.ppermute(low, axis, down))  17.7 us
  transfers between devices with their start and end apart: 18, of which 8 were waited for; matrix products, arithmetic and copies ran while one was open for 0% of the time, Pallas kernels for 6%

profile of v2, /device:TPU:41, one launch (start us, length us, event | category | flops | bytes accessed | tf_op | source)
XLA Modules:
  0.0 206.1 jit_solution(18197931586754019947)
XLA Ops:
  0.6 1.0 copy-done
  1.7 1.0 copy-done.1
  2.7 1.0 copy-done.2
  3.8 0.7 copy-done.3
  4.4 1.1 shard_map.59
  5.6 50.7 %all_to_all.10.got = f32[32,104,128]{2,1,0:T(8,128)S(1)} all-to-all(f32[32,104,128]{2,1,0:T(8,128)S(1)} %shard_map.59), channel_id=1, replica_groups=mesh['gx'=8,'gy'=4,'gz'=8] {'gx','gy'}, dimensions={0} | all-to-all | bytes 3407872 | tf_op jit(solution)/shard_map/all_to_all | solution.py:565
  56.2 1.3 shard_map.60
  57.5 42.9 %all_to_all.11.got = f32[32,12,8,128]{3,2,1,0:T(8,128)S(1)} all-to-all(f32[32,12,8,128]{3,2,1,0:T(8,128)S(1)} %shard_map.60), channel_id=1, replica_groups=mesh['gx'=8,'gy'=4,'gz'=8] {'gx','gy'}, dimensions={0} | all-to-all | bytes 3145728 | tf_op jit(solution)/shard_map/all_to_all | solution.py:568
  100.5 3.9 %shard_map.61 = (f32[2800,128]{1,0:T(8,128)S(1)}, f32[2800,128]{1,0:T(8,128)S(1)}, f32[2800,128]{1,0:T(8,128)S(1)}, f32[288,128]{1,0:T(8,128)S(1)}, f32[288,128]...) custom-call(f32[32,12,8,128]{3,2,1,0:T(8,128)S(1)} %all_to_all.11.got), custom_call_target="tpu_custom_call" | custom-call | bytes 6000000 | tf_op jit(solution)/shard_map/pallas_call | solution.py:50
  104.4 2.6 %collective-permute-start = (f32[288,128]{1,0:T(8,128)S(1)}, f32[288,128]{1,0:T(8,128)S(1)}, u32[]{:S(2)}, u32[]{:S(2)}) collective-permute-start(f32[288,128]{1,0:T(8,128)S(1)} %get-tuple-element.56), channel_id=1, source_target_pairs={{0,8},{8,16},{16,24},{1,9},{9,17},{17,25},{2,10},{10,18},{18,26},{... | collective-permute-start | bytes 442376 | tf_op jit(solution)/shard_map/ppermute | solution.py:555
  107.0 1.3 collective-permute-start.1
  108.3 0.8 collective-permute-done.ylo
  109.1 3.8 %collective-permute-done.1.yhi = f32[288,128]{1,0:T(8,128)S(1)} collective-permute-done((f32[288,128]{1,0:T(8,128)S(1)}, f32[288,128]{1,0:T(8,128)S(1)}, u32[]{:S(2)}, u32[]{:S(2)}) %collective-permute-start.1) | collective-permute-done | bytes 147488 | tf_op jit(solution)/shard_map/ppermute | solution.py:555
  112.9 0.3 shard_map.62
  113.1 2.2 %collective-permute-start.2 = (f32[200,128]{1,0:T(8,128)S(1)}, f32[200,128]{1,0:T(8,128)S(1)}, u32[]{:S(2)}, u32[]{:S(2)}) collective-permute-start(f32[200,128]{1,0:T(8,128)S(1)} %get-tuple-element.60), channel_id=1, source_target_pairs={{0,32},{32,64},{64,96},{96,128},{128,160},{160,192},{192,224},{1,3... | collective-permute-start | bytes 307208 | tf_op jit(solution)/shard_map/ppermute | solution.py:555
  115.4 3.1 %collective-permute-start.3 = (f32[200,128]{1,0:T(8,128)S(1)}, f32[200,128]{1,0:T(8,128)S(1)}, u32[]{:S(2)}, u32[]{:S(2)}) collective-permute-start(f32[200,128]{1,0:T(8,128)S(1)} %get-tuple-element.61), channel_id=1, source_target_pairs={{32,0},{64,32},{96,64},{128,96},{160,128},{192,160},{224,192},{33,... | collective-permute-start | bytes 307208 | tf_op jit(solution)/shard_map/ppermute | solution.py:555
  118.4 0.1 collective-permute-done.2.xlo
  118.5 2.2 %collective-permute-done.3.xhi = f32[200,128]{1,0:T(8,128)S(1)} collective-permute-done((f32[200,128]{1,0:T(8,128)S(1)}, f32[200,128]{1,0:T(8,128)S(1)}, u32[]{:S(2)}, u32[]{:S(2)}) %collective-permute-start.3) | collective-permute-done | bytes 102432 | tf_op jit(solution)/shard_map/ppermute | solution.py:555
  120.8 2.7 %shard_map.63 = (f32[2800,128]{1,0:T(8,128)S(1)}, f32[2800,128]{1,0:T(8,128)S(1)}, f32[2800,128]{1,0:T(8,128)S(1)}, f32[200,128]{1,0:T(8,128)S(1)}, f32[200,128]{1,0:T(8,128)S(1)}) custom-call(f32[2800,128]{1,0:T(8,128)S(1)} %get-tuple-element.53.rh0, f32[2800,128]{1,0:T(8,128)S(1)} %get-tuple-element.54.aa0, f32[2800,128]{1,0:T(8,128)S(1)} %get-tuple-element.55.bb0, ...), custom_call_target="tpu_custom_call" | custom-call | bytes 6000000 | tf_op jit(solution)/shard_map/pallas_call | solution.py:50
  123.5 9.5 %collective-permute-start.4 = (f32[200,128]{1,0:T(8,128)S(1)}, f32[200,128]{1,0:T(8,128)S(1)}, u32[]{:S(2)}, u32[]{:S(2)}) collective-permute-start(f32[200,128]{1,0:T(8,128)S(1)} %get-tuple-element.65), channel_id=1, source_target_pairs={{0,1},{1,2},{2,3},{3,4},{4,5},{5,6},{6,7},{8,9},{9,10},{10,11},{11... | collective-permute-start | bytes 307208 | tf_op jit(solution)/shard_map/ppermute | solution.py:555
  133.0 1.9 collective-permute-start.5
  134.9 4.0 %collective-permute-done.5.zhi = f32[200,128]{1,0:T(8,128)S(1)} collective-permute-done((f32[200,128]{1,0:T(8,128)S(1)}, f32[200,128]{1,0:T(8,128)S(1)}, u32[]{:S(2)}, u32[]{:S(2)}) %collective-permute-start.5) | collective-permute-done | bytes 102432 | tf_op jit(solution)/shard_map/ppermute | solution.py:555
  139.0 5.5 %shard_map.64 = (f32[2800,128]{1,0:T(8,128)S(1)}, f32[2800,128]{1,0:T(8,128)S(1)}, f32[2800,128]{1,0:T(8,128)S(1)}, f32[2800,128]{1,0:T(8,128)S(1)}, f32[2800,12...) custom-call(f32[2800,128]{1,0:T(8,128)S(1)} %get-tuple-element.62.rh, ...), custom_call_target="tpu_custom_call" | custom-call | bytes 24000000 | tf_op jit(solution)/shard_map/pallas_call | solution.py:50
  144.5 2.8 %collective-permute-start.6 = (f32[288,128]{1,0:T(8,128)S(1)}, f32[288,128]{1,0:T(8,128)S(1)}, u32[]{:S(2)}, u32[]{:S(2)}) collective-permute-start(f32[288,128]{1,0:T(8,128)S(1)} %get-tuple-element.67), channel_id=1, source_target_pairs={{0,8},{8,16},{16,24},{1,9},{9,17},{17,25},{2,10},{10,18},{18,26},{... | collective-permute-start | bytes 442376 | tf_op jit(solution)/shard_map/ppermute | solution.py:555
  147.3 1.5 collective-permute-start.7
  148.7 3.3 %shard_map.65 = (f32[2800,128]{1,0:T(8,128)S(1)}, f32[640,128]{1,0:T(8,128)S(1)}, f32[288,128]{1,0:T(8,128)S(1)}, f32[288,128]{1,0:T(8,128)S(1)}) custom-call(f32[2800,128]{1,0:T(8,128)S(1)} %get-tuple-element.69.f, f32[2800,128]{1,0:T(8,128)S(1)} %get-tuple-element.70.fx, f32[2800,128]{1,0:T(8,128)S(1)} %get-tuple-element.71.fy, ...), custom_call_target="tpu_custom_call" | custom-call | bytes 18000000 | tf_op jit(solution)/shard_map/pallas_call | solution.py:50
  152.1 2.1 %collective-permute-done.7.yhi = f32[288,128]{1,0:T(8,128)S(1)} collective-permute-done((f32[288,128]{1,0:T(8,128)S(1)}, f32[288,128]{1,0:T(8,128)S(1)}, u32[]{:S(2)}, u32[]{:S(2)}) %collective-permute-start.7) | collective-permute-done | bytes 147488 | tf_op jit(solution)/shard_map/ppermute | solution.py:555
  154.2 0.1 shard_map.68
  154.4 2.3 %collective-permute-start.14 = (f32[360,128]{1,0:T(8,128)S(1)}, f32[360,128]{1,0:T(8,128)S(1)}, u32[]{:S(2)}, u32[]{:S(2)}) collective-permute-start(f32[360,128]{1,0:T(8,128)S(1)} %get-tuple-element.93), channel_id=1, source_target_pairs={{0,32},{32,64},{64,96},{96,128},{128,160},{160,192},{192,224},{1,3... | collective-permute-start | bytes 552968 | tf_op jit(solution)/shard_map/ppermute | solution.py:555
  156.6 3.0 %collective-permute-start.15 = (f32[360,128]{1,0:T(8,128)S(1)}, f32[360,128]{1,0:T(8,128)S(1)}, u32[]{:S(2)}, u32[]{:S(2)}) collective-permute-start(f32[360,128]{1,0:T(8,128)S(1)} %get-tuple-element.94), channel_id=1, source_target_pairs={{32,0},{64,32},{96,64},{128,96},{160,128},{192,160},{224,192},{33,... | collective-permute-start | bytes 552968 | tf_op jit(solution)/shard_map/ppermute | solution.py:555
  159.7 3.0 %collective-permute-start.8 = (f32[288,128]{1,0:T(8,128)S(1)}, f32[288,128]{1,0:T(8,128)S(1)}, u32[]{:S(2)}, u32[]{:S(2)}) collective-permute-start(f32[288,128]{1,0:T(8,128)S(1)} %get-tuple-element.79), channel_id=1, source_target_pairs={{0,8},{8,16},{16,24},{1,9},{9,17},{17,25},{2,10},{10,18},{18,26},{... | collective-permute-start | bytes 442376 | tf_op jit(solution)/shard_map/ppermute | solution.py:555
  162.6 1.3 collective-permute-start.9
  163.9 1.1 collective-permute-done.8.ylo
  165.0 3.5 %collective-permute-done.9.yhi = f32[288,128]{1,0:T(8,128)S(1)} collective-permute-done((f32[288,128]{1,0:T(8,128)S(1)}, f32[288,128]{1,0:T(8,128)S(1)}, u32[]{:S(2)}, u32[]{:S(2)}) %collective-permute-start.9) | collective-permute-done | bytes 147488 | tf_op jit(solution)/shard_map/ppermute | solution.py:555
  168.5 0.3 shard_map.66
  168.8 2.4 %collective-permute-start.10 = (f32[360,128]{1,0:T(8,128)S(1)}, f32[360,128]{1,0:T(8,128)S(1)}, u32[]{:S(2)}, u32[]{:S(2)}) collective-permute-start(f32[360,128]{1,0:T(8,128)S(1)} %get-tuple-element.83), channel_id=1, source_target_pairs={{0,32},{32,64},{64,96},{96,128},{128,160},{160,192},{192,224},{1,3... | collective-permute-start | bytes 552968 | tf_op jit(solution)/shard_map/ppermute | solution.py:555
  171.2 2.9 %collective-permute-start.11 = (f32[360,128]{1,0:T(8,128)S(1)}, f32[360,128]{1,0:T(8,128)S(1)}, u32[]{:S(2)}, u32[]{:S(2)}) collective-permute-start(f32[360,128]{1,0:T(8,128)S(1)} %get-tuple-element.84), channel_id=1, source_target_pairs={{32,0},{64,32},{96,64},{128,96},{160,128},{192,160},{224,192},{33,... | collective-permute-start | bytes 552968 | tf_op jit(solution)/shard_map/ppermute | solution.py:555
  174.1 0.0 collective-permute-done.15.xhi
  174.1 1.1 shard_map.69
  175.3 6.1 %collective-permute-start.16 = (f32[600,128]{1,0:T(8,128)S(1)}, f32[600,128]{1,0:T(8,128)S(1)}, u32[]{:S(2)}, u32[]{:S(2)}) collective-permute-start(f32[600,128]{1,0:T(8,128)S(1)} %get-tuple-element.96), channel_id=1, source_target_pairs={{0,1},{1,2},{2,3},{3,4},{4,5},{5,6},{6,7},{8,9},{9,10},{10,11},{11... | collective-permute-start | bytes 921608 | tf_op jit(solution)/shard_map/ppermute | solution.py:555
  181.4 1.9 collective-permute-start.17
  183.3 0.0 collective-permute-done.11.xhi
  183.3 2.7 %shard_map.67 = (f32[1000,128]{1,0:T(8,128)S(1)}, f32[2800,128]{1,0:T(8,128)S(1)}, f32[280,128]{1,0:T(8,128)S(1)}, f32[280,128]{1,0:T(8,128)S(1)}) custom-call(f32[2000,128]{1,0:T(8,128)S(1)} %get-tuple-element.81.er, f32[2800,128]{1,0:T(8,128)S(1)} %get-tuple-element.82.vs0, f32[360,128]{1,0:T(8,128)S(1)} %collective-permute-done.10.xlo, ...), custom_call_target="tpu_custom_call" | custom-call | bytes 6000000 | tf_op jit(solution)/shard_map/pallas_call | solution.py:50
  186.0 3.6 %collective-permute-start.12 = (f32[280,128]{1,0:T(8,128)S(1)}, f32[280,128]{1,0:T(8,128)S(1)}, u32[]{:S(2)}, u32[]{:S(2)}) collective-permute-start(f32[280,128]{1,0:T(8,128)S(1)} %get-tuple-element.87), channel_id=1, source_target_pairs={{0,1},{1,2},{2,3},{3,4},{4,5},{5,6},{6,7},{8,9},{9,10},{10,11},{11... | collective-permute-start | bytes 430088 | tf_op jit(solution)/shard_map/ppermute | solution.py:555
  189.7 2.1 %collective-permute-start.13 = (f32[280,128]{1,0:T(8,128)S(1)}, f32[280,128]{1,0:T(8,128)S(1)}, u32[]{:S(2)}, u32[]{:S(2)}) collective-permute-start(f32[280,128]{1,0:T(8,128)S(1)} %get-tuple-element.88), channel_id=1, source_target_pairs={{1,0},{2,1},{3,2},{4,3},{5,4},{6,5},{7,6},{9,8},{10,9},{11,10},{12... | collective-permute-start | bytes 430088 | tf_op jit(solution)/shard_map/ppermute | solution.py:555
  191.8 0.0 collective-permute-done.17.zhi
  191.8 5.4 %shard_map.70 = (f32[1120,128]{1,0:T(8,128)S(1)}, f32[1120,128]{1,0:T(8,128)S(1)}, f32[1120,128]{1,0:T(8,128)S(1)}, f32[1120,128]{1,0:T(8,128)S(1)}, f32[1120,128]{1,0:T(8,128)S(1)}) custom-call(f32[2000,128]{1,0:T(8,128)S(1)} %get-tuple-element.95.ec, f32[600,128]{1,0:T(8,128)S(1)} %collective-permute-done.16.zlo, f32[600,128]{1,0:T(8,128)S(1)} %collective-permute-done.17.zhi), custom_call_target="tpu_custom_call" | custom-call | bytes 15000000 | tf_op jit(solution)/shard_map/pallas_call | solution.py:50
  197.3 8.8 %shard_map.71 = (f32[64,32,64]{2,1,0:T(8,128)}, f32[64,32,64]{2,1,0:T(8,128)}) custom-call(f32[1000,128]{1,0:T(8,128)S(1)} %get-tuple-element.85.rm, f32[2800,128]{1,0:T(8,128)S(1)} %get-tuple-element.86.vs, f32[280,128]{1,0:T(8,128)S(1)} %collective-permute-done.12.zlo, f32[280,128]{1,0:T(8,128)S(1)} %collective-permute-done.13.zhi, ...), custom_call_target="tpu_custom_call" | custom-call | bytes 24000000 | tf_op jit(solution)/shard_map/pallas_call | solution.py:50
  (12 shorter events, 0.0 us)
Async XLA Ops:
  0.6 1.0 copy-start
  1.7 1.0 copy-start.1
  2.7 1.0 copy-start.2
  3.8 0.7 copy-start.3
  104.4 4.7 %collective-permute-start = (f32[288,128]{1,0:T(8,128)S(1)}, f32[288,128]{1,0:T(8,128)S(1)}, u32[]{:S(2)}, u32[]{:S(2)}) collective-permute-start(f32[288,128]{1,0:T(8,128)S(1)} %get-tuple-element.56), channel_id=1, source_target_pairs={{0,8},{8,16},{16,24},{1,9},{9,17},{17,25},{2,10},{10,18},{18,26},{... | collective-permute-start | bytes 442376 | tf_op jit(solution)/shard_map/ppermute | solution.py:555
  107.0 5.9 %collective-permute-start.1 = (f32[288,128]{1,0:T(8,128)S(1)}, f32[288,128]{1,0:T(8,128)S(1)}, u32[]{:S(2)}, u32[]{:S(2)}) collective-permute-start(f32[288,128]{1,0:T(8,128)S(1)} %get-tuple-element.57), channel_id=1, source_target_pairs={{8,0},{16,8},{24,16},{9,1},{17,9},{25,17},{10,2},{18,10},{26,18},{... | collective-permute-start | bytes 442376 | tf_op jit(solution)/shard_map/ppermute | solution.py:555
  113.1 5.4 %collective-permute-start.2 = (f32[200,128]{1,0:T(8,128)S(1)}, f32[200,128]{1,0:T(8,128)S(1)}, u32[]{:S(2)}, u32[]{:S(2)}) collective-permute-start(f32[200,128]{1,0:T(8,128)S(1)} %get-tuple-element.60), channel_id=1, source_target_pairs={{0,32},{32,64},{64,96},{96,128},{128,160},{160,192},{192,224},{1,3... | collective-permute-start | bytes 307208 | tf_op jit(solution)/shard_map/ppermute | solution.py:555
  115.4 5.4 %collective-permute-start.3 = (f32[200,128]{1,0:T(8,128)S(1)}, f32[200,128]{1,0:T(8,128)S(1)}, u32[]{:S(2)}, u32[]{:S(2)}) collective-permute-start(f32[200,128]{1,0:T(8,128)S(1)} %get-tuple-element.61), channel_id=1, source_target_pairs={{32,0},{64,32},{96,64},{128,96},{160,128},{192,160},{224,192},{33,... | collective-permute-start | bytes 307208 | tf_op jit(solution)/shard_map/ppermute | solution.py:555
  123.5 11.5 %collective-permute-start.4 = (f32[200,128]{1,0:T(8,128)S(1)}, f32[200,128]{1,0:T(8,128)S(1)}, u32[]{:S(2)}, u32[]{:S(2)}) collective-permute-start(f32[200,128]{1,0:T(8,128)S(1)} %get-tuple-element.65), channel_id=1, source_target_pairs={{0,1},{1,2},{2,3},{3,4},{4,5},{5,6},{6,7},{8,9},{9,10},{10,11},{11... | collective-permute-start | bytes 307208 | tf_op jit(solution)/shard_map/ppermute | solution.py:555
  133.0 6.0 %collective-permute-start.5 = (f32[200,128]{1,0:T(8,128)S(1)}, f32[200,128]{1,0:T(8,128)S(1)}, u32[]{:S(2)}, u32[]{:S(2)}) collective-permute-start(f32[200,128]{1,0:T(8,128)S(1)} %get-tuple-element.66), channel_id=1, source_target_pairs={{1,0},{2,1},{3,2},{4,3},{5,4},{6,5},{7,6},{9,8},{10,9},{11,10},{12... | collective-permute-start | bytes 307208 | tf_op jit(solution)/shard_map/ppermute | solution.py:555
  144.5 7.6 %collective-permute-start.6 = (f32[288,128]{1,0:T(8,128)S(1)}, f32[288,128]{1,0:T(8,128)S(1)}, u32[]{:S(2)}, u32[]{:S(2)}) collective-permute-start(f32[288,128]{1,0:T(8,128)S(1)} %get-tuple-element.67), channel_id=1, source_target_pairs={{0,8},{8,16},{16,24},{1,9},{9,17},{17,25},{2,10},{10,18},{18,26},{... | collective-permute-start | bytes 442376 | tf_op jit(solution)/shard_map/ppermute | solution.py:555
  147.3 6.9 %collective-permute-start.7 = (f32[288,128]{1,0:T(8,128)S(1)}, f32[288,128]{1,0:T(8,128)S(1)}, u32[]{:S(2)}, u32[]{:S(2)}) collective-permute-start(f32[288,128]{1,0:T(8,128)S(1)} %get-tuple-element.68), channel_id=1, source_target_pairs={{8,0},{16,8},{24,16},{9,1},{17,9},{25,17},{10,2},{18,10},{26,18},{... | collective-permute-start | bytes 442376 | tf_op jit(solution)/shard_map/ppermute | solution.py:555
  154.4 19.8 %collective-permute-start.14 = (f32[360,128]{1,0:T(8,128)S(1)}, f32[360,128]{1,0:T(8,128)S(1)}, u32[]{:S(2)}, u32[]{:S(2)}) collective-permute-start(f32[360,128]{1,0:T(8,128)S(1)} %get-tuple-element.93), channel_id=1, source_target_pairs={{0,32},{32,64},{64,96},{96,128},{128,160},{160,192},{192,224},{1,3... | collective-permute-start | bytes 552968 | tf_op jit(solution)/shard_map/ppermute | solution.py:555
  156.6 17.5 %collective-permute-start.15 = (f32[360,128]{1,0:T(8,128)S(1)}, f32[360,128]{1,0:T(8,128)S(1)}, u32[]{:S(2)}, u32[]{:S(2)}) collective-permute-start(f32[360,128]{1,0:T(8,128)S(1)} %get-tuple-element.94), channel_id=1, source_target_pairs={{32,0},{64,32},{96,64},{128,96},{160,128},{192,160},{224,192},{33,... | collective-permute-start | bytes 552968 | tf_op jit(solution)/shard_map/ppermute | solution.py:555
  159.7 5.3 %collective-permute-start.8 = (f32[288,128]{1,0:T(8,128)S(1)}, f32[288,128]{1,0:T(8,128)S(1)}, u32[]{:S(2)}, u32[]{:S(2)}) collective-permute-start(f32[288,128]{1,0:T(8,128)S(1)} %get-tuple-element.79), channel_id=1, source_target_pairs={{0,8},{8,16},{16,24},{1,9},{9,17},{17,25},{2,10},{10,18},{18,26},{... | collective-permute-start | bytes 442376 | tf_op jit(solution)/shard_map/ppermute | solution.py:555
  162.6 5.9 %collective-permute-start.9 = (f32[288,128]{1,0:T(8,128)S(1)}, f32[288,128]{1,0:T(8,128)S(1)}, u32[]{:S(2)}, u32[]{:S(2)}) collective-permute-start(f32[288,128]{1,0:T(8,128)S(1)} %get-tuple-element.80), channel_id=1, source_target_pairs={{8,0},{16,8},{24,16},{9,1},{17,9},{25,17},{10,2},{18,10},{26,18},{... | collective-permute-start | bytes 442376 | tf_op jit(solution)/shard_map/ppermute | solution.py:555
  168.8 14.5 %collective-permute-start.10 = (f32[360,128]{1,0:T(8,128)S(1)}, f32[360,128]{1,0:T(8,128)S(1)}, u32[]{:S(2)}, u32[]{:S(2)}) collective-permute-start(f32[360,128]{1,0:T(8,128)S(1)} %get-tuple-element.83), channel_id=1, source_target_pairs={{0,32},{32,64},{64,96},{96,128},{128,160},{160,192},{192,224},{1,3... | collective-permute-start | bytes 552968 | tf_op jit(solution)/shard_map/ppermute | solution.py:555
  171.2 12.1 %collective-permute-start.11 = (f32[360,128]{1,0:T(8,128)S(1)}, f32[360,128]{1,0:T(8,128)S(1)}, u32[]{:S(2)}, u32[]{:S(2)}) collective-permute-start(f32[360,128]{1,0:T(8,128)S(1)} %get-tuple-element.84), channel_id=1, source_target_pairs={{32,0},{64,32},{96,64},{128,96},{160,128},{192,160},{224,192},{33,... | collective-permute-start | bytes 552968 | tf_op jit(solution)/shard_map/ppermute | solution.py:555
  175.3 16.5 %collective-permute-start.16 = (f32[600,128]{1,0:T(8,128)S(1)}, f32[600,128]{1,0:T(8,128)S(1)}, u32[]{:S(2)}, u32[]{:S(2)}) collective-permute-start(f32[600,128]{1,0:T(8,128)S(1)} %get-tuple-element.96), channel_id=1, source_target_pairs={{0,1},{1,2},{2,3},{3,4},{4,5},{5,6},{6,7},{8,9},{9,10},{10,11},{11... | collective-permute-start | bytes 921608 | tf_op jit(solution)/shard_map/ppermute | solution.py:555
  181.4 10.5 %collective-permute-start.17 = (f32[600,128]{1,0:T(8,128)S(1)}, f32[600,128]{1,0:T(8,128)S(1)}, u32[]{:S(2)}, u32[]{:S(2)}) collective-permute-start(f32[600,128]{1,0:T(8,128)S(1)} %get-tuple-element.97), channel_id=1, source_target_pairs={{1,0},{2,1},{3,2},{4,3},{5,4},{6,5},{7,6},{9,8},{10,9},{11,10},{12... | collective-permute-start | bytes 921608 | tf_op jit(solution)/shard_map/ppermute | solution.py:555
  186.0 11.3 %collective-permute-start.12 = (f32[280,128]{1,0:T(8,128)S(1)}, f32[280,128]{1,0:T(8,128)S(1)}, u32[]{:S(2)}, u32[]{:S(2)}) collective-permute-start(f32[280,128]{1,0:T(8,128)S(1)} %get-tuple-element.87), channel_id=1, source_target_pairs={{0,1},{1,2},{2,3},{3,4},{4,5},{5,6},{6,7},{8,9},{9,10},{10,11},{11... | collective-permute-start | bytes 430088 | tf_op jit(solution)/shard_map/ppermute | solution.py:555
  189.7 7.6 %collective-permute-start.13 = (f32[280,128]{1,0:T(8,128)S(1)}, f32[280,128]{1,0:T(8,128)S(1)}, u32[]{:S(2)}, u32[]{:S(2)}) collective-permute-start(f32[280,128]{1,0:T(8,128)S(1)} %get-tuple-element.88), channel_id=1, source_target_pairs={{1,0},{2,1},{3,2},{4,3},{5,4},{6,5},{7,6},{9,8},{10,9},{11,10},{12... | collective-permute-start | bytes 430088 | tf_op jit(solution)/shard_map/ppermute | solution.py:555

commit v3 on v2

--- a/solution.py
+++ b/solution.py
@@ -63,19 +63,32 @@
     return run
 
 
-def spread_kernel(place, rhs, a, b, out):
+def spread_kernel(place_hbm, rhs, a, b, out, buf, place, sem):
+    first = pltpu.make_async_copy(place_hbm, place, sem.at[12])
+    first.start()
+    copies = []
+    for f, src in enumerate((rhs, a, b)):
+        for part in range(4):
+            at = pl.ds(part * 8192, 8192)
+            copy = pltpu.make_async_copy(
+                src.at[0, :, at], buf.at[f, :, at], sem.at[f * 4 + part]
+            )
+            copy.start()
+            copies.append(copy)
+    first.wait()
     lane = lane_of(8)
     mark = jnp.zeros((8, 128), F32)
     for k in range(4):
         mark = jnp.where(lane == k, place[0, k].astype(F32), mark)
-
-    @pl.loop(0, 32)
-    def _(j):
-        for f, src in enumerate((rhs, a, b)):
-            for m in range(8):
-                col = pl.ds(pl.multiple_of(j * 1024 + m * 128, 128), 128)
-                out[j, f * 32 + m * 4 : f * 32 + m * 4 + 4, :] = src[0, :, col]
+    for j in range(32):
         out[j, 96:104, :] = mark
+    for f in range(3):
+        for part in range(4):
+            copies[f * 4 + part].wait()
+            for j in range(part * 8, part * 8 + 8):
+                for m in range(8):
+                    at = f * 32 + m * 4
+                    out[j, at : at + 4, :] = buf[f, :, j * 1024 + m * 128 : j * 1024 + m * 128 + 128]
 
 
 def route_kernel(place, got, out):
@@ -89,78 +102,115 @@
                 out[t, f * 4 + q] = got[s, every(f * 32 + k, 8, 4), :]
 
 
-def brick_kernel(got, rh, aa, bb, ylo, yhi, xlo, xhi):
+DEPTH = (2, 2, 3)
+FIRST = (0, 2, 4)
+ITEMS = tuple((f, r) for f in range(3) for r in range(DEPTH[f]))
+
+
+def strip_kernel(got, ylo, yhi):
+    quarter = lane_of(32) // 32
+    for f in range(3):
+        for dst, row, first in ((ylo, 0, 0), (yhi, 7, 4 - DEPTH[f])):
+            parts = [got[every((f * 4 + q) * 8 + row, 32, 96), :] for q in range(4)]
+            for r in range(DEPTH[f]):
+                w = rl(parts[0], -32 * (first + r))
+                for q in range(1, 4):
+                    w = jnp.where(quarter == q, rl(parts[q], 32 * (q - first - r)), w)
+                dst[plane(FIRST[f] + r, 32), :] = w
+
+
+def brick_kernel(got, rh, aa, bb, xlo, xhi):
     lane8 = lane_of(8)
     bricks = (rh, aa, bb)
     for br in bricks:
         br[...] = jnp.zeros_like(br)
 
-    @pl.loop(0, 32)
-    def _(j):
+    @pl.loop(0, 16)
+    def _(k):
+        for half in range(2):
+            j = 2 * k + half
+            for f, br in enumerate(bricks):
+                for qx in range(2):
+                    low = got[j, f * 4 + qx * 2]
+                    high = got[j, f * 4 + qx * 2 + 1]
+                    for c in range(4):
+                        w = jnp.where(lane8 < 64, rl(low, 32 - 32 * c), rl(high, 64 - 32 * c))
+                        start = (j + (qx * 32 + 3)) * YR + (FY0 + c)
+                        br[every(start, 8, 4), :] = own_lanes(w)
+
+    for f, br in enumerate(bricks):
+        size = DEPTH[f] * YR
+        xlo[pl.ds(FIRST[f] * YR, size), :] = br[pl.ds(3 * YR, size), :]
+        xhi[pl.ds(FIRST[f] * YR, size), :] = br[pl.ds(67 * YR - size, size), :]
+
+
+def fine_x_kernel(xlo, xhi, ylo, yhi, slo, shi, tlo, thi):
+    lane = lane_of(YR)
+    for own, out, tmp, upper in ((xlo, slo, tlo, False), (xhi, shi, thi, True)):
+        tmp[...] = own[...]
+        for n, (f, r) in enumerate(ITEMS):
+            d = DEPTH[f]
+            at = pl.ds(n * 32 + (32 - d if upper else 0), d)
+            shift = -32 if upper else 32
+            for src, row in ((ylo, FY0 - d + r), (yhi, FY0 + 32 + r)):
+                tmp[every(FIRST[f] * YR + row, d, YR), :] = own_lanes(rl(src[at, :], shift))
+        for m in range(4):
+            v = rl(tmp[plane(2 * m), :], -32)
+            w = rl(tmp[plane(2 * m + 1), :], 32) if m < 3 else jnp.zeros_like(v)
+            out[plane(m), :] = jnp.where(lane < 64, v, w)
+
+
+def z_slot(n):
+    return plane(n // 18), 7 * (n % 18)
+
+
+def fine_y_kernel(rh0, aa0, bb0, ylo, yhi, rh, aa, bb, zlo, zhi):
+    lane = lane_of(YR)
+    bricks = (rh, aa, bb)
+    for br0, br in zip((rh0, aa0, bb0), bricks):
+        br[...] = br0[...]
+    for n, (f, r) in enumerate(ITEMS):
+        for src, row in ((ylo, FY0 - DEPTH[f] + r), (yhi, FY0 + 32 + r)):
+            v = src[plane(n, 32), :]
+            bricks[f][every(3 * YR + row, 32, YR), :] = own_lanes(rl(v, 32))
+            bricks[f][every(35 * YR + row, 32, YR), :] = own_lanes(rl(v, -32))
+    lo = hi = None
+    for n in range(64):
+        group, base = z_slot(n)
+        if base == 0:
+            lo = jnp.zeros((YR, 128), F32)
+            hi = lo
         for f, br in enumerate(bricks):
-            for qx in range(2):
-                low = got[j, f * 4 + qx * 2]
-                high = got[j, f * 4 + qx * 2 + 1]
-                for c in range(4):
-                    both = jnp.where(lane8 < 64, rl(low, 32 - 32 * c), rl(high, 64 - 32 * c))
-                    start = (j + (qx * 32 + 3)) * YR + (FY0 + c)
-                    br[every(start, 8, 4), :] = own_lanes(both)
-
-    lane = lane_of(32)
-    for f, br in enumerate(bricks):
-        for r in range(3):
-            at = pl.ds((f * 3 + r) * 32, 32)
-            for dst, y in ((ylo, r), (yhi, 29 + r)):
-                first = br[every(3 * YR + FY0 + y, 32, YR), :]
-                second = br[every(35 * YR + FY0 + y, 32, YR), :]
-                dst[at, :] = jnp.where(lane < 64, rl(first, -32), rl(second, 32))
-        xlo[pl.ds(f * 3 * YR, 3 * YR), :] = br[pl.ds(3 * YR, 3 * YR), :]
-        xhi[pl.ds(f * 3 * YR, 3 * YR), :] = br[pl.ds(64 * YR, 3 * YR), :]
-
-
-def fine_x_kernel(xlo, xhi, ylo, yhi, slo, shi, tlo, thi):
-    lane = lane_of(YR)
-    for own, out, tmp, base, shift in ((xlo, slo, tlo, 0, 32), (xhi, shi, thi, 29, -32)):
-        tmp[...] = own[...]
-        for f in range(3):
-            for r in range(3):
-                at = pl.ds((f * 3 + r) * 32 + base, 3)
-                tmp[every(f * 3 * YR + FY0 - 3 + r, 3, YR), :] = own_lanes(rl(ylo[at, :], shift))
-                tmp[every(f * 3 * YR + FY0 + 32 + r, 3, YR), :] = own_lanes(rl(yhi[at, :], shift))
-        for m in range(5):
-            v = rl(tmp[plane(2 * m), :], -32)
-            w = rl(tmp[plane(2 * m + 1), :], 32) if m < 4 else jnp.zeros_like(v)
-            out[plane(m), :] = jnp.where(lane < 64, v, w)
-
-
-def fine_z_kernel(rh0, aa0, bb0, ylo, yhi, xlo, xhi, rh, aa, bb, zlo, zhi):
-    lane = lane_of(YR)
-    bricks = (rh, aa, bb)
-    for f, (br0, br) in enumerate(zip((rh0, aa0, bb0), bricks)):
-        br[...] = br0[...]
-        for r in range(3):
-            at = pl.ds((f * 3 + r) * 32, 32)
-            for src, row in ((ylo, FY0 - 3 + r), (yhi, FY0 + 32 + r)):
-                v = src[at, :]
-                br[every(3 * YR + row, 32, YR), :] = own_lanes(rl(v, 32))
-                br[every(35 * YR + row, 32, YR), :] = own_lanes(rl(v, -32))
-        for i in range(3):
-            n = f * 3 + i
-            shift = 32 if n % 2 == 0 else -32
-            br[plane(i), :] = own_lanes(rl(xlo[plane(n // 2), :], shift))
-            br[plane(67 + i), :] = own_lanes(rl(xhi[plane(n // 2), :], shift))
-    for group in range(5):
-        lo = jnp.zeros((YR, 128), F32)
-        hi = lo
-        for slot in range(14):
-            for f, br in enumerate(bricks):
-                v = br[plane(group * 14 + slot), :]
-                at = 9 * slot + 3 * f
-                here = (lane >= at) & (lane < at + 3)
-                lo = jnp.where(here, rl(v, at - Z0), lo)
-                hi = jnp.where(here, rl(v, at - Z0 - 61), hi)
-        zlo[plane(group), :] = lo
-        zhi[plane(group), :] = hi
+            v = br[plane(n + 3), :]
+            at = base + FIRST[f]
+            here = (lane >= at) & (lane < at + DEPTH[f])
+            lo = jnp.where(here, rl(v, at - Z0), lo)
+            hi = jnp.where(here, rl(v, at - Z0 - 64 + DEPTH[f]), hi)
+        if n % 18 == 17 or n == 63:
+            zlo[group, :] = lo
+            zhi[group, :] = hi
+
+
+def x_plane(f, r, src):
+    n = FIRST[f] + r
+    return own_lanes(rl(src[plane(n // 2), :], -32 if n % 2 else 32))
+
+
+def fine_z_kernel(zlo0, zhi0, xlo, xhi, zlo, zhi):
+    lane = lane_of(YR)
+    zlo[...] = zlo0[...]
+    zhi[...] = zhi0[...]
+    lo = zlo0[plane(3), :]
+    hi = zhi0[plane(3), :]
+    for f, r in ITEMS:
+        for src, n in ((xlo, 64 + 3 - DEPTH[f] + r), (xhi, 67 + r)):
+            v = x_plane(f, r, src)
+            at = z_slot(n)[1] + FIRST[f]
+            here = (lane >= at) & (lane < at + DEPTH[f])
+            lo = jnp.where(here, rl(v, at - Z0), lo)
+            hi = jnp.where(here, rl(v, at - Z0 - 64 + DEPTH[f]), hi)
+    zlo[plane(3), :] = lo
+    zhi[plane(3), :] = hi
 
 
 def span(x, count):
@@ -213,17 +263,26 @@
 
 
 def coefficient_kernel(
-    rh0, aa0, bb0, zlo, zhi, f, fx, fy, fz, ir, ib, dg, v, c1, slo, shi, a, b, ta, tx, ty, tz
+    rh0, aa0, bb0, xlo, xhi, zlo, zhi, f, fx, fy, fz, ir, ib, dg, v, c1, slo, shi, a, b, ta, tx, ty, tz
 ):
     lane = lane_of(YR)
     for x in range(FXN):
+        group, base = z_slot(x - 3 if 3 <= x < 67 else (64 + x if x < 3 else x))
         for n, (src, dst) in enumerate(((rh0, f), (aa0, a), (bb0, b))):
-            at = 9 * (x % 14) + 3 * n
-            w = src[plane(x), :]
-            lo = rl(zlo[plane(x // 14), :], Z0 - 3 - at)
-            hi = rl(zhi[plane(x // 14), :], Z0 + 64 - at)
-            w = jnp.where((lane >= Z0 - 3) & (lane < Z0), lo, w)
-            dst[plane(x), :] = jnp.where((lane >= Z0 + 64) & (lane < Z0 + 67), hi, w)
+            d = DEPTH[n]
+            if 3 <= x < 67:
+                w = src[plane(x), :]
+            elif 3 - d <= x < 3:
+                w = x_plane(n, x - 3 + d, xlo)
+            elif 67 <= x < 67 + d:
+                w = x_plane(n, x - 67, xhi)
+            else:
+                dst[plane(x), :] = jnp.zeros((YR, 128), F32)
+                continue
+            at = base + FIRST[n]
+            w = jnp.where((lane >= Z0 - d) & (lane < Z0), rl(zlo[group, :], Z0 - d - at), w)
+            above = (lane >= Z0 + 64) & (lane < Z0 + 64 + d)
+            dst[plane(x), :] = jnp.where(above, rl(zhi[group, :], Z0 + 64 - at), w)
 
     def faces(x, count):
         here = b[span(x, count), :]
@@ -559,8 +618,23 @@
     exchange = functools.partial(
         lax.all_to_all, axis_name=LAYER, split_axis=0, concat_axis=0, tiled=True
     )
-    (spread,) = call(spread_kernel, [(32, 104, 128)], smem=1)(
-        new_place, rhs_boxes, a_boxes, b_boxes
+    hbm = pl.BlockSpec(memory_space=pltpu.HBM)
+    spread = pl.pallas_call(
+        spread_kernel,
+        out_shape=jax.ShapeDtypeStruct((32, 104, 128), F32),
+        in_specs=[hbm] * 4,
+        out_specs=pl.BlockSpec(memory_space=pltpu.VMEM),
+        scratch_shapes=[
+            pltpu.VMEM((3, 4, 32768), F32),
+            pltpu.SMEM((1, 4), jnp.int32),
+            pltpu.SemaphoreType.DMA((13,)),
+        ],
+        compiler_params=pltpu.CompilerParams(vmem_limit_bytes=8 << 20),
+    )(
+        *(
+            pltpu.with_memory_space_constraint(w, pltpu.HBM)
+            for w in (new_place, rhs_boxes, a_boxes, b_boxes)
+        )
     )
     got = exchange(spread)
     place = got[:, 96, :4].astype(jnp.int32)
@@ -569,22 +643,24 @@
 
     fine = (FXN * YR, 128)
     coarse = (CXN * YR, 128)
-    rh, aa, bb, ylo, yhi, xlo, xhi = call(
-        brick_kernel, [fine] * 3 + [(288, 128)] * 2 + [(9 * YR, 128)] * 2
-    )(got)
+    ylo, yhi = call(strip_kernel, [(7 * 32, 128)] * 2, us=1)(got.reshape(3072, 128))
     ylo, yhi = swap(ylo, yhi, "gy")
-    xlo, xhi = call(fine_x_kernel, [(5 * YR, 128)] * 2, [(9 * YR, 128)] * 2)(xlo, xhi, ylo, yhi)
+    rh, aa, bb, xlo, xhi = call(brick_kernel, [fine] * 3 + [(7 * YR, 128)] * 2, us=4)(got)
+    xlo, xhi = call(fine_x_kernel, [(4 * YR, 128)] * 2, [(7 * YR, 128)] * 2, us=1)(
+        xlo, xhi, ylo, yhi
+    )
     xlo, xhi = swap(xlo, xhi, "gx")
-    rh, aa, bb, zlo, zhi = call(fine_z_kernel, [fine] * 3 + [(5 * YR, 128)] * 2)(
-        rh, aa, bb, ylo, yhi, xlo, xhi
+    rh, aa, bb, zlo, zhi = call(fine_y_kernel, [fine] * 3 + [(4 * YR, 128)] * 2)(
+        rh, aa, bb, ylo, yhi
     )
+    zlo, zhi = call(fine_z_kernel, [(4 * YR, 128)] * 2, us=1)(zlo, zhi, xlo, xhi)
     zlo, zhi = swap(zlo, zhi, "gz")
     f, fx, fy, fz, ir, ib, dg, v, c1, cylo, cyhi = call(
         coefficient_kernel,
         [fine] * 8 + [(640, 128)] + [(9 * 32, 128)] * 2,
         [fine, fine] + [(33 * YR, 128)] * 4,
         us=8,
-    )(rh, aa, bb, zlo, zhi)
+    )(rh, aa, bb, xlo, xhi, zlo, zhi)
     cylo, cyhi = swap(cylo, cyhi, "gy")
     v, rc, ylo, yhi = call(
         presmooth_kernel,

time: 207 us -> 197 us (0.952)
  waiting for transfers between devices: 17.7 us -> 12.2 us
  local copies, waits for them, and re-layouts: 3.77 us -> 0 us
    ppermute x18, waiting for transfers between devices: 17.7 us -> 12.2 us  [swap(): return (lax.ppermute(high, axis, up), lax.ppermute(low, axis, down))]
    unnamed x8 -> x0, local copies, waits for them, and re-layouts: 3.77 us -> none
    pallas_call x13 -> x14, Pallas kernels: 36.5 us -> 34.7 us  [run(): pl.pallas_call(kernel, out_shape=[jax.ShapeDtypeStruct(s, F32) for s in o...]
  transfers between devices with their start and end apart: 18 -> 18, of which waited for: 8 -> 5; matrix products, arithmetic and copies ran while one was open for 0% -> 0% of each run, Pallas kernels for 6% -> 9%
where the time goes in v3:
time: 197 us; the launch traced here: 196 us
  blocking collectives  93.6 us (48%)
  starting transfers between devices  53.2 us (27%)
  Pallas kernels  36.3 us (18%)
  waiting for transfers between devices  12.2 us (6%)
    ppermute x18, starting transfers between devices, swap(): return (lax.ppermute(high, axis, up), lax.ppermute(low, axis, down))  53.2 us
    all_to_all x1, blocking collectives, body(): got = exchange(spread)  50.7 us
    all_to_all x1, blocking collectives, body(): got = exchange(routed)  42.9 us
    pallas_call x14, Pallas kernels, run(): pl.pallas_call(kernel, out_shape=[jax.ShapeDtypeStruct(s, F32) for s in o...  34.7 us
    ppermute x18, waiting for transfers between devices, swap(): return (lax.ppermute(high, axis, up), lax.ppermute(low, axis, down))  12.2 us
  transfers between devices with their start and end apart: 18, of which 5 were waited for; matrix products, arithmetic and copies ran while one was open for 0% of the time, Pallas kernels for 9%

profile of v3, /device:TPU:41, one launch (start us, length us, event | category | flops | bytes accessed | tf_op | source)
XLA Modules:
  0.0 196.3 jit_solution(17224173838107287774)
XLA Ops:
  0.6 1.6 shard_map.59
  2.2 50.7 %all_to_all.10.got = f32[32,104,128]{2,1,0:T(8,128)S(1)} all-to-all(f32[32,104,128]{2,1,0:T(8,128)S(1)} %shard_map.59), channel_id=1, replica_groups=mesh['gx'=8,'gy'=4,'gz'=8] {'gx','gy'}, dimensions={0} | all-to-all | bytes 3407872 | tf_op jit(solution)/shard_map/all_to_all | solution.py:639
  52.9 1.3 shard_map.60
  54.2 42.9 %all_to_all.11.got = f32[32,12,8,128]{3,2,1,0:T(8,128)S(1)} all-to-all(f32[32,12,8,128]{3,2,1,0:T(8,128)S(1)} %shard_map.60), channel_id=1, replica_groups=mesh['gx'=8,'gy'=4,'gz'=8] {'gx','gy'}, dimensions={0} | all-to-all | bytes 3145728 | tf_op jit(solution)/shard_map/all_to_all | solution.py:642
  97.1 0.3 shard_map.62
  97.4 2.6 %collective-permute-start = (f32[224,128]{1,0:T(8,128)S(1)}, f32[224,128]{1,0:T(8,128)S(1)}, u32[]{:S(2)}, u32[]{:S(2)}) collective-permute-start(f32[224,128]{1,0:T(8,128)S(1)} %get-tuple-element.58), channel_id=1, source_target_pairs={{0,8},{8,16},{16,24},{1,9},{9,17},{17,25},{2,10},{10,18},{18,26},{... | collective-permute-start | bytes 344072 | tf_op jit(solution)/shard_map/ppermute | solution.py:614
  100.1 1.3 collective-permute-start.1
  101.4 2.6 %shard_map.61 = (f32[2800,128]{1,0:T(8,128)S(1)}, f32[2800,128]{1,0:T(8,128)S(1)}, f32[2800,128]{1,0:T(8,128)S(1)}, f32[280,128]{1,0:T(8,128)S(1)}, f32[280,128]{1,0:T(8,128)S(1)}) custom-call(f32[32,12,8,128]{3,2,1,0:T(8,128)S(1)} %all_to_all.11.got), custom_call_target="tpu_custom_call" | custom-call | bytes 12000000 | tf_op jit(solution)/shard_map/pallas_call | solution.py:50
  104.0 0.0 collective-permute-done.ylo
  104.0 1.6 collective-permute-done.1.yhi
  105.6 0.2 shard_map.64
  105.8 2.2 %collective-permute-start.2 = (f32[160,128]{1,0:T(8,128)S(1)}, f32[160,128]{1,0:T(8,128)S(1)}, u32[]{:S(2)}, u32[]{:S(2)}) collective-permute-start(f32[160,128]{1,0:T(8,128)S(1)} %get-tuple-element.65), channel_id=1, source_target_pairs={{0,32},{32,64},{64,96},{96,128},{128,160},{160,192},{192,224},{1,3... | collective-permute-start | bytes 245768 | tf_op jit(solution)/shard_map/ppermute | solution.py:614
  108.0 3.1 %collective-permute-start.3 = (f32[160,128]{1,0:T(8,128)S(1)}, f32[160,128]{1,0:T(8,128)S(1)}, u32[]{:S(2)}, u32[]{:S(2)}) collective-permute-start(f32[160,128]{1,0:T(8,128)S(1)} %get-tuple-element.66), channel_id=1, source_target_pairs={{32,0},{64,32},{96,64},{128,96},{160,128},{192,160},{224,192},{33,... | collective-permute-start | bytes 245768 | tf_op jit(solution)/shard_map/ppermute | solution.py:614
  111.1 2.4 %shard_map.63 = (f32[2800,128]{1,0:T(8,128)S(1)}, f32[2800,128]{1,0:T(8,128)S(1)}, f32[2800,128]{1,0:T(8,128)S(1)}, f32[160,128]{1,0:T(8,128)S(1)}, f32[160,128]{1,0:T(8,128)S(1)}) custom-call(f32[2800,128]{1,0:T(8,128)S(1)} %get-tuple-element.55.rh0, f32[2800,128]{1,0:T(8,128)S(1)} %get-tuple-element.56.aa0, f32[2800,128]{1,0:T(8,128)S(1)} %get-tuple-element.57.bb0, ...), custom_call_target="tpu_custom_call" | custom-call | bytes 6000000 | tf_op jit(solution)/shard_map/pallas_call | solution.py:50
  113.5 0.0 collective-permute-done.2.xlo
  113.5 0.0 collective-permute-done.3.xhi
  113.5 0.7 shard_map.65
  114.2 9.2 %collective-permute-start.4 = (f32[160,128]{1,0:T(8,128)S(1)}, f32[160,128]{1,0:T(8,128)S(1)}, u32[]{:S(2)}, u32[]{:S(2)}) collective-permute-start(f32[160,128]{1,0:T(8,128)S(1)} %get-tuple-element.69), channel_id=1, source_target_pairs={{0,1},{1,2},{2,3},{3,4},{4,5},{5,6},{6,7},{8,9},{9,10},{10,11},{11... | collective-permute-start | bytes 245768 | tf_op jit(solution)/shard_map/ppermute | solution.py:614
  123.4 1.9 collective-permute-start.5
  125.4 0.0 collective-permute-done.4.zlo
  125.4 3.8 %collective-permute-done.5.zhi = f32[160,128]{1,0:T(8,128)S(1)} collective-permute-done((f32[160,128]{1,0:T(8,128)S(1)}, f32[160,128]{1,0:T(8,128)S(1)}, u32[]{:S(2)}, u32[]{:S(2)}) %collective-permute-start.5) | collective-permute-done | bytes 81952 | tf_op jit(solution)/shard_map/ppermute | solution.py:614
  129.2 5.6 %shard_map.66 = (f32[2800,128]{1,0:T(8,128)S(1)}, f32[2800,128]{1,0:T(8,128)S(1)}, f32[2800,128]{1,0:T(8,128)S(1)}, f32[2800,128]{1,0:T(8,128)S(1)}, f32[2800,12...) custom-call(f32[2800,128]{1,0:T(8,128)S(1)} %get-tuple-element.60.rh, ...), custom_call_target="tpu_custom_call" | custom-call | bytes 24000000 | tf_op jit(solution)/shard_map/pallas_call | solution.py:50
  134.8 2.8 %collective-permute-start.6 = (f32[288,128]{1,0:T(8,128)S(1)}, f32[288,128]{1,0:T(8,128)S(1)}, u32[]{:S(2)}, u32[]{:S(2)}) collective-permute-start(f32[288,128]{1,0:T(8,128)S(1)} %get-tuple-element.71), channel_id=1, source_target_pairs={{0,8},{8,16},{16,24},{1,9},{9,17},{17,25},{2,10},{10,18},{18,26},{... | collective-permute-start | bytes 442376 | tf_op jit(solution)/shard_map/ppermute | solution.py:614
  137.6 1.5 collective-permute-start.7
  139.0 3.3 %shard_map.67 = (f32[2800,128]{1,0:T(8,128)S(1)}, f32[640,128]{1,0:T(8,128)S(1)}, f32[288,128]{1,0:T(8,128)S(1)}, f32[288,128]{1,0:T(8,128)S(1)}) custom-call(f32[2800,128]{1,0:T(8,128)S(1)} %get-tuple-element.73.f, f32[2800,128]{1,0:T(8,128)S(1)} %get-tuple-element.74.fx, f32[2800,128]{1,0:T(8,128)S(1)} %get-tuple-element.75.fy, ...), custom_call_target="tpu_custom_call" | custom-call | bytes 18000000 | tf_op jit(solution)/shard_map/pallas_call | solution.py:50
  142.4 2.1 %collective-permute-done.7.yhi = f32[288,128]{1,0:T(8,128)S(1)} collective-permute-done((f32[288,128]{1,0:T(8,128)S(1)}, f32[288,128]{1,0:T(8,128)S(1)}, u32[]{:S(2)}, u32[]{:S(2)}) %collective-permute-start.7) | collective-permute-done | bytes 147488 | tf_op jit(solution)/shard_map/ppermute | solution.py:614
  144.5 0.1 shard_map.70
  144.7 2.3 %collective-permute-start.14 = (f32[360,128]{1,0:T(8,128)S(1)}, f32[360,128]{1,0:T(8,128)S(1)}, u32[]{:S(2)}, u32[]{:S(2)}) collective-permute-start(f32[360,128]{1,0:T(8,128)S(1)} %get-tuple-element.97), channel_id=1, source_target_pairs={{0,32},{32,64},{64,96},{96,128},{128,160},{160,192},{192,224},{1,3... | collective-permute-start | bytes 552968 | tf_op jit(solution)/shard_map/ppermute | solution.py:614
  146.9 3.0 %collective-permute-start.15 = (f32[360,128]{1,0:T(8,128)S(1)}, f32[360,128]{1,0:T(8,128)S(1)}, u32[]{:S(2)}, u32[]{:S(2)}) collective-permute-start(f32[360,128]{1,0:T(8,128)S(1)} %get-tuple-element.98), channel_id=1, source_target_pairs={{32,0},{64,32},{96,64},{128,96},{160,128},{192,160},{224,192},{33,... | collective-permute-start | bytes 552968 | tf_op jit(solution)/shard_map/ppermute | solution.py:614
  150.0 3.0 %collective-permute-start.8 = (f32[288,128]{1,0:T(8,128)S(1)}, f32[288,128]{1,0:T(8,128)S(1)}, u32[]{:S(2)}, u32[]{:S(2)}) collective-permute-start(f32[288,128]{1,0:T(8,128)S(1)} %get-tuple-element.83), channel_id=1, source_target_pairs={{0,8},{8,16},{16,24},{1,9},{9,17},{17,25},{2,10},{10,18},{18,26},{... | collective-permute-start | bytes 442376 | tf_op jit(solution)/shard_map/ppermute | solution.py:614
  153.0 1.3 collective-permute-start.9
  154.3 1.0 collective-permute-done.8.ylo
  155.3 3.6 %collective-permute-done.9.yhi = f32[288,128]{1,0:T(8,128)S(1)} collective-permute-done((f32[288,128]{1,0:T(8,128)S(1)}, f32[288,128]{1,0:T(8,128)S(1)}, u32[]{:S(2)}, u32[]{:S(2)}) %collective-permute-start.9) | collective-permute-done | bytes 147488 | tf_op jit(solution)/shard_map/ppermute | solution.py:614
  158.8 0.3 shard_map.68
  159.1 2.4 %collective-permute-start.10 = (f32[360,128]{1,0:T(8,128)S(1)}, f32[360,128]{1,0:T(8,128)S(1)}, u32[]{:S(2)}, u32[]{:S(2)}) collective-permute-start(f32[360,128]{1,0:T(8,128)S(1)} %get-tuple-element.87), channel_id=1, source_target_pairs={{0,32},{32,64},{64,96},{96,128},{128,160},{160,192},{192,224},{1,3... | collective-permute-start | bytes 552968 | tf_op jit(solution)/shard_map/ppermute | solution.py:614
  161.5 2.9 %collective-permute-start.11 = (f32[360,128]{1,0:T(8,128)S(1)}, f32[360,128]{1,0:T(8,128)S(1)}, u32[]{:S(2)}, u32[]{:S(2)}) collective-permute-start(f32[360,128]{1,0:T(8,128)S(1)} %get-tuple-element.88), channel_id=1, source_target_pairs={{32,0},{64,32},{96,64},{128,96},{160,128},{192,160},{224,192},{33,... | collective-permute-start | bytes 552968 | tf_op jit(solution)/shard_map/ppermute | solution.py:614
  164.5 1.1 shard_map.71
  165.6 6.1 %collective-permute-start.16 = (f32[600,128]{1,0:T(8,128)S(1)}, f32[600,128]{1,0:T(8,128)S(1)}, u32[]{:S(2)}, u32[]{:S(2)}) collective-permute-start(f32[600,128]{1,0:T(8,128)S(1)} %get-tuple-element.100), channel_id=1, source_target_pairs={{0,1},{1,2},{2,3},{3,4},{4,5},{5,6},{6,7},{8,9},{9,10},{10,11},{11... | collective-permute-start | bytes 921608 | tf_op jit(solution)/shard_map/ppermute | solution.py:614
  171.7 1.9 collective-permute-start.17
  173.6 0.0 collective-permute-done.11.xhi
  173.7 2.7 %shard_map.69 = (f32[1000,128]{1,0:T(8,128)S(1)}, f32[2800,128]{1,0:T(8,128)S(1)}, f32[280,128]{1,0:T(8,128)S(1)}, f32[280,128]{1,0:T(8,128)S(1)}) custom-call(f32[2000,128]{1,0:T(8,128)S(1)} %get-tuple-element.85.er, f32[2800,128]{1,0:T(8,128)S(1)} %get-tuple-element.86.vs0, f32[360,128]{1,0:T(8,128)S(1)} %collective-permute-done.10.xlo, ...), custom_call_target="tpu_custom_call" | custom-call | bytes 6000000 | tf_op jit(solution)/shard_map/pallas_call | solution.py:50
  176.3 3.6 %collective-permute-start.12 = (f32[280,128]{1,0:T(8,128)S(1)}, f32[280,128]{1,0:T(8,128)S(1)}, u32[]{:S(2)}, u32[]{:S(2)}) collective-permute-start(f32[280,128]{1,0:T(8,128)S(1)} %get-tuple-element.91), channel_id=1, source_target_pairs={{0,1},{1,2},{2,3},{3,4},{4,5},{5,6},{6,7},{8,9},{9,10},{10,11},{11... | collective-permute-start | bytes 430088 | tf_op jit(solution)/shard_map/ppermute | solution.py:614
  180.0 2.1 %collective-permute-start.13 = (f32[280,128]{1,0:T(8,128)S(1)}, f32[280,128]{1,0:T(8,128)S(1)}, u32[]{:S(2)}, u32[]{:S(2)}) collective-permute-start(f32[280,128]{1,0:T(8,128)S(1)} %get-tuple-element.92), channel_id=1, source_target_pairs={{1,0},{2,1},{3,2},{4,3},{5,4},{6,5},{7,6},{9,8},{10,9},{11,10},{12... | collective-permute-start | bytes 430088 | tf_op jit(solution)/shard_map/ppermute | solution.py:614
  182.1 0.0 collective-permute-done.16.zlo
  182.2 0.0 collective-permute-done.17.zhi
  182.2 5.4 %shard_map.72 = (f32[1120,128]{1,0:T(8,128)S(1)}, f32[1120,128]{1,0:T(8,128)S(1)}, f32[1120,128]{1,0:T(8,128)S(1)}, f32[1120,128]{1,0:T(8,128)S(1)}, f32[1120,128]{1,0:T(8,128)S(1)}) custom-call(f32[2000,128]{1,0:T(8,128)S(1)} %get-tuple-element.99.ec, f32[600,128]{1,0:T(8,128)S(1)} %collective-permute-done.16.zlo, f32[600,128]{1,0:T(8,128)S(1)} %collective-permute-done.17.zhi), custom_call_target="tpu_custom_call" | custom-call | bytes 15000000 | tf_op jit(solution)/shard_map/pallas_call | solution.py:50
  187.6 0.0 collective-permute-done.13.zhi
  187.6 8.7 %shard_map.73 = (f32[64,32,64]{2,1,0:T(8,128)}, f32[64,32,64]{2,1,0:T(8,128)}) custom-call(f32[1000,128]{1,0:T(8,128)S(1)} %get-tuple-element.89.rm, f32[2800,128]{1,0:T(8,128)S(1)} %get-tuple-element.90.vs, f32[280,128]{1,0:T(8,128)S(1)} %collective-permute-done.12.zlo, f32[280,128]{1,0:T(8,128)S(1)} %collective-permute-done.13.zhi, ...), custom_call_target="tpu_custom_call" | custom-call | bytes 24000000 | tf_op jit(solution)/shard_map/pallas_call | solution.py:50
  (6 shorter events, 0.0 us)
Async XLA Ops:
  97.4 6.5 %collective-permute-start = (f32[224,128]{1,0:T(8,128)S(1)}, f32[224,128]{1,0:T(8,128)S(1)}, u32[]{:S(2)}, u32[]{:S(2)}) collective-permute-start(f32[224,128]{1,0:T(8,128)S(1)} %get-tuple-element.58), channel_id=1, source_target_pairs={{0,8},{8,16},{16,24},{1,9},{9,17},{17,25},{2,10},{10,18},{18,26},{... | collective-permute-start | bytes 344072 | tf_op jit(solution)/shard_map/ppermute | solution.py:614
  100.1 5.5 %collective-permute-start.1 = (f32[224,128]{1,0:T(8,128)S(1)}, f32[224,128]{1,0:T(8,128)S(1)}, u32[]{:S(2)}, u32[]{:S(2)}) collective-permute-start(f32[224,128]{1,0:T(8,128)S(1)} %get-tuple-element.59), channel_id=1, source_target_pairs={{8,0},{16,8},{24,16},{9,1},{17,9},{25,17},{10,2},{18,10},{26,18},{... | collective-permute-start | bytes 344072 | tf_op jit(solution)/shard_map/ppermute | solution.py:614
  105.8 7.7 %collective-permute-start.2 = (f32[160,128]{1,0:T(8,128)S(1)}, f32[160,128]{1,0:T(8,128)S(1)}, u32[]{:S(2)}, u32[]{:S(2)}) collective-permute-start(f32[160,128]{1,0:T(8,128)S(1)} %get-tuple-element.65), channel_id=1, source_target_pairs={{0,32},{32,64},{64,96},{96,128},{128,160},{160,192},{192,224},{1,3... | collective-permute-start | bytes 245768 | tf_op jit(solution)/shard_map/ppermute | solution.py:614
  108.0 5.5 %collective-permute-start.3 = (f32[160,128]{1,0:T(8,128)S(1)}, f32[160,128]{1,0:T(8,128)S(1)}, u32[]{:S(2)}, u32[]{:S(2)}) collective-permute-start(f32[160,128]{1,0:T(8,128)S(1)} %get-tuple-element.66), channel_id=1, source_target_pairs={{32,0},{64,32},{96,64},{128,96},{160,128},{192,160},{224,192},{33,... | collective-permute-start | bytes 245768 | tf_op jit(solution)/shard_map/ppermute | solution.py:614
  114.2 11.2 %collective-permute-start.4 = (f32[160,128]{1,0:T(8,128)S(1)}, f32[160,128]{1,0:T(8,128)S(1)}, u32[]{:S(2)}, u32[]{:S(2)}) collective-permute-start(f32[160,128]{1,0:T(8,128)S(1)} %get-tuple-element.69), channel_id=1, source_target_pairs={{0,1},{1,2},{2,3},{3,4},{4,5},{5,6},{6,7},{8,9},{9,10},{10,11},{11... | collective-permute-start | bytes 245768 | tf_op jit(solution)/shard_map/ppermute | solution.py:614
  123.4 5.8 %collective-permute-start.5 = (f32[160,128]{1,0:T(8,128)S(1)}, f32[160,128]{1,0:T(8,128)S(1)}, u32[]{:S(2)}, u32[]{:S(2)}) collective-permute-start(f32[160,128]{1,0:T(8,128)S(1)} %get-tuple-element.70), channel_id=1, source_target_pairs={{1,0},{2,1},{3,2},{4,3},{5,4},{6,5},{7,6},{9,8},{10,9},{11,10},{12... | collective-permute-start | bytes 245768 | tf_op jit(solution)/shard_map/ppermute | solution.py:614
  134.8 7.6 %collective-permute-start.6 = (f32[288,128]{1,0:T(8,128)S(1)}, f32[288,128]{1,0:T(8,128)S(1)}, u32[]{:S(2)}, u32[]{:S(2)}) collective-permute-start(f32[288,128]{1,0:T(8,128)S(1)} %get-tuple-element.71), channel_id=1, source_target_pairs={{0,8},{8,16},{16,24},{1,9},{9,17},{17,25},{2,10},{10,18},{18,26},{... | collective-permute-start | bytes 442376 | tf_op jit(solution)/shard_map/ppermute | solution.py:614
  137.6 7.0 %collective-permute-start.7 = (f32[288,128]{1,0:T(8,128)S(1)}, f32[288,128]{1,0:T(8,128)S(1)}, u32[]{:S(2)}, u32[]{:S(2)}) collective-permute-start(f32[288,128]{1,0:T(8,128)S(1)} %get-tuple-element.72), channel_id=1, source_target_pairs={{8,0},{16,8},{24,16},{9,1},{17,9},{25,17},{10,2},{18,10},{26,18},{... | collective-permute-start | bytes 442376 | tf_op jit(solution)/shard_map/ppermute | solution.py:614
  144.7 19.8 %collective-permute-start.14 = (f32[360,128]{1,0:T(8,128)S(1)}, f32[360,128]{1,0:T(8,128)S(1)}, u32[]{:S(2)}, u32[]{:S(2)}) collective-permute-start(f32[360,128]{1,0:T(8,128)S(1)} %get-tuple-element.97), channel_id=1, source_target_pairs={{0,32},{32,64},{64,96},{96,128},{128,160},{160,192},{192,224},{1,3... | collective-permute-start | bytes 552968 | tf_op jit(solution)/shard_map/ppermute | solution.py:614
  146.9 17.5 %collective-permute-start.15 = (f32[360,128]{1,0:T(8,128)S(1)}, f32[360,128]{1,0:T(8,128)S(1)}, u32[]{:S(2)}, u32[]{:S(2)}) collective-permute-start(f32[360,128]{1,0:T(8,128)S(1)} %get-tuple-element.98), channel_id=1, source_target_pairs={{32,0},{64,32},{96,64},{128,96},{160,128},{192,160},{224,192},{33,... | collective-permute-start | bytes 552968 | tf_op jit(solution)/shard_map/ppermute | solution.py:614
  150.0 5.3 %collective-permute-start.8 = (f32[288,128]{1,0:T(8,128)S(1)}, f32[288,128]{1,0:T(8,128)S(1)}, u32[]{:S(2)}, u32[]{:S(2)}) collective-permute-start(f32[288,128]{1,0:T(8,128)S(1)} %get-tuple-element.83), channel_id=1, source_target_pairs={{0,8},{8,16},{16,24},{1,9},{9,17},{17,25},{2,10},{10,18},{18,26},{... | collective-permute-start | bytes 442376 | tf_op jit(solution)/shard_map/ppermute | solution.py:614
  153.0 5.9 %collective-permute-start.9 = (f32[288,128]{1,0:T(8,128)S(1)}, f32[288,128]{1,0:T(8,128)S(1)}, u32[]{:S(2)}, u32[]{:S(2)}) collective-permute-start(f32[288,128]{1,0:T(8,128)S(1)} %get-tuple-element.84), channel_id=1, source_target_pairs={{8,0},{16,8},{24,16},{9,1},{17,9},{25,17},{10,2},{18,10},{26,18},{... | collective-permute-start | bytes 442376 | tf_op jit(solution)/shard_map/ppermute | solution.py:614
  159.1 14.5 %collective-permute-start.10 = (f32[360,128]{1,0:T(8,128)S(1)}, f32[360,128]{1,0:T(8,128)S(1)}, u32[]{:S(2)}, u32[]{:S(2)}) collective-permute-start(f32[360,128]{1,0:T(8,128)S(1)} %get-tuple-element.87), channel_id=1, source_target_pairs={{0,32},{32,64},{64,96},{96,128},{128,160},{160,192},{192,224},{1,3... | collective-permute-start | bytes 552968 | tf_op jit(solution)/shard_map/ppermute | solution.py:614
  161.5 12.1 %collective-permute-start.11 = (f32[360,128]{1,0:T(8,128)S(1)}, f32[360,128]{1,0:T(8,128)S(1)}, u32[]{:S(2)}, u32[]{:S(2)}) collective-permute-start(f32[360,128]{1,0:T(8,128)S(1)} %get-tuple-element.88), channel_id=1, source_target_pairs={{32,0},{64,32},{96,64},{128,96},{160,128},{192,160},{224,192},{33,... | collective-permute-start | bytes 552968 | tf_op jit(solution)/shard_map/ppermute | solution.py:614
  165.6 16.6 %collective-permute-start.16 = (f32[600,128]{1,0:T(8,128)S(1)}, f32[600,128]{1,0:T(8,128)S(1)}, u32[]{:S(2)}, u32[]{:S(2)}) collective-permute-start(f32[600,128]{1,0:T(8,128)S(1)} %get-tuple-element.100), channel_id=1, source_target_pairs={{0,1},{1,2},{2,3},{3,4},{4,5},{5,6},{6,7},{8,9},{9,10},{10,11},{11... | collective-permute-start | bytes 921608 | tf_op jit(solution)/shard_map/ppermute | solution.py:614
  171.7 10.5 %collective-permute-start.17 = (f32[600,128]{1,0:T(8,128)S(1)}, f32[600,128]{1,0:T(8,128)S(1)}, u32[]{:S(2)}, u32[]{:S(2)}) collective-permute-start(f32[600,128]{1,0:T(8,128)S(1)} %get-tuple-element.101), channel_id=1, source_target_pairs={{1,0},{2,1},{3,2},{4,3},{5,4},{6,5},{7,6},{9,8},{10,9},{11,10},{12... | collective-permute-start | bytes 921608 | tf_op jit(solution)/shard_map/ppermute | solution.py:614
  176.3 11.3 %collective-permute-start.12 = (f32[280,128]{1,0:T(8,128)S(1)}, f32[280,128]{1,0:T(8,128)S(1)}, u32[]{:S(2)}, u32[]{:S(2)}) collective-permute-start(f32[280,128]{1,0:T(8,128)S(1)} %get-tuple-element.91), channel_id=1, source_target_pairs={{0,1},{1,2},{2,3},{3,4},{4,5},{5,6},{6,7},{8,9},{9,10},{10,11},{11... | collective-permute-start | bytes 430088 | tf_op jit(solution)/shard_map/ppermute | solution.py:614
  180.0 7.6 %collective-permute-start.13 = (f32[280,128]{1,0:T(8,128)S(1)}, f32[280,128]{1,0:T(8,128)S(1)}, u32[]{:S(2)}, u32[]{:S(2)}) collective-permute-start(f32[280,128]{1,0:T(8,128)S(1)} %get-tuple-element.92), channel_id=1, source_target_pairs={{1,0},{2,1},{3,2},{4,3},{5,4},{6,5},{7,6},{9,8},{10,9},{11,10},{12... | collective-permute-start | bytes 430088 | tf_op jit(solution)/shard_map/ppermute | solution.py:614

commit v4 on v3

--- a/solution.py
+++ b/solution.py
@@ -14,7 +14,6 @@
 CXN = 50
 FY0 = 4
 CY0 = 12
-Z0 = 32
 
 
 def lane_of(rows):
@@ -42,7 +41,7 @@
 
 def own_lanes(v):
     lane = lane_of(v.shape[0])
-    return jnp.where((lane >= Z0) & (lane < Z0 + 64), v, 0.0)
+    return jnp.where(lane < 64, v, 0.0)
 
 
 def call(kernel, outs, scratch=(), limit=24, smem=0, us=2):
@@ -134,7 +133,7 @@
                     low = got[j, f * 4 + qx * 2]
                     high = got[j, f * 4 + qx * 2 + 1]
                     for c in range(4):
-                        w = jnp.where(lane8 < 64, rl(low, 32 - 32 * c), rl(high, 64 - 32 * c))
+                        w = jnp.where(lane8 < 32, rl(low, -32 * c), rl(high, 32 - 32 * c))
                         start = (j + (qx * 32 + 3)) * YR + (FY0 + c)
                         br[every(start, 8, 4), :] = own_lanes(w)
 
@@ -151,12 +150,12 @@
         for n, (f, r) in enumerate(ITEMS):
             d = DEPTH[f]
             at = pl.ds(n * 32 + (32 - d if upper else 0), d)
-            shift = -32 if upper else 32
+            shift = 64 if upper else 0
             for src, row in ((ylo, FY0 - d + r), (yhi, FY0 + 32 + r)):
                 tmp[every(FIRST[f] * YR + row, d, YR), :] = own_lanes(rl(src[at, :], shift))
         for m in range(4):
-            v = rl(tmp[plane(2 * m), :], -32)
-            w = rl(tmp[plane(2 * m + 1), :], 32) if m < 3 else jnp.zeros_like(v)
+            v = tmp[plane(2 * m), :]
+            w = rl(tmp[plane(2 * m + 1), :], 64) if m < 3 else jnp.zeros_like(v)
             out[plane(m), :] = jnp.where(lane < 64, v, w)
 
 
@@ -172,8 +171,8 @@
     for n, (f, r) in enumerate(ITEMS):
         for src, row in ((ylo, FY0 - DEPTH[f] + r), (yhi, FY0 + 32 + r)):
             v = src[plane(n, 32), :]
-            bricks[f][every(3 * YR + row, 32, YR), :] = own_lanes(rl(v, 32))
-            bricks[f][every(35 * YR + row, 32, YR), :] = own_lanes(rl(v, -32))
+            bricks[f][every(3 * YR + row, 32, YR), :] = own_lanes(v)
+            bricks[f][every(35 * YR + row, 32, YR), :] = own_lanes(rl(v, 64))
     lo = hi = None
     for n in range(64):
         group, base = z_slot(n)
@@ -184,8 +183,8 @@
             v = br[plane(n + 3), :]
             at = base + FIRST[f]
             here = (lane >= at) & (lane < at + DEPTH[f])
-            lo = jnp.where(here, rl(v, at - Z0), lo)
-            hi = jnp.where(here, rl(v, at - Z0 - 64 + DEPTH[f]), hi)
+            lo = jnp.where(here, rl(v, at), lo)
+            hi = jnp.where(here, rl(v, at - 64 + DEPTH[f]), hi)
         if n % 18 == 17 or n == 63:
             zlo[group, :] = lo
             zhi[group, :] = hi
@@ -193,7 +192,7 @@
 
 def x_plane(f, r, src):
     n = FIRST[f] + r
-    return own_lanes(rl(src[plane(n // 2), :], -32 if n % 2 else 32))
+    return own_lanes(rl(src[plane(n // 2), :], 64 * (n % 2)))
 
 
 def fine_z_kernel(zlo0, zhi0, xlo, xhi, zlo, zhi):
@@ -207,8 +206,8 @@
             v = x_plane(f, r, src)
             at = z_slot(n)[1] + FIRST[f]
             here = (lane >= at) & (lane < at + DEPTH[f])
-            lo = jnp.where(here, rl(v, at - Z0), lo)
-            hi = jnp.where(here, rl(v, at - Z0 - 64 + DEPTH[f]), hi)
+            lo = jnp.where(here, rl(v, at), lo)
+            hi = jnp.where(here, rl(v, at - 64 + DEPTH[f]), hi)
     zlo[plane(3), :] = lo
     zhi[plane(3), :] = hi
 
@@ -238,9 +237,14 @@
     return run
 
 
-def red_rows(rows, odd):
-    row = lax.broadcasted_iota(jnp.int32, (rows, 128), 0)
-    return (row + row // YR + lane_of(rows) + odd) % 2 == 0
+def even_lane(rows):
+    return (lane_of(rows) & 1) == 0
+
+
+def red_rows(planes):
+    row = lax.broadcasted_iota(jnp.int32, (YR, 128), 0)
+    first = (row + lane_of(YR)) & 1
+    return jnp.concatenate([first, 1 - first] * (planes // 2), axis=0) == 0
 
 
 FC = 4
@@ -249,7 +253,7 @@
 
 
 def zpair(s):
-    return s + jnp.where(lane_of(s.shape[0]) % 2 == 0, rl(s, -1), rl(s, 1))
+    return s + jnp.where(even_lane(s.shape[0]), rl(s, -1), rl(s, 1))
 
 
 def halves(w):
@@ -280,9 +284,9 @@
                 dst[plane(x), :] = jnp.zeros((YR, 128), F32)
                 continue
             at = base + FIRST[n]
-            w = jnp.where((lane >= Z0 - d) & (lane < Z0), rl(zlo[group, :], Z0 - d - at), w)
-            above = (lane >= Z0 + 64) & (lane < Z0 + 64 + d)
-            dst[plane(x), :] = jnp.where(above, rl(zhi[group, :], Z0 + 64 - at), w)
+            w = jnp.where(lane >= 128 - d, rl(zlo[group, :], -d - at), w)
+            above = (lane >= 64) & (lane < 64 + d)
+            dst[plane(x), :] = jnp.where(above, rl(zhi[group, :], 64 - at), w)
 
     def faces(x, count):
         here = b[span(x, count), :]
@@ -302,6 +306,8 @@
     for ref in (ir, ib, dg, v):
         ref[plane(0), :] = nothing
         ref[plane(FXN - 1), :] = nothing
+
+    red = red_rows(FS)
 
     @steps(STEPS)
     def _(k):
@@ -314,14 +320,13 @@
         diag = ax + total
         inside = ax > 0.0
         one = jnp.where(inside, 1.0 / jnp.where(inside, diag, 1.0), 0.0)
-        red = red_rows(FS * YR, 0)
         dg[at, :] = diag
         ir[at, :] = jnp.where(red, one, 0.0)
         ib[at, :] = jnp.where(red, 0.0, one)
         v[at, :] = jnp.where(red, f[at, :] * one, 0.0)
 
     edge = fx[plane(2), :]
-    edge = edge + jnp.where(lane % 2 == 0, rl(edge, -1), rl(edge, 1))
+    edge = edge + jnp.where(even_lane(YR), rl(edge, -1), rl(edge, 1))
     tx[plane(0), :] = edge
 
     @steps(64 // FC)
@@ -336,7 +341,7 @@
     @steps(8)
     def _(k):
         base = k * 4 * YR
-        even = lane_of(80) % 2 == 0
+        even = even_lane(80)
 
         def rows(ref, first, planes=0):
             return ref[every(base + planes * YR + first, 80, 2), :]
@@ -350,7 +355,7 @@
         diag = acoef + 0.25 * (fxp + fxm + fyp + ry(fyp, 1) + fzp + rl(fzp, 2))
         pa = jnp.where(even, fxp, fyp)
         pb = jnp.where(even, fzp, diag)
-        c1[pl.ds(k * 80, 80), :] = jnp.where(lane_of(80) < 64, rl(pa, -32), rl(pb, 32))
+        c1[pl.ds(k * 80, 80), :] = jnp.where(lane_of(80) < 64, pa, rl(pb, 64))
 
     for dst, y0 in ((slo, 2), (shi, 9)):
         for r in range(9):
@@ -379,7 +384,7 @@
     def _(k):
         base = k * 4 * YR
         rhs = tr[every(base, 80, 2), :] + tr[every(base + 1, 80, 2), :]
-        rc[pl.ds(k * 80, 80), :] = jnp.where(lane_of(80) < 64, rl(0.125 * rhs, -32), 0.0)
+        rc[pl.ds(k * 80, 80), :] = jnp.where(lane_of(80) < 64, 0.125 * rhs, 0.0)
 
     lane32 = lane_of(32)
     for dst, y0, fine0 in ((slo, 2, 0), (shi, 9, 29)):
@@ -387,7 +392,7 @@
             w = rc[every(y0 + r, 32, 20), :]
             if r < 6:
                 start = (3 + 32 * (r // 3)) * YR + FY0 + fine0 + r % 3
-                w = jnp.where(lane32 < 64, w, rl(v[every(start, 32, YR), :], 32))
+                w = jnp.where(lane32 < 64, w, rl(v[every(start, 32, YR), :], 64))
             dst[plane(r, 32), :] = w
 
 
@@ -416,12 +421,12 @@
             er[every(9 * YR + crow + r, 32, YR), :] = w
             if r < 6:
                 start = (3 + 32 * (r // 3)) * YR + frow + r % 3
-                vs[every(start, 32, YR), :] = own_lanes(rl(w, -32))
+                vs[every(start, 32, YR), :] = own_lanes(rl(w, 64))
     for dst, first, fine in ((slo, 9, 3), (shi, 32, 64)):
         for i in range(9):
             w = er[plane(first + i), :]
             if i < 3:
-                w = jnp.where(lane < 64, w, rl(own_lanes(vs[plane(fine + i), :]), 32))
+                w = jnp.where(lane < 64, w, rl(own_lanes(vs[plane(fine + i), :]), 64))
             dst[plane(i), :] = w
 
 
@@ -451,34 +456,52 @@
             zhi[plane(n // 7), :] = hi
 
 
-def rhs_z_kernel(er, vs0, xlo, xhi, rm, vs, zlo, zhi):
-    lane = lane_of(YR)
-    even = lane % 2 == 0
-    own = (lane >= Z0) & (lane < Z0 + 64)
-    vs[...] = vs0[...]
-    for src, fine in ((xlo, 0), (xhi, 67)):
-        for i in range(3):
-            vs[plane(fine + i), :] = own_lanes(rl(src[plane(i), :], -32))
+def smooth_slot(n):
+    return plane(n // 12), 27 * (n // 3 % 4) + 18 + 3 * (n % 3)
+
+
+def smooth_z_kernel(vs, zlo, zhi):
+    lane = lane_of(YR)
+    lo = hi = jnp.zeros((YR, 128), F32)
+    zlo[plane(6), :] = lo
+    zhi[plane(6), :] = lo
+    for n in range(3, 67):
+        group, to = smooth_slot(n)
+        if n % 12 == 0:
+            lo = hi = jnp.zeros((YR, 128), F32)
+        w = vs[plane(n), :]
+        here = (lane >= to) & (lane < to + 3)
+        lo = jnp.where(here, rl(w, to), lo)
+        hi = jnp.where(here, rl(w, to - 61), hi)
+        if n % 12 == 11 or n == 66:
+            zlo[group, :] = lo
+            zhi[group, :] = hi
+
+
+def rhs_z_kernel(er, xlo, xhi, plo, phi, rm, zlo, zhi):
+    lane = lane_of(YR)
+    even = even_lane(YR)
+    own = lane < 64
     lo = hi = None
     for n in range(25):
         at = 27 * (n % 4)
         if at == 0:
-            lo = jnp.zeros((YR, 128), F32)
-            hi = lo
+            lo = plo[plane(n // 4), :]
+            hi = phi[plane(n // 4), :]
         first = xlo[plane(n), :] if n < 9 else er[plane(n), :]
         second = xhi[plane(n - 16), :] if n >= 16 else er[plane(n + 25), :]
-        w = rl(jnp.where(even, first, second), 32)
+        w = jnp.where(even, first, second)
         rm[plane(n), :] = jnp.where(own, w, 0.0)
         here = (lane >= at) & (lane < at + 18)
-        lo = jnp.where(here, rl(w, at - Z0), lo)
-        hi = jnp.where(here, rl(w, at - Z0 - 46), hi)
-        for i in range(3):
-            if 3 * n + i < FXN:
-                w = vs[plane(3 * n + i), :]
-                to = at + 18 + 3 * i
+        lo = jnp.where(here, rl(w, at), lo)
+        hi = jnp.where(here, rl(w, at - 46), hi)
+        for m in range(3 * n, 3 * n + 3):
+            if m < 3 or 67 <= m < FXN:
+                w = rl((xlo if m < 3 else xhi)[plane(m if m < 3 else m - 67), :], 64)
+                to = smooth_slot(m)[1]
                 here = (lane >= to) & (lane < to + 3)
-                lo = jnp.where(here, rl(w, to - Z0), lo)
-                hi = jnp.where(here, rl(w, to - Z0 - 61), hi)
+                lo = jnp.where(here, rl(w, to), lo)
+                hi = jnp.where(here, rl(w, to - 61), hi)
         if at == 81 or n == 24:
             zlo[plane(n // 4), :] = lo
             zhi[plane(n // 4), :] = hi
@@ -490,21 +513,21 @@
 
 def merge_kernel(ec, zlo, zhi, cx, cy, cz, jr, jb):
     lane = lane_of(YR)
-    even = lane % 2 == 0
-    own = (lane >= Z0) & (lane < Z0 + 64)
-    below = (lane >= Z0 - 18) & (lane < Z0)
-    above = (lane >= Z0 + 64) & (lane < Z0 + 82)
+    even = even_lane(YR)
+    own = lane < 64
+    below = lane >= 110
+    above = (lane >= 64) & (lane < 82)
     nothing = jnp.zeros((YR, 128), F32)
     row = lax.broadcasted_iota(jnp.int32, (YR, 128), 0)
-    colour = (row + lane // 2 + 1) % 2
+    reds = ((row + (lane >> 1) + jnp.where(even, 0, 1)) & 1) == 0
 
     def load(which, x):
         if not 0 <= x < CXN:
             return nothing
         group, at = coef_slot(which, x)
-        w = jnp.where(own, rl(ec[plane(x), :], 32 - 64 * which), 0.0)
-        w = jnp.where(below, rl(zlo[group, :], Z0 - 18 - at), w)
-        return jnp.where(above, rl(zhi[group, :], Z0 + 64 - at), w)
+        w = jnp.where(own, rl(ec[plane(x), :], 64 * which), 0.0)
+        w = jnp.where(below, rl(zlo[group, :], -18 - at), w)
+        return jnp.where(above, rl(zhi[group, :], 64 - at), w)
 
     for p in range(27):
         first, second = load(0, p - 1), load(0, p + 24)
@@ -515,38 +538,43 @@
         diag = jnp.where(even, rl(first, -1), second)
         inside = diag > 0.0
         one = jnp.where(inside, 1.0 / jnp.where(inside, diag, 1.0), 0.0)
-        isred = jnp.where(even, colour + p - 1, colour + p + 24) % 2 == 0
-        jr[plane(p), :] = jnp.where(isred, one, 0.0)
-        jb[plane(p), :] = jnp.where(isred, 0.0, one)
+        mine, other = (jr, jb) if p % 2 == 0 else (jb, jr)
+        mine[plane(p), :] = jnp.where(reds, one, 0.0)
+        other[plane(p), :] = jnp.where(reds, 0.0, one)
     for ref in (cx, cy, cz, jr, jb):
         ref[plane(27), :] = nothing
 
 
 def finish_kernel(
-    rm, vs, zlo, zhi, cx, cy, cz, jr, jb, f, fx, fy, fz, ir, ib, dg, out, res, cf, red, blk, v, w0, tmp
+    rm, vs, xlo, xhi, zlo, zhi, cx, cy, cz, jr, jb, f, fx, fy, fz, ir, ib, dg, out, res, cf, red, blk, v, w0, tmp
 ):
     lane = lane_of(YR)
-    even = lane % 2 == 0
-    below = (lane >= Z0 - 18) & (lane < Z0)
-    above = (lane >= Z0 + 64) & (lane < Z0 + 82)
+    even = even_lane(YR)
+    below = lane >= 110
+    above = (lane >= 64) & (lane < 82)
     nothing = jnp.zeros((YR, 128), F32)
     for ref in (cf, red, blk):
         for p in (0, 26, 27):
             ref[plane(p), :] = nothing
     for n in range(25):
         at = 27 * (n % 4)
-        w = jnp.where(below, rl(zlo[plane(n // 4), :], Z0 - 18 - at), rm[plane(n), :])
-        w = jnp.where(above, rl(zhi[plane(n // 4), :], Z0 + 64 - at), w)
+        w = jnp.where(below, rl(zlo[plane(n // 4), :], -18 - at), rm[plane(n), :])
+        w = jnp.where(above, rl(zhi[plane(n // 4), :], 64 - at), w)
         cf[plane(n + 1), :] = w
         red[plane(n + 1), :] = w * jr[plane(n + 1), :]
     for n in range(FXN):
-        at = 27 * (n // 3 % 4) + 18 + 3 * (n % 3)
-        group = plane(n // 12)
-        w = own_lanes(vs[plane(n), :])
-        low = rl(zlo[group, :], Z0 - 3 - at)
-        high = rl(zhi[group, :], Z0 + 64 - at)
-        w = jnp.where((lane >= Z0 - 3) & (lane < Z0), low, w)
-        v[plane(n), :] = jnp.where((lane >= Z0 + 64) & (lane < Z0 + 67), high, w)
+        group, at = smooth_slot(n)
+        if n < 3:
+            w = rl(xlo[plane(n), :], 64)
+        elif n >= 67:
+            w = rl(xhi[plane(n - 67), :], 64)
+        else:
+            w = vs[plane(n), :]
+        w = own_lanes(w)
+        low = rl(zlo[group, :], -3 - at)
+        high = rl(zhi[group, :], 64 - at)
+        w = jnp.where(lane >= 125, low, w)
+        v[plane(n), :] = jnp.where((lane >= 64) & (lane < 67), high, w)
 
     def seam(ref):
         ref[plane(26), :] = jnp.where(even, rl(ref[plane(1), :], -1), 0.0)
@@ -595,7 +623,7 @@
         v[at, :] = new + w0[at, :]
 
     def crop(w):
-        return rl(w, -32).reshape(FC, YR, 128)[:, FY0 : FY0 + 32, :64]
+        return w.reshape(FC, YR, 128)[:, FY0 : FY0 + 32, :64]
 
     @steps(64 // FC)
     def _(k):
@@ -678,9 +706,11 @@
     xlo, xhi = swap(xlo, xhi, "gx")
     ec, czlo, czhi = call(coef_z_kernel, [coarse] + [(15 * YR, 128)] * 2)(ec, cxlo, cxhi)
     czlo, czhi = swap(czlo, czhi, "gz")
-    rm, vs, zlo, zhi = call(
-        rhs_z_kernel, [(25 * YR, 128), fine] + [(7 * YR, 128)] * 2
-    )(er, vs, xlo, xhi)
+    plo, phi = call(smooth_z_kernel, [(7 * YR, 128)] * 2)(vs)
+    rm, zlo, zhi = call(rhs_z_kernel, [(25 * YR, 128)] + [(7 * YR, 128)] * 2, us=1)(
+        er, xlo, xhi, plo, phi
+    )
+    rxlo, rxhi = xlo, xhi
     zlo, zhi = swap(zlo, zhi, "gz")
     merged = (MXN * YR, 128)
     coefs = call(merge_kernel, [merged] * 5, us=5)(ec, czlo, czhi)
@@ -690,7 +720,7 @@
             [(64, 32, 64)] * 2,
             [merged] * 3 + [fine, fine, (8 * YR, 128)],
             us=8,
-        )(rm, vs, zlo, zhi, *coefs, f, fx, fy, fz, ir, ib, dg)
+        )(rm, vs, rxlo, rxhi, zlo, zhi, *coefs, f, fx, fy, fz, ir, ib, dg)
     )
 
 

time: 197 us -> 194 us (0.985)
  Pallas kernels: 36.3 us -> 33.4 us
    pallas_call x14 -> x15, Pallas kernels: 34.7 us -> 31.8 us  [run(): pl.pallas_call(kernel, out_shape=[jax.ShapeDtypeStruct(s, F32) for s in o...]
  transfers between devices with their start and end apart: 18 -> 18, of which waited for: 5 -> 5; matrix products, arithmetic and copies ran while one was open for 0% -> 0% of each run, Pallas kernels for 9% -> 8%
where the time goes in v4:
time: 194 us; the launch traced here: 193 us
  blocking collectives  93.6 us (48%)
  starting transfers between devices  53.3 us (27%)
  Pallas kernels  33.4 us (17%)
  waiting for transfers between devices  12.1 us (6%)
    ppermute x18, starting transfers between devices, swap(): return (lax.ppermute(high, axis, up), lax.ppermute(low, axis, down))  53.3 us
    all_to_all x1, blocking collectives, body(): got = exchange(spread)  50.7 us
    all_to_all x1, blocking collectives, body(): got = exchange(routed)  42.9 us
    pallas_call x15, Pallas kernels, run(): pl.pallas_call(kernel, out_shape=[jax.ShapeDtypeStruct(s, F32) for s in o...  31.8 us
    ppermute x18, waiting for transfers between devices, swap(): return (lax.ppermute(high, axis, up), lax.ppermute(low, axis, down))  12.1 us
  transfers between devices with their start and end apart: 18, of which 5 were waited for; matrix products, arithmetic and copies ran while one was open for 0% of the time, Pallas kernels for 8%

profile of v4, /device:TPU:41, one launch (start us, length us, event | category | flops | bytes accessed | tf_op | source)
XLA Modules:
  0.0 193.4 jit_solution(12124829040917821202)
XLA Ops:
  0.6 1.6 shard_map.59
  2.2 50.7 %all_to_all.10.got = f32[32,104,128]{2,1,0:T(8,128)S(1)} all-to-all(f32[32,104,128]{2,1,0:T(8,128)S(1)} %shard_map.59), channel_id=1, replica_groups=mesh['gx'=8,'gy'=4,'gz'=8] {'gx','gy'}, dimensions={0} | all-to-all | bytes 3407872 | tf_op jit(solution)/shard_map/all_to_all | solution.py:667
  52.9 1.3 shard_map.60
  54.2 42.9 %all_to_all.11.got = f32[32,12,8,128]{3,2,1,0:T(8,128)S(1)} all-to-all(f32[32,12,8,128]{3,2,1,0:T(8,128)S(1)} %shard_map.60), channel_id=1, replica_groups=mesh['gx'=8,'gy'=4,'gz'=8] {'gx','gy'}, dimensions={0} | all-to-all | bytes 3145728 | tf_op jit(solution)/shard_map/all_to_all | solution.py:670
  97.1 0.3 shard_map.62
  97.4 2.6 %collective-permute-start = (f32[224,128]{1,0:T(8,128)S(1)}, f32[224,128]{1,0:T(8,128)S(1)}, u32[]{:S(2)}, u32[]{:S(2)}) collective-permute-start(f32[224,128]{1,0:T(8,128)S(1)} %get-tuple-element.59), channel_id=1, source_target_pairs={{0,8},{8,16},{16,24},{1,9},{9,17},{17,25},{2,10},{10,18},{18,26},{... | collective-permute-start | bytes 344072 | tf_op jit(solution)/shard_map/ppermute | solution.py:642
  100.1 1.3 collective-permute-start.1
  101.4 2.6 %shard_map.61 = (f32[2800,128]{1,0:T(8,128)S(1)}, f32[2800,128]{1,0:T(8,128)S(1)}, f32[2800,128]{1,0:T(8,128)S(1)}, f32[280,128]{1,0:T(8,128)S(1)}, f32[280,128]{1,0:T(8,128)S(1)}) custom-call(f32[32,12,8,128]{3,2,1,0:T(8,128)S(1)} %all_to_all.11.got), custom_call_target="tpu_custom_call" | custom-call | bytes 12000000 | tf_op jit(solution)/shard_map/pallas_call | solution.py:49
  103.9 0.0 collective-permute-done.ylo
  104.0 1.6 collective-permute-done.1.yhi
  105.6 0.2 shard_map.64
  105.7 2.2 %collective-permute-start.2 = (f32[160,128]{1,0:T(8,128)S(1)}, f32[160,128]{1,0:T(8,128)S(1)}, u32[]{:S(2)}, u32[]{:S(2)}) collective-permute-start(f32[160,128]{1,0:T(8,128)S(1)} %get-tuple-element.66), channel_id=1, source_target_pairs={{0,32},{32,64},{64,96},{96,128},{128,160},{160,192},{192,224},{1,3... | collective-permute-start | bytes 245768 | tf_op jit(solution)/shard_map/ppermute | solution.py:642
  108.0 3.1 %collective-permute-start.3 = (f32[160,128]{1,0:T(8,128)S(1)}, f32[160,128]{1,0:T(8,128)S(1)}, u32[]{:S(2)}, u32[]{:S(2)}) collective-permute-start(f32[160,128]{1,0:T(8,128)S(1)} %get-tuple-element.67), channel_id=1, source_target_pairs={{32,0},{64,32},{96,64},{128,96},{160,128},{192,160},{224,192},{33,... | collective-permute-start | bytes 245768 | tf_op jit(solution)/shard_map/ppermute | solution.py:642
  111.0 2.3 %shard_map.63 = (f32[2800,128]{1,0:T(8,128)S(1)}, f32[2800,128]{1,0:T(8,128)S(1)}, f32[2800,128]{1,0:T(8,128)S(1)}, f32[160,128]{1,0:T(8,128)S(1)}, f32[160,128]{1,0:T(8,128)S(1)}) custom-call(f32[2800,128]{1,0:T(8,128)S(1)} %get-tuple-element.56.rh0, f32[2800,128]{1,0:T(8,128)S(1)} %get-tuple-element.57.aa0, f32[2800,128]{1,0:T(8,128)S(1)} %get-tuple-element.58.bb0, ...), custom_call_target="tpu_custom_call" | custom-call | bytes 6000000 | tf_op jit(solution)/shard_map/pallas_call | solution.py:49
  113.4 0.4 shard_map.65
  113.9 9.3 %collective-permute-start.4 = (f32[160,128]{1,0:T(8,128)S(1)}, f32[160,128]{1,0:T(8,128)S(1)}, u32[]{:S(2)}, u32[]{:S(2)}) collective-permute-start(f32[160,128]{1,0:T(8,128)S(1)} %get-tuple-element.70), channel_id=1, source_target_pairs={{0,1},{1,2},{2,3},{3,4},{4,5},{5,6},{6,7},{8,9},{9,10},{10,11},{11... | collective-permute-start | bytes 245768 | tf_op jit(solution)/shard_map/ppermute | solution.py:642
  123.2 1.9 collective-permute-start.5
  125.1 0.0 collective-permute-done.4.zlo
  125.1 3.8 %collective-permute-done.5.zhi = f32[160,128]{1,0:T(8,128)S(1)} collective-permute-done((f32[160,128]{1,0:T(8,128)S(1)}, f32[160,128]{1,0:T(8,128)S(1)}, u32[]{:S(2)}, u32[]{:S(2)}) %collective-permute-start.5) | collective-permute-done | bytes 81952 | tf_op jit(solution)/shard_map/ppermute | solution.py:642
  128.9 5.5 %shard_map.66 = (f32[2800,128]{1,0:T(8,128)S(1)}, f32[2800,128]{1,0:T(8,128)S(1)}, f32[2800,128]{1,0:T(8,128)S(1)}, f32[2800,128]{1,0:T(8,128)S(1)}, f32[2800,12...) custom-call(f32[2800,128]{1,0:T(8,128)S(1)} %get-tuple-element.61.rh, ...), custom_call_target="tpu_custom_call" | custom-call | bytes 24000000 | tf_op jit(solution)/shard_map/pallas_call | solution.py:49
  134.5 2.8 %collective-permute-start.6 = (f32[288,128]{1,0:T(8,128)S(1)}, f32[288,128]{1,0:T(8,128)S(1)}, u32[]{:S(2)}, u32[]{:S(2)}) collective-permute-start(f32[288,128]{1,0:T(8,128)S(1)} %get-tuple-element.72), channel_id=1, source_target_pairs={{0,8},{8,16},{16,24},{1,9},{9,17},{17,25},{2,10},{10,18},{18,26},{... | collective-permute-start | bytes 442376 | tf_op jit(solution)/shard_map/ppermute | solution.py:642
  137.3 1.5 collective-permute-start.7
  138.7 3.4 %shard_map.67 = (f32[2800,128]{1,0:T(8,128)S(1)}, f32[640,128]{1,0:T(8,128)S(1)}, f32[288,128]{1,0:T(8,128)S(1)}, f32[288,128]{1,0:T(8,128)S(1)}) custom-call(f32[2800,128]{1,0:T(8,128)S(1)} %get-tuple-element.74.f, f32[2800,128]{1,0:T(8,128)S(1)} %get-tuple-element.75.fx, f32[2800,128]{1,0:T(8,128)S(1)} %get-tuple-element.76.fy, ...), custom_call_target="tpu_custom_call" | custom-call | bytes 18000000 | tf_op jit(solution)/shard_map/pallas_call | solution.py:49
  142.1 0.0 collective-permute-done.6.ylo
  142.2 2.1 %collective-permute-done.7.yhi = f32[288,128]{1,0:T(8,128)S(1)} collective-permute-done((f32[288,128]{1,0:T(8,128)S(1)}, f32[288,128]{1,0:T(8,128)S(1)}, u32[]{:S(2)}, u32[]{:S(2)}) %collective-permute-start.7) | collective-permute-done | bytes 147488 | tf_op jit(solution)/shard_map/ppermute | solution.py:642
  144.2 0.1 shard_map.71
  144.4 2.3 %collective-permute-start.14 = (f32[360,128]{1,0:T(8,128)S(1)}, f32[360,128]{1,0:T(8,128)S(1)}, u32[]{:S(2)}, u32[]{:S(2)}) collective-permute-start(f32[360,128]{1,0:T(8,128)S(1)} %get-tuple-element.99), channel_id=1, source_target_pairs={{0,32},{32,64},{64,96},{96,128},{128,160},{160,192},{192,224},{1,3... | collective-permute-start | bytes 552968 | tf_op jit(solution)/shard_map/ppermute | solution.py:642
  146.7 3.0 %collective-permute-start.15 = (f32[360,128]{1,0:T(8,128)S(1)}, f32[360,128]{1,0:T(8,128)S(1)}, u32[]{:S(2)}, u32[]{:S(2)}) collective-permute-start(f32[360,128]{1,0:T(8,128)S(1)} %get-tuple-element.100), channel_id=1, source_target_pairs={{32,0},{64,32},{96,64},{128,96},{160,128},{192,160},{224,192},{33,... | collective-permute-start | bytes 552968 | tf_op jit(solution)/shard_map/ppermute | solution.py:642
  149.7 3.0 %collective-permute-start.8 = (f32[288,128]{1,0:T(8,128)S(1)}, f32[288,128]{1,0:T(8,128)S(1)}, u32[]{:S(2)}, u32[]{:S(2)}) collective-permute-start(f32[288,128]{1,0:T(8,128)S(1)} %get-tuple-element.84), channel_id=1, source_target_pairs={{0,8},{8,16},{16,24},{1,9},{9,17},{17,25},{2,10},{10,18},{18,26},{... | collective-permute-start | bytes 442376 | tf_op jit(solution)/shard_map/ppermute | solution.py:642
  152.7 1.3 collective-permute-start.9
  154.0 1.0 collective-permute-done.8.ylo
  155.0 3.6 %collective-permute-done.9.yhi = f32[288,128]{1,0:T(8,128)S(1)} collective-permute-done((f32[288,128]{1,0:T(8,128)S(1)}, f32[288,128]{1,0:T(8,128)S(1)}, u32[]{:S(2)}, u32[]{:S(2)}) %collective-permute-start.9) | collective-permute-done | bytes 147488 | tf_op jit(solution)/shard_map/ppermute | solution.py:642
  158.6 0.3 shard_map.68
  158.9 2.4 %collective-permute-start.10 = (f32[360,128]{1,0:T(8,128)S(1)}, f32[360,128]{1,0:T(8,128)S(1)}, u32[]{:S(2)}, u32[]{:S(2)}) collective-permute-start(f32[360,128]{1,0:T(8,128)S(1)} %get-tuple-element.87), channel_id=1, source_target_pairs={{0,32},{32,64},{64,96},{96,128},{128,160},{160,192},{192,224},{1,3... | collective-permute-start | bytes 552968 | tf_op jit(solution)/shard_map/ppermute | solution.py:642
  161.3 2.9 %collective-permute-start.11 = (f32[360,128]{1,0:T(8,128)S(1)}, f32[360,128]{1,0:T(8,128)S(1)}, u32[]{:S(2)}, u32[]{:S(2)}) collective-permute-start(f32[360,128]{1,0:T(8,128)S(1)} %get-tuple-element.88), channel_id=1, source_target_pairs={{32,0},{64,32},{96,64},{128,96},{160,128},{192,160},{224,192},{33,... | collective-permute-start | bytes 552968 | tf_op jit(solution)/shard_map/ppermute | solution.py:642
  164.2 0.0 collective-permute-done.14.xlo
  164.2 1.1 shard_map.72
  165.3 6.1 %collective-permute-start.16 = (f32[600,128]{1,0:T(8,128)S(1)}, f32[600,128]{1,0:T(8,128)S(1)}, u32[]{:S(2)}, u32[]{:S(2)}) collective-permute-start(f32[600,128]{1,0:T(8,128)S(1)} %get-tuple-element.102), channel_id=1, source_target_pairs={{0,1},{1,2},{2,3},{3,4},{4,5},{5,6},{6,7},{8,9},{9,10},{10,11},{11... | collective-permute-start | bytes 921608 | tf_op jit(solution)/shard_map/ppermute | solution.py:642
  171.4 1.9 collective-permute-start.17
  173.3 0.7 shard_map.69
  174.1 0.0 collective-permute-done.10.xlo
  174.1 0.5 shard_map.70
  174.6 3.6 %collective-permute-start.12 = (f32[280,128]{1,0:T(8,128)S(1)}, f32[280,128]{1,0:T(8,128)S(1)}, u32[]{:S(2)}, u32[]{:S(2)}) collective-permute-start(f32[280,128]{1,0:T(8,128)S(1)} %get-tuple-element.93), channel_id=1, source_target_pairs={{0,1},{1,2},{2,3},{3,4},{4,5},{5,6},{6,7},{8,9},{9,10},{10,11},{11... | collective-permute-start | bytes 430088 | tf_op jit(solution)/shard_map/ppermute | solution.py:642
  178.2 2.1 %collective-permute-start.13 = (f32[280,128]{1,0:T(8,128)S(1)}, f32[280,128]{1,0:T(8,128)S(1)}, u32[]{:S(2)}, u32[]{:S(2)}) collective-permute-start(f32[280,128]{1,0:T(8,128)S(1)} %get-tuple-element.94), channel_id=1, source_target_pairs={{1,0},{2,1},{3,2},{4,3},{5,4},{6,5},{7,6},{9,8},{10,9},{11,10},{12... | collective-permute-start | bytes 430088 | tf_op jit(solution)/shard_map/ppermute | solution.py:642
  180.4 0.0 collective-permute-done.16.zlo
  180.4 5.1 %shard_map.73 = (f32[1120,128]{1,0:T(8,128)S(1)}, f32[1120,128]{1,0:T(8,128)S(1)}, f32[1120,128]{1,0:T(8,128)S(1)}, f32[1120,128]{1,0:T(8,128)S(1)}, f32[1120,128]{1,0:T(8,128)S(1)}) custom-call(f32[2000,128]{1,0:T(8,128)S(1)} %get-tuple-element.101.ec, f32[600,128]{1,0:T(8,128)S(1)} %collective-permute-done.16.zlo, f32[600,128]{1,0:T(8,128)S(1)} %collective-permute-done.17.zhi), custom_call_target="tpu_custom_call" | custom-call | bytes 15000000 | tf_op jit(solution)/shard_map/pallas_call | solution.py:49
  185.5 0.0 collective-permute-done.12.zlo
  185.5 7.9 %shard_map.74 = (f32[64,32,64]{2,1,0:T(8,128)}, f32[64,32,64]{2,1,0:T(8,128)}) custom-call(f32[1000,128]{1,0:T(8,128)S(1)} %get-tuple-element.92.rm, f32[2800,128]{1,0:T(8,128)S(1)} %get-tuple-element.89.vs, f32[360,128]{1,0:T(8,128)S(1)} %collective-permute-done.10.xlo, f32[360,128]{1,0:T(8,128)S(1)} %collective-permute-done.11.xhi, ...), custom_call_target="tpu_custom_call" | custom-call | bytes 24000000 | tf_op jit(solution)/shard_map/pallas_call | solution.py:49
  (7 shorter events, 0.0 us)
Async XLA Ops:
  97.4 6.5 %collective-permute-start = (f32[224,128]{1,0:T(8,128)S(1)}, f32[224,128]{1,0:T(8,128)S(1)}, u32[]{:S(2)}, u32[]{:S(2)}) collective-permute-start(f32[224,128]{1,0:T(8,128)S(1)} %get-tuple-element.59), channel_id=1, source_target_pairs={{0,8},{8,16},{16,24},{1,9},{9,17},{17,25},{2,10},{10,18},{18,26},{... | collective-permute-start | bytes 344072 | tf_op jit(solution)/shard_map/ppermute | solution.py:642
  100.1 5.5 %collective-permute-start.1 = (f32[224,128]{1,0:T(8,128)S(1)}, f32[224,128]{1,0:T(8,128)S(1)}, u32[]{:S(2)}, u32[]{:S(2)}) collective-permute-start(f32[224,128]{1,0:T(8,128)S(1)} %get-tuple-element.60), channel_id=1, source_target_pairs={{8,0},{16,8},{24,16},{9,1},{17,9},{25,17},{10,2},{18,10},{26,18},{... | collective-permute-start | bytes 344072 | tf_op jit(solution)/shard_map/ppermute | solution.py:642
  105.7 7.6 %collective-permute-start.2 = (f32[160,128]{1,0:T(8,128)S(1)}, f32[160,128]{1,0:T(8,128)S(1)}, u32[]{:S(2)}, u32[]{:S(2)}) collective-permute-start(f32[160,128]{1,0:T(8,128)S(1)} %get-tuple-element.66), channel_id=1, source_target_pairs={{0,32},{32,64},{64,96},{96,128},{128,160},{160,192},{192,224},{1,3... | collective-permute-start | bytes 245768 | tf_op jit(solution)/shard_map/ppermute | solution.py:642
  108.0 5.4 %collective-permute-start.3 = (f32[160,128]{1,0:T(8,128)S(1)}, f32[160,128]{1,0:T(8,128)S(1)}, u32[]{:S(2)}, u32[]{:S(2)}) collective-permute-start(f32[160,128]{1,0:T(8,128)S(1)} %get-tuple-element.67), channel_id=1, source_target_pairs={{32,0},{64,32},{96,64},{128,96},{160,128},{192,160},{224,192},{33,... | collective-permute-start | bytes 245768 | tf_op jit(solution)/shard_map/ppermute | solution.py:642
  113.9 11.2 %collective-permute-start.4 = (f32[160,128]{1,0:T(8,128)S(1)}, f32[160,128]{1,0:T(8,128)S(1)}, u32[]{:S(2)}, u32[]{:S(2)}) collective-permute-start(f32[160,128]{1,0:T(8,128)S(1)} %get-tuple-element.70), channel_id=1, source_target_pairs={{0,1},{1,2},{2,3},{3,4},{4,5},{5,6},{6,7},{8,9},{9,10},{10,11},{11... | collective-permute-start | bytes 245768 | tf_op jit(solution)/shard_map/ppermute | solution.py:642
  123.2 5.8 %collective-permute-start.5 = (f32[160,128]{1,0:T(8,128)S(1)}, f32[160,128]{1,0:T(8,128)S(1)}, u32[]{:S(2)}, u32[]{:S(2)}) collective-permute-start(f32[160,128]{1,0:T(8,128)S(1)} %get-tuple-element.71), channel_id=1, source_target_pairs={{1,0},{2,1},{3,2},{4,3},{5,4},{6,5},{7,6},{9,8},{10,9},{11,10},{12... | collective-permute-start | bytes 245768 | tf_op jit(solution)/shard_map/ppermute | solution.py:642
  134.5 7.7 %collective-permute-start.6 = (f32[288,128]{1,0:T(8,128)S(1)}, f32[288,128]{1,0:T(8,128)S(1)}, u32[]{:S(2)}, u32[]{:S(2)}) collective-permute-start(f32[288,128]{1,0:T(8,128)S(1)} %get-tuple-element.72), channel_id=1, source_target_pairs={{0,8},{8,16},{16,24},{1,9},{9,17},{17,25},{2,10},{10,18},{18,26},{... | collective-permute-start | bytes 442376 | tf_op jit(solution)/shard_map/ppermute | solution.py:642
  137.3 7.0 %collective-permute-start.7 = (f32[288,128]{1,0:T(8,128)S(1)}, f32[288,128]{1,0:T(8,128)S(1)}, u32[]{:S(2)}, u32[]{:S(2)}) collective-permute-start(f32[288,128]{1,0:T(8,128)S(1)} %get-tuple-element.73), channel_id=1, source_target_pairs={{8,0},{16,8},{24,16},{9,1},{17,9},{25,17},{10,2},{18,10},{26,18},{... | collective-permute-start | bytes 442376 | tf_op jit(solution)/shard_map/ppermute | solution.py:642
  144.4 19.8 %collective-permute-start.14 = (f32[360,128]{1,0:T(8,128)S(1)}, f32[360,128]{1,0:T(8,128)S(1)}, u32[]{:S(2)}, u32[]{:S(2)}) collective-permute-start(f32[360,128]{1,0:T(8,128)S(1)} %get-tuple-element.99), channel_id=1, source_target_pairs={{0,32},{32,64},{64,96},{96,128},{128,160},{160,192},{192,224},{1,3... | collective-permute-start | bytes 552968 | tf_op jit(solution)/shard_map/ppermute | solution.py:642
  146.7 17.5 %collective-permute-start.15 = (f32[360,128]{1,0:T(8,128)S(1)}, f32[360,128]{1,0:T(8,128)S(1)}, u32[]{:S(2)}, u32[]{:S(2)}) collective-permute-start(f32[360,128]{1,0:T(8,128)S(1)} %get-tuple-element.100), channel_id=1, source_target_pairs={{32,0},{64,32},{96,64},{128,96},{160,128},{192,160},{224,192},{33,... | collective-permute-start | bytes 552968 | tf_op jit(solution)/shard_map/ppermute | solution.py:642
  149.7 5.3 %collective-permute-start.8 = (f32[288,128]{1,0:T(8,128)S(1)}, f32[288,128]{1,0:T(8,128)S(1)}, u32[]{:S(2)}, u32[]{:S(2)}) collective-permute-start(f32[288,128]{1,0:T(8,128)S(1)} %get-tuple-element.84), channel_id=1, source_target_pairs={{0,8},{8,16},{16,24},{1,9},{9,17},{17,25},{2,10},{10,18},{18,26},{... | collective-permute-start | bytes 442376 | tf_op jit(solution)/shard_map/ppermute | solution.py:642
  152.7 5.9 %collective-permute-start.9 = (f32[288,128]{1,0:T(8,128)S(1)}, f32[288,128]{1,0:T(8,128)S(1)}, u32[]{:S(2)}, u32[]{:S(2)}) collective-permute-start(f32[288,128]{1,0:T(8,128)S(1)} %get-tuple-element.85), channel_id=1, source_target_pairs={{8,0},{16,8},{24,16},{9,1},{17,9},{25,17},{10,2},{18,10},{26,18},{... | collective-permute-start | bytes 442376 | tf_op jit(solution)/shard_map/ppermute | solution.py:642
  158.9 15.2 %collective-permute-start.10 = (f32[360,128]{1,0:T(8,128)S(1)}, f32[360,128]{1,0:T(8,128)S(1)}, u32[]{:S(2)}, u32[]{:S(2)}) collective-permute-start(f32[360,128]{1,0:T(8,128)S(1)} %get-tuple-element.87), channel_id=1, source_target_pairs={{0,32},{32,64},{64,96},{96,128},{128,160},{160,192},{192,224},{1,3... | collective-permute-start | bytes 552968 | tf_op jit(solution)/shard_map/ppermute | solution.py:642
  161.3 12.9 %collective-permute-start.11 = (f32[360,128]{1,0:T(8,128)S(1)}, f32[360,128]{1,0:T(8,128)S(1)}, u32[]{:S(2)}, u32[]{:S(2)}) collective-permute-start(f32[360,128]{1,0:T(8,128)S(1)} %get-tuple-element.88), channel_id=1, source_target_pairs={{32,0},{64,32},{96,64},{128,96},{160,128},{192,160},{224,192},{33,... | collective-permute-start | bytes 552968 | tf_op jit(solution)/shard_map/ppermute | solution.py:642
  165.3 15.1 %collective-permute-start.16 = (f32[600,128]{1,0:T(8,128)S(1)}, f32[600,128]{1,0:T(8,128)S(1)}, u32[]{:S(2)}, u32[]{:S(2)}) collective-permute-start(f32[600,128]{1,0:T(8,128)S(1)} %get-tuple-element.102), channel_id=1, source_target_pairs={{0,1},{1,2},{2,3},{3,4},{4,5},{5,6},{6,7},{8,9},{9,10},{10,11},{11... | collective-permute-start | bytes 921608 | tf_op jit(solution)/shard_map/ppermute | solution.py:642
  171.4 9.0 %collective-permute-start.17 = (f32[600,128]{1,0:T(8,128)S(1)}, f32[600,128]{1,0:T(8,128)S(1)}, u32[]{:S(2)}, u32[]{:S(2)}) collective-permute-start(f32[600,128]{1,0:T(8,128)S(1)} %get-tuple-element.103), channel_id=1, source_target_pairs={{1,0},{2,1},{3,2},{4,3},{5,4},{6,5},{7,6},{9,8},{10,9},{11,10},{12... | collective-permute-start | bytes 921608 | tf_op jit(solution)/shard_map/ppermute | solution.py:642
  174.6 10.9 %collective-permute-start.12 = (f32[280,128]{1,0:T(8,128)S(1)}, f32[280,128]{1,0:T(8,128)S(1)}, u32[]{:S(2)}, u32[]{:S(2)}) collective-permute-start(f32[280,128]{1,0:T(8,128)S(1)} %get-tuple-element.93), channel_id=1, source_target_pairs={{0,1},{1,2},{2,3},{3,4},{4,5},{5,6},{6,7},{8,9},{9,10},{10,11},{11... | collective-permute-start | bytes 430088 | tf_op jit(solution)/shard_map/ppermute | solution.py:642
  178.2 7.3 %collective-permute-start.13 = (f32[280,128]{1,0:T(8,128)S(1)}, f32[280,128]{1,0:T(8,128)S(1)}, u32[]{:S(2)}, u32[]{:S(2)}) collective-permute-start(f32[280,128]{1,0:T(8,128)S(1)} %get-tuple-element.94), channel_id=1, source_target_pairs={{1,0},{2,1},{3,2},{4,3},{5,4},{6,5},{7,6},{9,8},{10,9},{11,10},{12... | collective-permute-start | bytes 430088 | tf_op jit(solution)/shard_map/ppermute | solution.py:642

commit v5 on v4

--- a/solution.py
+++ b/solution.py
@@ -44,13 +44,12 @@
     return jnp.where(lane < 64, v, 0.0)
 
 
-def call(kernel, outs, scratch=(), limit=24, smem=0, us=2):
+def call(kernel, outs, scratch=(), limit=24, us=2):
     def run(*args):
         return pl.pallas_call(
             kernel,
             out_shape=[jax.ShapeDtypeStruct(s, F32) for s in outs],
-            in_specs=[pl.BlockSpec(memory_space=pltpu.SMEM)] * smem
-            + [pl.BlockSpec(memory_space=pltpu.VMEM)] * (len(args) - smem),
+            in_specs=[pl.BlockSpec(memory_space=pltpu.VMEM)] * len(args),
             out_specs=[pl.BlockSpec(memory_space=pltpu.VMEM)] * len(outs),
             scratch_shapes=[pltpu.VMEM(s, F32) for s in scratch],
             cost_estimate=pl.CostEstimate(
@@ -75,22 +74,27 @@
             copy.start()
             copies.append(copy)
     first.wait()
-    lane = lane_of(8)
-    mark = jnp.zeros((8, 128), F32)
+    lane = lane_of(1)
+    mark = jnp.zeros((1, 128), F32)
     for k in range(4):
         mark = jnp.where(lane == k, place[0, k].astype(F32), mark)
     for j in range(32):
-        out[j, 96:104, :] = mark
+        out[j * 97 + 96 : j * 97 + 97, :] = mark
     for f in range(3):
         for part in range(4):
             copies[f * 4 + part].wait()
             for j in range(part * 8, part * 8 + 8):
                 for m in range(8):
-                    at = f * 32 + m * 4
-                    out[j, at : at + 4, :] = buf[f, :, j * 1024 + m * 128 : j * 1024 + m * 128 + 128]
-
-
-def route_kernel(place, got, out):
+                    at = j * 97 + f * 32 + m * 4
+                    out[at : at + 4, :] = buf[f, :, j * 1024 + m * 128 : j * 1024 + m * 128 + 128]
+
+
+def route_kernel(got, out, ints, place, sem):
+    ints[...] = got[every(96, 32, 97), :].astype(jnp.int32)
+    copy = pltpu.make_async_copy(ints, place, sem.at[0])
+    copy.start()
+    copy.wait()
+
     @pl.loop(0, 32)
     def _(s):
         for k in range(4):
@@ -98,7 +102,7 @@
             t = lax.shift_right_logical(p, 2)
             q = lax.bitwise_and(p, 3)
             for f in range(3):
-                out[t, f * 4 + q] = got[s, every(f * 32 + k, 8, 4), :]
+                out[t, f * 4 + q] = got[every(s * 97 + f * 32 + k, 8, 4), :]
 
 
 DEPTH = (2, 2, 3)
@@ -649,7 +653,7 @@
     hbm = pl.BlockSpec(memory_space=pltpu.HBM)
     spread = pl.pallas_call(
         spread_kernel,
-        out_shape=jax.ShapeDtypeStruct((32, 104, 128), F32),
+        out_shape=jax.ShapeDtypeStruct((32 * 97, 128), F32),
         in_specs=[hbm] * 4,
         out_specs=pl.BlockSpec(memory_space=pltpu.VMEM),
         scratch_shapes=[
@@ -664,9 +668,20 @@
             for w in (new_place, rhs_boxes, a_boxes, b_boxes)
         )
     )
-    got = exchange(spread)
-    place = got[:, 96, :4].astype(jnp.int32)
-    (routed,) = call(route_kernel, [(32, 12, 8, 128)], smem=1)(place, got)
+    got = exchange(spread.reshape(32, 1, 97 * 128)).reshape(32 * 97, 128)
+    vmem = pl.BlockSpec(memory_space=pltpu.VMEM)
+    routed = pl.pallas_call(
+        route_kernel,
+        out_shape=jax.ShapeDtypeStruct((32, 12, 8, 128), F32),
+        in_specs=[vmem],
+        out_specs=vmem,
+        scratch_shapes=[
+            pltpu.VMEM((32, 128), jnp.int32),
+            pltpu.SMEM((32, 128), jnp.int32),
+            pltpu.SemaphoreType.DMA((1,)),
+        ],
+        compiler_params=pltpu.CompilerParams(vmem_limit_bytes=8 << 20),
+    )(got)
     got = exchange(routed)
 
     fine = (FXN * YR, 128)

time: 194 us -> 192 us (0.990)
  blocking collectives: 93.6 us -> 91.1 us
    all_to_all x1, blocking collectives: 50.7 us -> 48.4 us  [body(): got = exchange(spread.reshape(32, 1, 97 * 128)).reshape(32 * 97, 128)]
    pallas_call x15 -> x14, Pallas kernels: 31.8 us -> 30.5 us  [run(): pl.pallas_call(kernel, out_shape=[jax.ShapeDtypeStruct(s, F32) for s in o...]
  transfers between devices with their start and end apart: 18 -> 18, of which waited for: 5 -> 6; matrix products, arithmetic and copies ran while one was open for 0% -> 0% of each run, Pallas kernels for 8% -> 8%
where the time goes in v5:
time: 192 us; the launch traced here: 191 us
  blocking collectives  91.1 us (47%)
  starting transfers between devices  53.2 us (28%)
  Pallas kernels  33.4 us (17%)
  waiting for transfers between devices  12.2 us (6%)
    ppermute x18, starting transfers between devices, swap(): return (lax.ppermute(high, axis, up), lax.ppermute(low, axis, down))  53.2 us
    all_to_all x1, blocking collectives, body(): got = exchange(spread.reshape(32, 1, 97 * 128)).reshape(32 * 97, 128)  48.4 us
    all_to_all x1, blocking collectives, body(): got = exchange(routed)  42.7 us
    pallas_call x14, Pallas kernels, run(): pl.pallas_call(kernel, out_shape=[jax.ShapeDtypeStruct(s, F32) for s in o...  30.5 us
    ppermute x18, waiting for transfers between devices, swap(): return (lax.ppermute(high, axis, up), lax.ppermute(low, axis, down))  12.2 us
  transfers between devices with their start and end apart: 18, of which 6 were waited for; matrix products, arithmetic and copies ran while one was open for 0% of the time, Pallas kernels for 8%

profile of v5, /device:TPU:41, one launch (start us, length us, event | category | flops | bytes accessed | tf_op | source)
XLA Modules:
  0.0 190.9 jit_solution(11652681414663741162)
XLA Ops:
  0.6 1.6 shard_map.59
  2.2 48.4 %all_to_all.10 = f32[32,1,12416]{2,1,0:T(1,128)S(1)} all-to-all(f32[32,1,12416]{2,1,0:T(1,128)S(1)} %bitcast.5), channel_id=1, replica_groups=mesh['gx'=8,'gy'=4,'gz'=8] {'gx','gy'}, dimensions={0} | all-to-all | bytes 3178496 | tf_op jit(solution)/shard_map/all_to_all | solution.py:671
  50.6 1.3 shard_map.60
  51.9 42.7 %all_to_all.11.got = f32[32,12,8,128]{3,2,1,0:T(8,128)S(1)} all-to-all(f32[32,12,8,128]{3,2,1,0:T(8,128)S(1)} %shard_map.60), channel_id=1, replica_groups=mesh['gx'=8,'gy'=4,'gz'=8] {'gx','gy'}, dimensions={0} | all-to-all | bytes 3145728 | tf_op jit(solution)/shard_map/all_to_all | solution.py:685
  94.6 0.3 shard_map.62
  94.9 2.5 %collective-permute-start = (f32[224,128]{1,0:T(8,128)S(1)}, f32[224,128]{1,0:T(8,128)S(1)}, u32[]{:S(2)}, u32[]{:S(2)}) collective-permute-start(f32[224,128]{1,0:T(8,128)S(1)} %get-tuple-element.59), channel_id=1, source_target_pairs={{0,8},{8,16},{16,24},{1,9},{9,17},{17,25},{2,10},{10,18},{18,26},{... | collective-permute-start | bytes 344072 | tf_op jit(solution)/shard_map/ppermute | solution.py:646
  97.4 1.3 collective-permute-start.1
  98.7 2.6 %shard_map.61 = (f32[2800,128]{1,0:T(8,128)S(1)}, f32[2800,128]{1,0:T(8,128)S(1)}, f32[2800,128]{1,0:T(8,128)S(1)}, f32[280,128]{1,0:T(8,128)S(1)}, f32[280,128]{1,0:T(8,128)S(1)}) custom-call(f32[32,12,8,128]{3,2,1,0:T(8,128)S(1)} %all_to_all.11.got), custom_call_target="tpu_custom_call" | custom-call | bytes 12000000 | tf_op jit(solution)/shard_map/pallas_call | solution.py:49
  101.3 1.6 collective-permute-done.1.yhi
  102.9 0.2 shard_map.64
  103.1 2.5 %collective-permute-start.2 = (f32[160,128]{1,0:T(8,128)S(1)}, f32[160,128]{1,0:T(8,128)S(1)}, u32[]{:S(2)}, u32[]{:S(2)}) collective-permute-start(f32[160,128]{1,0:T(8,128)S(1)} %get-tuple-element.66), channel_id=1, source_target_pairs={{0,32},{32,64},{64,96},{96,128},{128,160},{160,192},{192,224},{1,3... | collective-permute-start | bytes 245768 | tf_op jit(solution)/shard_map/ppermute | solution.py:646
  105.6 2.7 %collective-permute-start.3 = (f32[160,128]{1,0:T(8,128)S(1)}, f32[160,128]{1,0:T(8,128)S(1)}, u32[]{:S(2)}, u32[]{:S(2)}) collective-permute-start(f32[160,128]{1,0:T(8,128)S(1)} %get-tuple-element.67), channel_id=1, source_target_pairs={{32,0},{64,32},{96,64},{128,96},{160,128},{192,160},{224,192},{33,... | collective-permute-start | bytes 245768 | tf_op jit(solution)/shard_map/ppermute | solution.py:646
  108.4 2.3 %shard_map.63 = (f32[2800,128]{1,0:T(8,128)S(1)}, f32[2800,128]{1,0:T(8,128)S(1)}, f32[2800,128]{1,0:T(8,128)S(1)}, f32[160,128]{1,0:T(8,128)S(1)}, f32[160,128]{1,0:T(8,128)S(1)}) custom-call(f32[2800,128]{1,0:T(8,128)S(1)} %get-tuple-element.56.rh0, f32[2800,128]{1,0:T(8,128)S(1)} %get-tuple-element.57.aa0, f32[2800,128]{1,0:T(8,128)S(1)} %get-tuple-element.58.bb0, ...), custom_call_target="tpu_custom_call" | custom-call | bytes 6000000 | tf_op jit(solution)/shard_map/pallas_call | solution.py:49
  110.7 0.1 collective-permute-done.3.xhi
  110.8 0.4 shard_map.65
  111.3 9.3 %collective-permute-start.4 = (f32[160,128]{1,0:T(8,128)S(1)}, f32[160,128]{1,0:T(8,128)S(1)}, u32[]{:S(2)}, u32[]{:S(2)}) collective-permute-start(f32[160,128]{1,0:T(8,128)S(1)} %get-tuple-element.70), channel_id=1, source_target_pairs={{0,1},{1,2},{2,3},{3,4},{4,5},{5,6},{6,7},{8,9},{9,10},{10,11},{11... | collective-permute-start | bytes 245768 | tf_op jit(solution)/shard_map/ppermute | solution.py:646
  120.6 1.9 %collective-permute-start.5 = (f32[160,128]{1,0:T(8,128)S(1)}, f32[160,128]{1,0:T(8,128)S(1)}, u32[]{:S(2)}, u32[]{:S(2)}) collective-permute-start(f32[160,128]{1,0:T(8,128)S(1)} %get-tuple-element.71), channel_id=1, source_target_pairs={{1,0},{2,1},{3,2},{4,3},{5,4},{6,5},{7,6},{9,8},{10,9},{11,10},{12... | collective-permute-start | bytes 245768 | tf_op jit(solution)/shard_map/ppermute | solution.py:646
  122.5 3.8 %collective-permute-done.5.zhi = f32[160,128]{1,0:T(8,128)S(1)} collective-permute-done((f32[160,128]{1,0:T(8,128)S(1)}, f32[160,128]{1,0:T(8,128)S(1)}, u32[]{:S(2)}, u32[]{:S(2)}) %collective-permute-start.5) | collective-permute-done | bytes 81952 | tf_op jit(solution)/shard_map/ppermute | solution.py:646
  126.4 5.5 %shard_map.66 = (f32[2800,128]{1,0:T(8,128)S(1)}, f32[2800,128]{1,0:T(8,128)S(1)}, f32[2800,128]{1,0:T(8,128)S(1)}, f32[2800,128]{1,0:T(8,128)S(1)}, f32[2800,12...) custom-call(f32[2800,128]{1,0:T(8,128)S(1)} %get-tuple-element.61.rh, ...), custom_call_target="tpu_custom_call" | custom-call | bytes 24000000 | tf_op jit(solution)/shard_map/pallas_call | solution.py:49
  131.9 2.8 %collective-permute-start.6 = (f32[288,128]{1,0:T(8,128)S(1)}, f32[288,128]{1,0:T(8,128)S(1)}, u32[]{:S(2)}, u32[]{:S(2)}) collective-permute-start(f32[288,128]{1,0:T(8,128)S(1)} %get-tuple-element.72), channel_id=1, source_target_pairs={{0,8},{8,16},{16,24},{1,9},{9,17},{17,25},{2,10},{10,18},{18,26},{... | collective-permute-start | bytes 442376 | tf_op jit(solution)/shard_map/ppermute | solution.py:646
  134.8 1.5 collective-permute-start.7
  136.2 3.4 %shard_map.67 = (f32[2800,128]{1,0:T(8,128)S(1)}, f32[640,128]{1,0:T(8,128)S(1)}, f32[288,128]{1,0:T(8,128)S(1)}, f32[288,128]{1,0:T(8,128)S(1)}) custom-call(f32[2800,128]{1,0:T(8,128)S(1)} %get-tuple-element.74.f, f32[2800,128]{1,0:T(8,128)S(1)} %get-tuple-element.75.fx, f32[2800,128]{1,0:T(8,128)S(1)} %get-tuple-element.76.fy, ...), custom_call_target="tpu_custom_call" | custom-call | bytes 18000000 | tf_op jit(solution)/shard_map/pallas_call | solution.py:49
  139.7 2.1 %collective-permute-done.7.yhi = f32[288,128]{1,0:T(8,128)S(1)} collective-permute-done((f32[288,128]{1,0:T(8,128)S(1)}, f32[288,128]{1,0:T(8,128)S(1)}, u32[]{:S(2)}, u32[]{:S(2)}) %collective-permute-start.7) | collective-permute-done | bytes 147488 | tf_op jit(solution)/shard_map/ppermute | solution.py:646
  141.7 0.1 shard_map.71
  141.9 2.1 %collective-permute-start.14 = (f32[360,128]{1,0:T(8,128)S(1)}, f32[360,128]{1,0:T(8,128)S(1)}, u32[]{:S(2)}, u32[]{:S(2)}) collective-permute-start(f32[360,128]{1,0:T(8,128)S(1)} %get-tuple-element.99), channel_id=1, source_target_pairs={{0,32},{32,64},{64,96},{96,128},{128,160},{160,192},{192,224},{1,3... | collective-permute-start | bytes 552968 | tf_op jit(solution)/shard_map/ppermute | solution.py:646
  144.0 3.2 %collective-permute-start.15 = (f32[360,128]{1,0:T(8,128)S(1)}, f32[360,128]{1,0:T(8,128)S(1)}, u32[]{:S(2)}, u32[]{:S(2)}) collective-permute-start(f32[360,128]{1,0:T(8,128)S(1)} %get-tuple-element.100), channel_id=1, source_target_pairs={{32,0},{64,32},{96,64},{128,96},{160,128},{192,160},{224,192},{33,... | collective-permute-start | bytes 552968 | tf_op jit(solution)/shard_map/ppermute | solution.py:646
  147.2 2.9 %collective-permute-start.8 = (f32[288,128]{1,0:T(8,128)S(1)}, f32[288,128]{1,0:T(8,128)S(1)}, u32[]{:S(2)}, u32[]{:S(2)}) collective-permute-start(f32[288,128]{1,0:T(8,128)S(1)} %get-tuple-element.84), channel_id=1, source_target_pairs={{0,8},{8,16},{16,24},{1,9},{9,17},{17,25},{2,10},{10,18},{18,26},{... | collective-permute-start | bytes 442376 | tf_op jit(solution)/shard_map/ppermute | solution.py:646
  150.1 1.3 collective-permute-start.9
  151.4 1.0 collective-permute-done.8.ylo
  152.4 3.6 %collective-permute-done.9.yhi = f32[288,128]{1,0:T(8,128)S(1)} collective-permute-done((f32[288,128]{1,0:T(8,128)S(1)}, f32[288,128]{1,0:T(8,128)S(1)}, u32[]{:S(2)}, u32[]{:S(2)}) %collective-permute-start.9) | collective-permute-done | bytes 147488 | tf_op jit(solution)/shard_map/ppermute | solution.py:646
  156.0 0.3 shard_map.68
  156.3 2.4 %collective-permute-start.10 = (f32[360,128]{1,0:T(8,128)S(1)}, f32[360,128]{1,0:T(8,128)S(1)}, u32[]{:S(2)}, u32[]{:S(2)}) collective-permute-start(f32[360,128]{1,0:T(8,128)S(1)} %get-tuple-element.87), channel_id=1, source_target_pairs={{0,32},{32,64},{64,96},{96,128},{128,160},{160,192},{192,224},{1,3... | collective-permute-start | bytes 552968 | tf_op jit(solution)/shard_map/ppermute | solution.py:646
  158.7 2.9 %collective-permute-start.11 = (f32[360,128]{1,0:T(8,128)S(1)}, f32[360,128]{1,0:T(8,128)S(1)}, u32[]{:S(2)}, u32[]{:S(2)}) collective-permute-start(f32[360,128]{1,0:T(8,128)S(1)} %get-tuple-element.88), channel_id=1, source_target_pairs={{32,0},{64,32},{96,64},{128,96},{160,128},{192,160},{224,192},{33,... | collective-permute-start | bytes 552968 | tf_op jit(solution)/shard_map/ppermute | solution.py:646
  161.6 0.0 collective-permute-done.14.xlo
  161.6 0.0 collective-permute-done.15.xhi
  161.6 1.1 shard_map.72
  162.7 6.1 %collective-permute-start.16 = (f32[600,128]{1,0:T(8,128)S(1)}, f32[600,128]{1,0:T(8,128)S(1)}, u32[]{:S(2)}, u32[]{:S(2)}) collective-permute-start(f32[600,128]{1,0:T(8,128)S(1)} %get-tuple-element.102), channel_id=1, source_target_pairs={{0,1},{1,2},{2,3},{3,4},{4,5},{5,6},{6,7},{8,9},{9,10},{10,11},{11... | collective-permute-start | bytes 921608 | tf_op jit(solution)/shard_map/ppermute | solution.py:646
  168.9 1.9 %collective-permute-start.17 = (f32[600,128]{1,0:T(8,128)S(1)}, f32[600,128]{1,0:T(8,128)S(1)}, u32[]{:S(2)}, u32[]{:S(2)}) collective-permute-start(f32[600,128]{1,0:T(8,128)S(1)} %get-tuple-element.103), channel_id=1, source_target_pairs={{1,0},{2,1},{3,2},{4,3},{5,4},{6,5},{7,6},{9,8},{10,9},{11,10},{12... | collective-permute-start | bytes 921608 | tf_op jit(solution)/shard_map/ppermute | solution.py:646
  170.8 0.7 shard_map.69
  171.5 0.0 collective-permute-done.10.xlo
  171.6 0.0 collective-permute-done.11.xhi
  171.6 0.5 shard_map.70
  172.0 3.6 %collective-permute-start.12 = (f32[280,128]{1,0:T(8,128)S(1)}, f32[280,128]{1,0:T(8,128)S(1)}, u32[]{:S(2)}, u32[]{:S(2)}) collective-permute-start(f32[280,128]{1,0:T(8,128)S(1)} %get-tuple-element.93), channel_id=1, source_target_pairs={{0,1},{1,2},{2,3},{3,4},{4,5},{5,6},{6,7},{8,9},{9,10},{10,11},{11... | collective-permute-start | bytes 430088 | tf_op jit(solution)/shard_map/ppermute | solution.py:646
  175.7 2.1 %collective-permute-start.13 = (f32[280,128]{1,0:T(8,128)S(1)}, f32[280,128]{1,0:T(8,128)S(1)}, u32[]{:S(2)}, u32[]{:S(2)}) collective-permute-start(f32[280,128]{1,0:T(8,128)S(1)} %get-tuple-element.94), channel_id=1, source_target_pairs={{1,0},{2,1},{3,2},{4,3},{5,4},{6,5},{7,6},{9,8},{10,9},{11,10},{12... | collective-permute-start | bytes 430088 | tf_op jit(solution)/shard_map/ppermute | solution.py:646
  177.8 0.0 collective-permute-done.16.zlo
  177.9 0.0 collective-permute-done.17.zhi
  177.9 5.1 %shard_map.73 = (f32[1120,128]{1,0:T(8,128)S(1)}, f32[1120,128]{1,0:T(8,128)S(1)}, f32[1120,128]{1,0:T(8,128)S(1)}, f32[1120,128]{1,0:T(8,128)S(1)}, f32[1120,128]{1,0:T(8,128)S(1)}) custom-call(f32[2000,128]{1,0:T(8,128)S(1)} %get-tuple-element.101.ec, f32[600,128]{1,0:T(8,128)S(1)} %collective-permute-done.16.zlo, f32[600,128]{1,0:T(8,128)S(1)} %collective-permute-done.17.zhi), custom_call_target="tpu_custom_call" | custom-call | bytes 15000000 | tf_op jit(solution)/shard_map/pallas_call | solution.py:49
  183.0 7.9 %shard_map.74 = (f32[64,32,64]{2,1,0:T(8,128)}, f32[64,32,64]{2,1,0:T(8,128)}) custom-call(f32[1000,128]{1,0:T(8,128)S(1)} %get-tuple-element.92.rm, f32[2800,128]{1,0:T(8,128)S(1)} %get-tuple-element.89.vs, f32[360,128]{1,0:T(8,128)S(1)} %collective-permute-done.10.xlo, f32[360,128]{1,0:T(8,128)S(1)} %collective-permute-done.11.xhi, ...), custom_call_target="tpu_custom_call" | custom-call | bytes 24000000 | tf_op jit(solution)/shard_map/pallas_call | solution.py:49
  (6 shorter events, 0.0 us)
Async XLA Ops:
  94.9 6.4 %collective-permute-start = (f32[224,128]{1,0:T(8,128)S(1)}, f32[224,128]{1,0:T(8,128)S(1)}, u32[]{:S(2)}, u32[]{:S(2)}) collective-permute-start(f32[224,128]{1,0:T(8,128)S(1)} %get-tuple-element.59), channel_id=1, source_target_pairs={{0,8},{8,16},{16,24},{1,9},{9,17},{17,25},{2,10},{10,18},{18,26},{... | collective-permute-start | bytes 344072 | tf_op jit(solution)/shard_map/ppermute | solution.py:646
  97.4 5.5 %collective-permute-start.1 = (f32[224,128]{1,0:T(8,128)S(1)}, f32[224,128]{1,0:T(8,128)S(1)}, u32[]{:S(2)}, u32[]{:S(2)}) collective-permute-start(f32[224,128]{1,0:T(8,128)S(1)} %get-tuple-element.60), channel_id=1, source_target_pairs={{8,0},{16,8},{24,16},{9,1},{17,9},{25,17},{10,2},{18,10},{26,18},{... | collective-permute-start | bytes 344072 | tf_op jit(solution)/shard_map/ppermute | solution.py:646
  103.1 7.6 %collective-permute-start.2 = (f32[160,128]{1,0:T(8,128)S(1)}, f32[160,128]{1,0:T(8,128)S(1)}, u32[]{:S(2)}, u32[]{:S(2)}) collective-permute-start(f32[160,128]{1,0:T(8,128)S(1)} %get-tuple-element.66), channel_id=1, source_target_pairs={{0,32},{32,64},{64,96},{96,128},{128,160},{160,192},{192,224},{1,3... | collective-permute-start | bytes 245768 | tf_op jit(solution)/shard_map/ppermute | solution.py:646
  105.6 5.2 %collective-permute-start.3 = (f32[160,128]{1,0:T(8,128)S(1)}, f32[160,128]{1,0:T(8,128)S(1)}, u32[]{:S(2)}, u32[]{:S(2)}) collective-permute-start(f32[160,128]{1,0:T(8,128)S(1)} %get-tuple-element.67), channel_id=1, source_target_pairs={{32,0},{64,32},{96,64},{128,96},{160,128},{192,160},{224,192},{33,... | collective-permute-start | bytes 245768 | tf_op jit(solution)/shard_map/ppermute | solution.py:646
  111.3 11.3 %collective-permute-start.4 = (f32[160,128]{1,0:T(8,128)S(1)}, f32[160,128]{1,0:T(8,128)S(1)}, u32[]{:S(2)}, u32[]{:S(2)}) collective-permute-start(f32[160,128]{1,0:T(8,128)S(1)} %get-tuple-element.70), channel_id=1, source_target_pairs={{0,1},{1,2},{2,3},{3,4},{4,5},{5,6},{6,7},{8,9},{9,10},{10,11},{11... | collective-permute-start | bytes 245768 | tf_op jit(solution)/shard_map/ppermute | solution.py:646
  120.6 5.8 %collective-permute-start.5 = (f32[160,128]{1,0:T(8,128)S(1)}, f32[160,128]{1,0:T(8,128)S(1)}, u32[]{:S(2)}, u32[]{:S(2)}) collective-permute-start(f32[160,128]{1,0:T(8,128)S(1)} %get-tuple-element.71), channel_id=1, source_target_pairs={{1,0},{2,1},{3,2},{4,3},{5,4},{6,5},{7,6},{9,8},{10,9},{11,10},{12... | collective-permute-start | bytes 245768 | tf_op jit(solution)/shard_map/ppermute | solution.py:646
  131.9 7.7 %collective-permute-start.6 = (f32[288,128]{1,0:T(8,128)S(1)}, f32[288,128]{1,0:T(8,128)S(1)}, u32[]{:S(2)}, u32[]{:S(2)}) collective-permute-start(f32[288,128]{1,0:T(8,128)S(1)} %get-tuple-element.72), channel_id=1, source_target_pairs={{0,8},{8,16},{16,24},{1,9},{9,17},{17,25},{2,10},{10,18},{18,26},{... | collective-permute-start | bytes 442376 | tf_op jit(solution)/shard_map/ppermute | solution.py:646
  134.8 7.0 %collective-permute-start.7 = (f32[288,128]{1,0:T(8,128)S(1)}, f32[288,128]{1,0:T(8,128)S(1)}, u32[]{:S(2)}, u32[]{:S(2)}) collective-permute-start(f32[288,128]{1,0:T(8,128)S(1)} %get-tuple-element.73), channel_id=1, source_target_pairs={{8,0},{16,8},{24,16},{9,1},{17,9},{25,17},{10,2},{18,10},{26,18},{... | collective-permute-start | bytes 442376 | tf_op jit(solution)/shard_map/ppermute | solution.py:646
  141.9 19.7 %collective-permute-start.14 = (f32[360,128]{1,0:T(8,128)S(1)}, f32[360,128]{1,0:T(8,128)S(1)}, u32[]{:S(2)}, u32[]{:S(2)}) collective-permute-start(f32[360,128]{1,0:T(8,128)S(1)} %get-tuple-element.99), channel_id=1, source_target_pairs={{0,32},{32,64},{64,96},{96,128},{128,160},{160,192},{192,224},{1,3... | collective-permute-start | bytes 552968 | tf_op jit(solution)/shard_map/ppermute | solution.py:646
  144.0 17.6 %collective-permute-start.15 = (f32[360,128]{1,0:T(8,128)S(1)}, f32[360,128]{1,0:T(8,128)S(1)}, u32[]{:S(2)}, u32[]{:S(2)}) collective-permute-start(f32[360,128]{1,0:T(8,128)S(1)} %get-tuple-element.100), channel_id=1, source_target_pairs={{32,0},{64,32},{96,64},{128,96},{160,128},{192,160},{224,192},{33,... | collective-permute-start | bytes 552968 | tf_op jit(solution)/shard_map/ppermute | solution.py:646
  147.2 5.3 %collective-permute-start.8 = (f32[288,128]{1,0:T(8,128)S(1)}, f32[288,128]{1,0:T(8,128)S(1)}, u32[]{:S(2)}, u32[]{:S(2)}) collective-permute-start(f32[288,128]{1,0:T(8,128)S(1)} %get-tuple-element.84), channel_id=1, source_target_pairs={{0,8},{8,16},{16,24},{1,9},{9,17},{17,25},{2,10},{10,18},{18,26},{... | collective-permute-start | bytes 442376 | tf_op jit(solution)/shard_map/ppermute | solution.py:646
  150.1 5.9 %collective-permute-start.9 = (f32[288,128]{1,0:T(8,128)S(1)}, f32[288,128]{1,0:T(8,128)S(1)}, u32[]{:S(2)}, u32[]{:S(2)}) collective-permute-start(f32[288,128]{1,0:T(8,128)S(1)} %get-tuple-element.85), channel_id=1, source_target_pairs={{8,0},{16,8},{24,16},{9,1},{17,9},{25,17},{10,2},{18,10},{26,18},{... | collective-permute-start | bytes 442376 | tf_op jit(solution)/shard_map/ppermute | solution.py:646
  156.3 15.2 %collective-permute-start.10 = (f32[360,128]{1,0:T(8,128)S(1)}, f32[360,128]{1,0:T(8,128)S(1)}, u32[]{:S(2)}, u32[]{:S(2)}) collective-permute-start(f32[360,128]{1,0:T(8,128)S(1)} %get-tuple-element.87), channel_id=1, source_target_pairs={{0,32},{32,64},{64,96},{96,128},{128,160},{160,192},{192,224},{1,3... | collective-permute-start | bytes 552968 | tf_op jit(solution)/shard_map/ppermute | solution.py:646
  158.7 12.9 %collective-permute-start.11 = (f32[360,128]{1,0:T(8,128)S(1)}, f32[360,128]{1,0:T(8,128)S(1)}, u32[]{:S(2)}, u32[]{:S(2)}) collective-permute-start(f32[360,128]{1,0:T(8,128)S(1)} %get-tuple-element.88), channel_id=1, source_target_pairs={{32,0},{64,32},{96,64},{128,96},{160,128},{192,160},{224,192},{33,... | collective-permute-start | bytes 552968 | tf_op jit(solution)/shard_map/ppermute | solution.py:646
  162.7 15.1 %collective-permute-start.16 = (f32[600,128]{1,0:T(8,128)S(1)}, f32[600,128]{1,0:T(8,128)S(1)}, u32[]{:S(2)}, u32[]{:S(2)}) collective-permute-start(f32[600,128]{1,0:T(8,128)S(1)} %get-tuple-element.102), channel_id=1, source_target_pairs={{0,1},{1,2},{2,3},{3,4},{4,5},{5,6},{6,7},{8,9},{9,10},{10,11},{11... | collective-permute-start | bytes 921608 | tf_op jit(solution)/shard_map/ppermute | solution.py:646
  168.9 9.0 %collective-permute-start.17 = (f32[600,128]{1,0:T(8,128)S(1)}, f32[600,128]{1,0:T(8,128)S(1)}, u32[]{:S(2)}, u32[]{:S(2)}) collective-permute-start(f32[600,128]{1,0:T(8,128)S(1)} %get-tuple-element.103), channel_id=1, source_target_pairs={{1,0},{2,1},{3,2},{4,3},{5,4},{6,5},{7,6},{9,8},{10,9},{11,10},{12... | collective-permute-start | bytes 921608 | tf_op jit(solution)/shard_map/ppermute | solution.py:646
  172.0 10.9 %collective-permute-start.12 = (f32[280,128]{1,0:T(8,128)S(1)}, f32[280,128]{1,0:T(8,128)S(1)}, u32[]{:S(2)}, u32[]{:S(2)}) collective-permute-start(f32[280,128]{1,0:T(8,128)S(1)} %get-tuple-element.93), channel_id=1, source_target_pairs={{0,1},{1,2},{2,3},{3,4},{4,5},{5,6},{6,7},{8,9},{9,10},{10,11},{11... | collective-permute-start | bytes 430088 | tf_op jit(solution)/shard_map/ppermute | solution.py:646
  175.7 7.3 %collective-permute-start.13 = (f32[280,128]{1,0:T(8,128)S(1)}, f32[280,128]{1,0:T(8,128)S(1)}, u32[]{:S(2)}, u32[]{:S(2)}) collective-permute-start(f32[280,128]{1,0:T(8,128)S(1)} %get-tuple-element.94), channel_id=1, source_target_pairs={{1,0},{2,1},{3,2},{4,3},{5,4},{6,5},{7,6},{9,8},{10,9},{11,10},{12... | collective-permute-start | bytes 430088 | tf_op jit(solution)/shard_map/ppermute | solution.py:646

commit v6 on v5

--- a/solution.py
+++ b/solution.py
@@ -270,8 +270,20 @@
     return first + second
 
 
+def mean_kernel(aa, bb, xlo, xhi, ta, tx, ty):
+    tx[plane(0), :] = zpair(0.5 * (x_plane(2, 2, xlo) + bb[plane(3), :]))
+    for i in range(32):
+        x = 2 * i + 3
+        first = bb[plane(x), :]
+        second = bb[plane(x + 1), :]
+        third = bb[plane(x + 2), :] if i < 31 else x_plane(2, 0, xhi)
+        ta[plane(i), :] = zpair(aa[plane(x), :] + aa[plane(x + 1), :])
+        tx[plane(i + 1), :] = zpair(0.5 * (second + third))
+        ty[plane(i), :] = zpair(0.5 * (first + ry(first, -1)) + 0.5 * (second + ry(second, -1)))
+
+
 def coefficient_kernel(
-    rh0, aa0, bb0, xlo, xhi, zlo, zhi, f, fx, fy, fz, ir, ib, dg, v, c1, slo, shi, a, b, ta, tx, ty, tz
+    rh0, aa0, bb0, xlo, xhi, zlo, zhi, ta, tx, ty, f, a, fx, fy, fz, c1, slo, shi, b, tz
 ):
     lane = lane_of(YR)
     for x in range(FXN):
@@ -307,9 +319,38 @@
     nothing = jnp.zeros((YR, 128), F32)
     for ref in (fx, fy, fz):
         ref[plane(FXN - 1), :] = nothing
-    for ref in (ir, ib, dg, v):
-        ref[plane(0), :] = nothing
-        ref[plane(FXN - 1), :] = nothing
+    @steps(64 // FC)
+    def _(k):
+        tz[span(k * (FC // 2), FC // 2), :] = both(fz[span(3 + k * FC, FC), :])
+
+    @steps(8)
+    def _(k):
+        base = k * 4 * YR
+        even = even_lane(80)
+
+        def rows(ref, first, planes=0):
+            return ref[every(base + planes * YR + first, 80, 2), :]
+
+        acoef = 0.125 * (rows(ta, 0) + rows(ta, 1))
+        fxp = 0.25 * (rows(tx, 0, 1) + rows(tx, 1, 1))
+        fxm = 0.25 * (rows(tx, 0) + rows(tx, 1))
+        fyp = 0.25 * rows(ty, 1)
+        s = 0.25 * (rows(tz, 0) + rows(tz, 1))
+        fzp = jnp.where(even, rl(s, -1), s)
+        diag = acoef + 0.25 * (fxp + fxm + fyp + ry(fyp, 1) + fzp + rl(fzp, 2))
+        pa = jnp.where(even, fxp, fyp)
+        pb = jnp.where(even, fzp, diag)
+        c1[pl.ds(k * 80, 80), :] = jnp.where(lane_of(80) < 64, pa, rl(pb, 64))
+
+    for dst, y0 in ((slo, 2), (shi, 9)):
+        for r in range(9):
+            dst[plane(r, 32), :] = c1[every(y0 + r, 32, 20), :]
+
+
+def presmooth_kernel(f, a, fx, fy, fz, ir, ib, dg, v, rc, slo, shi, tr, v0):
+    for ref in (ir, ib, dg, v0):
+        ref[plane(0), :] = jnp.zeros((YR, 128), F32)
+        ref[plane(FXN - 1), :] = jnp.zeros((YR, 128), F32)
 
     red = red_rows(FS)
 
@@ -327,46 +368,8 @@
         dg[at, :] = diag
         ir[at, :] = jnp.where(red, one, 0.0)
         ib[at, :] = jnp.where(red, 0.0, one)
-        v[at, :] = jnp.where(red, f[at, :] * one, 0.0)
-
-    edge = fx[plane(2), :]
-    edge = edge + jnp.where(even_lane(YR), rl(edge, -1), rl(edge, 1))
-    tx[plane(0), :] = edge
-
-    @steps(64 // FC)
-    def _(k):
-        at = span(3 + k * FC, FC)
-        to = span(k * (FC // 2), FC // 2)
-        ta[to, :] = zpair(both(a[at, :]))
-        tx[span(k * (FC // 2) + 1, FC // 2), :] = zpair(halves(fx[at, :])[1])
-        ty[to, :] = zpair(both(fy[at, :]))
-        tz[to, :] = both(fz[at, :])
-
-    @steps(8)
-    def _(k):
-        base = k * 4 * YR
-        even = even_lane(80)
-
-        def rows(ref, first, planes=0):
-            return ref[every(base + planes * YR + first, 80, 2), :]
-
-        acoef = 0.125 * (rows(ta, 0) + rows(ta, 1))
-        fxp = 0.25 * (rows(tx, 0, 1) + rows(tx, 1, 1))
-        fxm = 0.25 * (rows(tx, 0) + rows(tx, 1))
-        fyp = 0.25 * rows(ty, 1)
-        s = 0.25 * (rows(tz, 0) + rows(tz, 1))
-        fzp = jnp.where(even, rl(s, -1), s)
-        diag = acoef + 0.25 * (fxp + fxm + fyp + ry(fyp, 1) + fzp + rl(fzp, 2))
-        pa = jnp.where(even, fxp, fyp)
-        pb = jnp.where(even, fzp, diag)
-        c1[pl.ds(k * 80, 80), :] = jnp.where(lane_of(80) < 64, pa, rl(pb, 64))
-
-    for dst, y0 in ((slo, 2), (shi, 9)):
-        for r in range(9):
-            dst[plane(r, 32), :] = c1[every(y0 + r, 32, 20), :]
-
-
-def presmooth_kernel(f, fx, fy, fz, ib, dg, v0, v, rc, slo, shi, tr):
+        v0[at, :] = jnp.where(red, f[at, :] * one, 0.0)
+
     for x in (0, FXN - 1):
         v[plane(x), :] = v0[plane(x), :]
 
@@ -698,19 +701,20 @@
     )
     zlo, zhi = call(fine_z_kernel, [(4 * YR, 128)] * 2, us=1)(zlo, zhi, xlo, xhi)
     zlo, zhi = swap(zlo, zhi, "gz")
-    f, fx, fy, fz, ir, ib, dg, v, c1, cylo, cyhi = call(
+    means = call(mean_kernel, [(33 * YR, 128)] * 3)(aa, bb, xlo, xhi)
+    f, a, fx, fy, fz, c1, cylo, cyhi = call(
         coefficient_kernel,
-        [fine] * 8 + [(640, 128)] + [(9 * 32, 128)] * 2,
-        [fine, fine] + [(33 * YR, 128)] * 4,
-        us=8,
-    )(rh, aa, bb, xlo, xhi, zlo, zhi)
+        [fine] * 5 + [(640, 128)] + [(9 * 32, 128)] * 2,
+        [fine, (33 * YR, 128)],
+        us=4,
+    )(rh, aa, bb, xlo, xhi, zlo, zhi, *means)
     cylo, cyhi = swap(cylo, cyhi, "gy")
-    v, rc, ylo, yhi = call(
+    ir, ib, dg, v, rc, ylo, yhi = call(
         presmooth_kernel,
-        [fine, (640, 128)] + [(9 * 32, 128)] * 2,
-        [(32 * YR, 128)],
+        [fine] * 4 + [(640, 128)] + [(9 * 32, 128)] * 2,
+        [(32 * YR, 128), fine],
         us=6,
-    )(f, fx, fy, fz, ib, dg, v)
+    )(f, a, fx, fy, fz)
     cylo, cyhi, rc = lax.optimization_barrier((cylo, cyhi, rc))
     ylo, yhi = swap(ylo, yhi, "gy")
     ec, cxlo, cxhi = call(coef_x_kernel, [coarse] + [(9 * YR, 128)] * 2, us=1)(c1, cylo, cyhi)

time: 192 us -> 190 us (0.990)
    pallas_call x14 -> x15, Pallas kernels: 30.5 us -> 30.4 us  [run(): pl.pallas_call(kernel, out_shape=[jax.ShapeDtypeStruct(s, F32) for s in o...]
  transfers between devices with their start and end apart: 18 -> 18, of which waited for: 6 -> 5; matrix products, arithmetic and copies ran while one was open for 0% -> 0% of each run, Pallas kernels for 8% -> 9%
where the time goes in v6:
time: 190 us; the launch traced here: 189 us
  blocking collectives  91.1 us (48%)
  starting transfers between devices  53.2 us (28%)
  Pallas kernels  33.3 us (18%)
  waiting for transfers between devices  10.3 us (5%)
    ppermute x18, starting transfers between devices, swap(): return (lax.ppermute(high, axis, up), lax.ppermute(low, axis, down))  53.2 us
    all_to_all x1, blocking collectives, body(): got = exchange(spread.reshape(32, 1, 97 * 128)).reshape(32 * 97, 128)  48.4 us
    all_to_all x1, blocking collectives, body(): got = exchange(routed)  42.7 us
    pallas_call x15, Pallas kernels, run(): pl.pallas_call(kernel, out_shape=[jax.ShapeDtypeStruct(s, F32) for s in o...  30.4 us
    ppermute x18, waiting for transfers between devices, swap(): return (lax.ppermute(high, axis, up), lax.ppermute(low, axis, down))  10.3 us
  transfers between devices with their start and end apart: 18, of which 5 were waited for; matrix products, arithmetic and copies ran while one was open for 0% of the time, Pallas kernels for 9%

profile of v6, /device:TPU:41, one launch (start us, length us, event | category | flops | bytes accessed | tf_op | source)
XLA Modules:
  0.0 188.9 jit_solution(11834749911226870935)
XLA Ops:
  0.6 1.6 shard_map.59
  2.2 48.4 %all_to_all.10 = f32[32,1,12416]{2,1,0:T(1,128)S(1)} all-to-all(f32[32,1,12416]{2,1,0:T(1,128)S(1)} %bitcast.5), channel_id=1, replica_groups=mesh['gx'=8,'gy'=4,'gz'=8] {'gx','gy'}, dimensions={0} | all-to-all | bytes 3178496 | tf_op jit(solution)/shard_map/all_to_all | solution.py:674
  50.6 1.3 shard_map.60
  51.9 42.7 %all_to_all.11.got = f32[32,12,8,128]{3,2,1,0:T(8,128)S(1)} all-to-all(f32[32,12,8,128]{3,2,1,0:T(8,128)S(1)} %shard_map.60), channel_id=1, replica_groups=mesh['gx'=8,'gy'=4,'gz'=8] {'gx','gy'}, dimensions={0} | all-to-all | bytes 3145728 | tf_op jit(solution)/shard_map/all_to_all | solution.py:688
  94.6 0.3 shard_map.62
  94.9 2.5 %collective-permute-start = (f32[224,128]{1,0:T(8,128)S(1)}, f32[224,128]{1,0:T(8,128)S(1)}, u32[]{:S(2)}, u32[]{:S(2)}) collective-permute-start(f32[224,128]{1,0:T(8,128)S(1)} %get-tuple-element.62), channel_id=1, source_target_pairs={{0,8},{8,16},{16,24},{1,9},{9,17},{17,25},{2,10},{10,18},{18,26},{... | collective-permute-start | bytes 344072 | tf_op jit(solution)/shard_map/ppermute | solution.py:649
  97.4 1.3 collective-permute-start.1
  98.7 2.6 %shard_map.61 = (f32[2800,128]{1,0:T(8,128)S(1)}, f32[2800,128]{1,0:T(8,128)S(1)}, f32[2800,128]{1,0:T(8,128)S(1)}, f32[280,128]{1,0:T(8,128)S(1)}, f32[280,128]{1,0:T(8,128)S(1)}) custom-call(f32[32,12,8,128]{3,2,1,0:T(8,128)S(1)} %all_to_all.11.got), custom_call_target="tpu_custom_call" | custom-call | bytes 12000000 | tf_op jit(solution)/shard_map/pallas_call | solution.py:49
  101.3 1.6 collective-permute-done.1.yhi
  102.9 0.2 shard_map.64
  103.1 2.5 %collective-permute-start.2 = (f32[160,128]{1,0:T(8,128)S(1)}, f32[160,128]{1,0:T(8,128)S(1)}, u32[]{:S(2)}, u32[]{:S(2)}) collective-permute-start(f32[160,128]{1,0:T(8,128)S(1)} %get-tuple-element.69), channel_id=1, source_target_pairs={{0,32},{32,64},{64,96},{96,128},{128,160},{160,192},{192,224},{1,3... | collective-permute-start | bytes 245768 | tf_op jit(solution)/shard_map/ppermute | solution.py:649
  105.6 2.7 %collective-permute-start.3 = (f32[160,128]{1,0:T(8,128)S(1)}, f32[160,128]{1,0:T(8,128)S(1)}, u32[]{:S(2)}, u32[]{:S(2)}) collective-permute-start(f32[160,128]{1,0:T(8,128)S(1)} %get-tuple-element.70), channel_id=1, source_target_pairs={{32,0},{64,32},{96,64},{128,96},{160,128},{192,160},{224,192},{33,... | collective-permute-start | bytes 245768 | tf_op jit(solution)/shard_map/ppermute | solution.py:649
  108.4 2.4 %shard_map.63 = (f32[2800,128]{1,0:T(8,128)S(1)}, f32[2800,128]{1,0:T(8,128)S(1)}, f32[2800,128]{1,0:T(8,128)S(1)}, f32[160,128]{1,0:T(8,128)S(1)}, f32[160,128]{1,0:T(8,128)S(1)}) custom-call(f32[2800,128]{1,0:T(8,128)S(1)} %get-tuple-element.59.rh0, f32[2800,128]{1,0:T(8,128)S(1)} %get-tuple-element.60.aa0, f32[2800,128]{1,0:T(8,128)S(1)} %get-tuple-element.61.bb0, ...), custom_call_target="tpu_custom_call" | custom-call | bytes 6000000 | tf_op jit(solution)/shard_map/pallas_call | solution.py:49
  110.7 0.0 collective-permute-done.3.xhi
  110.8 0.4 shard_map.65
  111.3 9.3 %collective-permute-start.4 = (f32[160,128]{1,0:T(8,128)S(1)}, f32[160,128]{1,0:T(8,128)S(1)}, u32[]{:S(2)}, u32[]{:S(2)}) collective-permute-start(f32[160,128]{1,0:T(8,128)S(1)} %get-tuple-element.73), channel_id=1, source_target_pairs={{0,1},{1,2},{2,3},{3,4},{4,5},{5,6},{6,7},{8,9},{9,10},{10,11},{11... | collective-permute-start | bytes 245768 | tf_op jit(solution)/shard_map/ppermute | solution.py:649
  120.6 1.9 %collective-permute-start.5 = (f32[160,128]{1,0:T(8,128)S(1)}, f32[160,128]{1,0:T(8,128)S(1)}, u32[]{:S(2)}, u32[]{:S(2)}) collective-permute-start(f32[160,128]{1,0:T(8,128)S(1)} %get-tuple-element.74), channel_id=1, source_target_pairs={{1,0},{2,1},{3,2},{4,3},{5,4},{6,5},{7,6},{9,8},{10,9},{11,10},{12... | collective-permute-start | bytes 245768 | tf_op jit(solution)/shard_map/ppermute | solution.py:649
  122.5 1.1 shard_map.66
  123.6 2.7 %collective-permute-done.5.zhi = f32[160,128]{1,0:T(8,128)S(1)} collective-permute-done((f32[160,128]{1,0:T(8,128)S(1)}, f32[160,128]{1,0:T(8,128)S(1)}, u32[]{:S(2)}, u32[]{:S(2)}) %collective-permute-start.5) | collective-permute-done | bytes 81952 | tf_op jit(solution)/shard_map/ppermute | solution.py:649
  126.4 3.5 %shard_map.67 = (f32[2800,128]{1,0:T(8,128)S(1)}, f32[2800,128]{1,0:T(8,128)S(1)}, f32[2800,128]{1,0:T(8,128)S(1)}, f32[2800,128]{1,0:T(8,128)S(1)}, f32[2800,12...) custom-call(f32[2800,128]{1,0:T(8,128)S(1)} %get-tuple-element.64.rh0, ...), custom_call_target="tpu_custom_call" | custom-call | bytes 12000000 | tf_op jit(solution)/shard_map/pallas_call | solution.py:49
  129.9 2.8 %collective-permute-start.6 = (f32[288,128]{1,0:T(8,128)S(1)}, f32[288,128]{1,0:T(8,128)S(1)}, u32[]{:S(2)}, u32[]{:S(2)}) collective-permute-start(f32[288,128]{1,0:T(8,128)S(1)} %get-tuple-element.78), channel_id=1, source_target_pairs={{0,8},{8,16},{16,24},{1,9},{9,17},{17,25},{2,10},{10,18},{18,26},{... | collective-permute-start | bytes 442376 | tf_op jit(solution)/shard_map/ppermute | solution.py:649
  132.7 1.5 collective-permute-start.7
  134.2 4.2 %shard_map.68 = (f32[2800,128]{1,0:T(8,128)S(1)}, f32[2800,128]{1,0:T(8,128)S(1)}, f32[2800,128]{1,0:T(8,128)S(1)}, f32[2800,128]{1,0:T(8,128)S(1)}, f32[640,128...) custom-call(f32[2800,128]{1,0:T(8,128)S(1)} %get-tuple-element.80.f, ...), custom_call_target="tpu_custom_call" | custom-call | bytes 18000000 | tf_op jit(solution)/shard_map/pallas_call | solution.py:49
  138.4 0.0 collective-permute-done.6.ylo
  138.4 1.3 collective-permute-done.7.yhi
  139.7 0.1 shard_map.72
  139.9 2.1 %collective-permute-start.14 = (f32[360,128]{1,0:T(8,128)S(1)}, f32[360,128]{1,0:T(8,128)S(1)}, u32[]{:S(2)}, u32[]{:S(2)}) collective-permute-start(f32[360,128]{1,0:T(8,128)S(1)} %get-tuple-element.103), channel_id=1, source_target_pairs={{0,32},{32,64},{64,96},{96,128},{128,160},{160,192},{192,224},{1,3... | collective-permute-start | bytes 552968 | tf_op jit(solution)/shard_map/ppermute | solution.py:649
  142.0 3.2 %collective-permute-start.15 = (f32[360,128]{1,0:T(8,128)S(1)}, f32[360,128]{1,0:T(8,128)S(1)}, u32[]{:S(2)}, u32[]{:S(2)}) collective-permute-start(f32[360,128]{1,0:T(8,128)S(1)} %get-tuple-element.104), channel_id=1, source_target_pairs={{32,0},{64,32},{96,64},{128,96},{160,128},{192,160},{224,192},{33,... | collective-permute-start | bytes 552968 | tf_op jit(solution)/shard_map/ppermute | solution.py:649
  145.2 2.9 %collective-permute-start.8 = (f32[288,128]{1,0:T(8,128)S(1)}, f32[288,128]{1,0:T(8,128)S(1)}, u32[]{:S(2)}, u32[]{:S(2)}) collective-permute-start(f32[288,128]{1,0:T(8,128)S(1)} %get-tuple-element.88), channel_id=1, source_target_pairs={{0,8},{8,16},{16,24},{1,9},{9,17},{17,25},{2,10},{10,18},{18,26},{... | collective-permute-start | bytes 442376 | tf_op jit(solution)/shard_map/ppermute | solution.py:649
  148.1 1.3 collective-permute-start.9
  149.4 1.0 collective-permute-done.8.ylo
  150.4 3.6 %collective-permute-done.9.yhi = f32[288,128]{1,0:T(8,128)S(1)} collective-permute-done((f32[288,128]{1,0:T(8,128)S(1)}, f32[288,128]{1,0:T(8,128)S(1)}, u32[]{:S(2)}, u32[]{:S(2)}) %collective-permute-start.9) | collective-permute-done | bytes 147488 | tf_op jit(solution)/shard_map/ppermute | solution.py:649
  154.0 0.3 shard_map.69
  154.3 3.4 %collective-permute-start.10 = (f32[360,128]{1,0:T(8,128)S(1)}, f32[360,128]{1,0:T(8,128)S(1)}, u32[]{:S(2)}, u32[]{:S(2)}) collective-permute-start(f32[360,128]{1,0:T(8,128)S(1)} %get-tuple-element.91), channel_id=1, source_target_pairs={{0,32},{32,64},{64,96},{96,128},{128,160},{160,192},{192,224},{1,3... | collective-permute-start | bytes 552968 | tf_op jit(solution)/shard_map/ppermute | solution.py:649
  157.7 1.9 %collective-permute-start.11 = (f32[360,128]{1,0:T(8,128)S(1)}, f32[360,128]{1,0:T(8,128)S(1)}, u32[]{:S(2)}, u32[]{:S(2)}) collective-permute-start(f32[360,128]{1,0:T(8,128)S(1)} %get-tuple-element.92), channel_id=1, source_target_pairs={{32,0},{64,32},{96,64},{128,96},{160,128},{192,160},{224,192},{33,... | collective-permute-start | bytes 552968 | tf_op jit(solution)/shard_map/ppermute | solution.py:649
  159.7 0.0 collective-permute-done.15.xhi
  159.7 1.1 shard_map.73
  160.8 6.0 %collective-permute-start.16 = (f32[600,128]{1,0:T(8,128)S(1)}, f32[600,128]{1,0:T(8,128)S(1)}, u32[]{:S(2)}, u32[]{:S(2)}) collective-permute-start(f32[600,128]{1,0:T(8,128)S(1)} %get-tuple-element.106), channel_id=1, source_target_pairs={{0,1},{1,2},{2,3},{3,4},{4,5},{5,6},{6,7},{8,9},{9,10},{10,11},{11... | collective-permute-start | bytes 921608 | tf_op jit(solution)/shard_map/ppermute | solution.py:649
  166.8 1.9 %collective-permute-start.17 = (f32[600,128]{1,0:T(8,128)S(1)}, f32[600,128]{1,0:T(8,128)S(1)}, u32[]{:S(2)}, u32[]{:S(2)}) collective-permute-start(f32[600,128]{1,0:T(8,128)S(1)} %get-tuple-element.107), channel_id=1, source_target_pairs={{1,0},{2,1},{3,2},{4,3},{5,4},{6,5},{7,6},{9,8},{10,9},{11,10},{12... | collective-permute-start | bytes 921608 | tf_op jit(solution)/shard_map/ppermute | solution.py:649
  168.8 0.7 shard_map.70
  169.5 0.0 collective-permute-done.10.xlo
  169.5 0.5 shard_map.71
  170.0 3.6 %collective-permute-start.12 = (f32[280,128]{1,0:T(8,128)S(1)}, f32[280,128]{1,0:T(8,128)S(1)}, u32[]{:S(2)}, u32[]{:S(2)}) collective-permute-start(f32[280,128]{1,0:T(8,128)S(1)} %get-tuple-element.97), channel_id=1, source_target_pairs={{0,1},{1,2},{2,3},{3,4},{4,5},{5,6},{6,7},{8,9},{9,10},{10,11},{11... | collective-permute-start | bytes 430088 | tf_op jit(solution)/shard_map/ppermute | solution.py:649
  173.7 2.1 %collective-permute-start.13 = (f32[280,128]{1,0:T(8,128)S(1)}, f32[280,128]{1,0:T(8,128)S(1)}, u32[]{:S(2)}, u32[]{:S(2)}) collective-permute-start(f32[280,128]{1,0:T(8,128)S(1)} %get-tuple-element.98), channel_id=1, source_target_pairs={{1,0},{2,1},{3,2},{4,3},{5,4},{6,5},{7,6},{9,8},{10,9},{11,10},{12... | collective-permute-start | bytes 430088 | tf_op jit(solution)/shard_map/ppermute | solution.py:649
  175.8 0.0 collective-permute-done.17.zhi
  175.9 5.1 %shard_map.74 = (f32[1120,128]{1,0:T(8,128)S(1)}, f32[1120,128]{1,0:T(8,128)S(1)}, f32[1120,128]{1,0:T(8,128)S(1)}, f32[1120,128]{1,0:T(8,128)S(1)}, f32[1120,128]{1,0:T(8,128)S(1)}) custom-call(f32[2000,128]{1,0:T(8,128)S(1)} %get-tuple-element.105.ec, f32[600,128]{1,0:T(8,128)S(1)} %collective-permute-done.16.zlo, f32[600,128]{1,0:T(8,128)S(1)} %collective-permute-done.17.zhi), custom_call_target="tpu_custom_call" | custom-call | bytes 15000000 | tf_op jit(solution)/shard_map/pallas_call | solution.py:49
  181.0 0.0 collective-permute-done.13.zhi
  181.0 7.9 %shard_map.75 = (f32[64,32,64]{2,1,0:T(8,128)}, f32[64,32,64]{2,1,0:T(8,128)}) custom-call(f32[1000,128]{1,0:T(8,128)S(1)} %get-tuple-element.96.rm, f32[2800,128]{1,0:T(8,128)S(1)} %get-tuple-element.93.vs, f32[360,128]{1,0:T(8,128)S(1)} %collective-permute-done.10.xlo, f32[360,128]{1,0:T(8,128)S(1)} %collective-permute-done.11.xhi, ...), custom_call_target="tpu_custom_call" | custom-call | bytes 24000000 | tf_op jit(solution)/shard_map/pallas_call | solution.py:49
  (7 shorter events, 0.0 us)
Async XLA Ops:
  94.9 6.4 %collective-permute-start = (f32[224,128]{1,0:T(8,128)S(1)}, f32[224,128]{1,0:T(8,128)S(1)}, u32[]{:S(2)}, u32[]{:S(2)}) collective-permute-start(f32[224,128]{1,0:T(8,128)S(1)} %get-tuple-element.62), channel_id=1, source_target_pairs={{0,8},{8,16},{16,24},{1,9},{9,17},{17,25},{2,10},{10,18},{18,26},{... | collective-permute-start | bytes 344072 | tf_op jit(solution)/shard_map/ppermute | solution.py:649
  97.4 5.5 %collective-permute-start.1 = (f32[224,128]{1,0:T(8,128)S(1)}, f32[224,128]{1,0:T(8,128)S(1)}, u32[]{:S(2)}, u32[]{:S(2)}) collective-permute-start(f32[224,128]{1,0:T(8,128)S(1)} %get-tuple-element.63), channel_id=1, source_target_pairs={{8,0},{16,8},{24,16},{9,1},{17,9},{25,17},{10,2},{18,10},{26,18},{... | collective-permute-start | bytes 344072 | tf_op jit(solution)/shard_map/ppermute | solution.py:649
  103.1 7.7 %collective-permute-start.2 = (f32[160,128]{1,0:T(8,128)S(1)}, f32[160,128]{1,0:T(8,128)S(1)}, u32[]{:S(2)}, u32[]{:S(2)}) collective-permute-start(f32[160,128]{1,0:T(8,128)S(1)} %get-tuple-element.69), channel_id=1, source_target_pairs={{0,32},{32,64},{64,96},{96,128},{128,160},{160,192},{192,224},{1,3... | collective-permute-start | bytes 245768 | tf_op jit(solution)/shard_map/ppermute | solution.py:649
  105.6 5.2 %collective-permute-start.3 = (f32[160,128]{1,0:T(8,128)S(1)}, f32[160,128]{1,0:T(8,128)S(1)}, u32[]{:S(2)}, u32[]{:S(2)}) collective-permute-start(f32[160,128]{1,0:T(8,128)S(1)} %get-tuple-element.70), channel_id=1, source_target_pairs={{32,0},{64,32},{96,64},{128,96},{160,128},{192,160},{224,192},{33,... | collective-permute-start | bytes 245768 | tf_op jit(solution)/shard_map/ppermute | solution.py:649
  111.3 12.4 %collective-permute-start.4 = (f32[160,128]{1,0:T(8,128)S(1)}, f32[160,128]{1,0:T(8,128)S(1)}, u32[]{:S(2)}, u32[]{:S(2)}) collective-permute-start(f32[160,128]{1,0:T(8,128)S(1)} %get-tuple-element.73), channel_id=1, source_target_pairs={{0,1},{1,2},{2,3},{3,4},{4,5},{5,6},{6,7},{8,9},{9,10},{10,11},{11... | collective-permute-start | bytes 245768 | tf_op jit(solution)/shard_map/ppermute | solution.py:649
  120.6 5.8 %collective-permute-start.5 = (f32[160,128]{1,0:T(8,128)S(1)}, f32[160,128]{1,0:T(8,128)S(1)}, u32[]{:S(2)}, u32[]{:S(2)}) collective-permute-start(f32[160,128]{1,0:T(8,128)S(1)} %get-tuple-element.74), channel_id=1, source_target_pairs={{1,0},{2,1},{3,2},{4,3},{5,4},{6,5},{7,6},{9,8},{10,9},{11,10},{12... | collective-permute-start | bytes 245768 | tf_op jit(solution)/shard_map/ppermute | solution.py:649
  129.9 8.5 %collective-permute-start.6 = (f32[288,128]{1,0:T(8,128)S(1)}, f32[288,128]{1,0:T(8,128)S(1)}, u32[]{:S(2)}, u32[]{:S(2)}) collective-permute-start(f32[288,128]{1,0:T(8,128)S(1)} %get-tuple-element.78), channel_id=1, source_target_pairs={{0,8},{8,16},{16,24},{1,9},{9,17},{17,25},{2,10},{10,18},{18,26},{... | collective-permute-start | bytes 442376 | tf_op jit(solution)/shard_map/ppermute | solution.py:649
  132.7 7.0 %collective-permute-start.7 = (f32[288,128]{1,0:T(8,128)S(1)}, f32[288,128]{1,0:T(8,128)S(1)}, u32[]{:S(2)}, u32[]{:S(2)}) collective-permute-start(f32[288,128]{1,0:T(8,128)S(1)} %get-tuple-element.79), channel_id=1, source_target_pairs={{8,0},{16,8},{24,16},{9,1},{17,9},{25,17},{10,2},{18,10},{26,18},{... | collective-permute-start | bytes 442376 | tf_op jit(solution)/shard_map/ppermute | solution.py:649
  139.9 19.8 %collective-permute-start.14 = (f32[360,128]{1,0:T(8,128)S(1)}, f32[360,128]{1,0:T(8,128)S(1)}, u32[]{:S(2)}, u32[]{:S(2)}) collective-permute-start(f32[360,128]{1,0:T(8,128)S(1)} %get-tuple-element.103), channel_id=1, source_target_pairs={{0,32},{32,64},{64,96},{96,128},{128,160},{160,192},{192,224},{1,3... | collective-permute-start | bytes 552968 | tf_op jit(solution)/shard_map/ppermute | solution.py:649
  142.0 17.7 %collective-permute-start.15 = (f32[360,128]{1,0:T(8,128)S(1)}, f32[360,128]{1,0:T(8,128)S(1)}, u32[]{:S(2)}, u32[]{:S(2)}) collective-permute-start(f32[360,128]{1,0:T(8,128)S(1)} %get-tuple-element.104), channel_id=1, source_target_pairs={{32,0},{64,32},{96,64},{128,96},{160,128},{192,160},{224,192},{33,... | collective-permute-start | bytes 552968 | tf_op jit(solution)/shard_map/ppermute | solution.py:649
  145.2 5.3 %collective-permute-start.8 = (f32[288,128]{1,0:T(8,128)S(1)}, f32[288,128]{1,0:T(8,128)S(1)}, u32[]{:S(2)}, u32[]{:S(2)}) collective-permute-start(f32[288,128]{1,0:T(8,128)S(1)} %get-tuple-element.88), channel_id=1, source_target_pairs={{0,8},{8,16},{16,24},{1,9},{9,17},{17,25},{2,10},{10,18},{18,26},{... | collective-permute-start | bytes 442376 | tf_op jit(solution)/shard_map/ppermute | solution.py:649
  148.1 5.9 %collective-permute-start.9 = (f32[288,128]{1,0:T(8,128)S(1)}, f32[288,128]{1,0:T(8,128)S(1)}, u32[]{:S(2)}, u32[]{:S(2)}) collective-permute-start(f32[288,128]{1,0:T(8,128)S(1)} %get-tuple-element.89), channel_id=1, source_target_pairs={{8,0},{16,8},{24,16},{9,1},{17,9},{25,17},{10,2},{18,10},{26,18},{... | collective-permute-start | bytes 442376 | tf_op jit(solution)/shard_map/ppermute | solution.py:649
  154.3 15.2 %collective-permute-start.10 = (f32[360,128]{1,0:T(8,128)S(1)}, f32[360,128]{1,0:T(8,128)S(1)}, u32[]{:S(2)}, u32[]{:S(2)}) collective-permute-start(f32[360,128]{1,0:T(8,128)S(1)} %get-tuple-element.91), channel_id=1, source_target_pairs={{0,32},{32,64},{64,96},{96,128},{128,160},{160,192},{192,224},{1,3... | collective-permute-start | bytes 552968 | tf_op jit(solution)/shard_map/ppermute | solution.py:649
  157.7 11.8 %collective-permute-start.11 = (f32[360,128]{1,0:T(8,128)S(1)}, f32[360,128]{1,0:T(8,128)S(1)}, u32[]{:S(2)}, u32[]{:S(2)}) collective-permute-start(f32[360,128]{1,0:T(8,128)S(1)} %get-tuple-element.92), channel_id=1, source_target_pairs={{32,0},{64,32},{96,64},{128,96},{160,128},{192,160},{224,192},{33,... | collective-permute-start | bytes 552968 | tf_op jit(solution)/shard_map/ppermute | solution.py:649
  160.8 15.0 %collective-permute-start.16 = (f32[600,128]{1,0:T(8,128)S(1)}, f32[600,128]{1,0:T(8,128)S(1)}, u32[]{:S(2)}, u32[]{:S(2)}) collective-permute-start(f32[600,128]{1,0:T(8,128)S(1)} %get-tuple-element.106), channel_id=1, source_target_pairs={{0,1},{1,2},{2,3},{3,4},{4,5},{5,6},{6,7},{8,9},{9,10},{10,11},{11... | collective-permute-start | bytes 921608 | tf_op jit(solution)/shard_map/ppermute | solution.py:649
  166.8 9.0 %collective-permute-start.17 = (f32[600,128]{1,0:T(8,128)S(1)}, f32[600,128]{1,0:T(8,128)S(1)}, u32[]{:S(2)}, u32[]{:S(2)}) collective-permute-start(f32[600,128]{1,0:T(8,128)S(1)} %get-tuple-element.107), channel_id=1, source_target_pairs={{1,0},{2,1},{3,2},{4,3},{5,4},{6,5},{7,6},{9,8},{10,9},{11,10},{12... | collective-permute-start | bytes 921608 | tf_op jit(solution)/shard_map/ppermute | solution.py:649
  170.0 10.9 %collective-permute-start.12 = (f32[280,128]{1,0:T(8,128)S(1)}, f32[280,128]{1,0:T(8,128)S(1)}, u32[]{:S(2)}, u32[]{:S(2)}) collective-permute-start(f32[280,128]{1,0:T(8,128)S(1)} %get-tuple-element.97), channel_id=1, source_target_pairs={{0,1},{1,2},{2,3},{3,4},{4,5},{5,6},{6,7},{8,9},{9,10},{10,11},{11... | collective-permute-start | bytes 430088 | tf_op jit(solution)/shard_map/ppermute | solution.py:649
  173.7 7.3 %collective-permute-start.13 = (f32[280,128]{1,0:T(8,128)S(1)}, f32[280,128]{1,0:T(8,128)S(1)}, u32[]{:S(2)}, u32[]{:S(2)}) collective-permute-start(f32[280,128]{1,0:T(8,128)S(1)} %get-tuple-element.98), channel_id=1, source_target_pairs={{1,0},{2,1},{3,2},{4,3},{5,4},{6,5},{7,6},{9,8},{10,9},{11,10},{12... | collective-permute-start | bytes 430088 | tf_op jit(solution)/shard_map/ppermute | solution.py:649

commit v7 on v6

--- a/solution.py
+++ b/solution.py
@@ -518,7 +518,22 @@
 CC = 1
 
 
-def merge_kernel(ec, zlo, zhi, cx, cy, cz, jr, jb):
+def merge_own_kernel(ec, ox, oy, oz, od):
+    even = even_lane(YR)
+
+    def load(which, x):
+        if not 0 <= x < CXN:
+            return jnp.zeros((YR, 128), F32)
+        return rl(ec[plane(x), :], 64 * which)
+
+    for p in range(27):
+        for which, (low, high) in enumerate(((ox, oy), (oz, od))):
+            first, second = load(which, p - 1), load(which, p + 24)
+            low[plane(p), :] = jnp.where(even, first, rl(second, 1))
+            high[plane(p), :] = jnp.where(even, rl(first, -1), second)
+
+
+def merge_kernel(ox, oy, oz, od, zlo, zhi, cx, cy, cz, jr, jb):
     lane = lane_of(YR)
     even = even_lane(YR)
     own = lane < 64
@@ -532,17 +547,19 @@
         if not 0 <= x < CXN:
             return nothing
         group, at = coef_slot(which, x)
-        w = jnp.where(own, rl(ec[plane(x), :], 64 * which), 0.0)
-        w = jnp.where(below, rl(zlo[group, :], -18 - at), w)
+        w = jnp.where(below, rl(zlo[group, :], -18 - at), 0.0)
         return jnp.where(above, rl(zhi[group, :], 64 - at), w)
 
     for p in range(27):
         first, second = load(0, p - 1), load(0, p + 24)
-        cx[plane(p), :] = 0.25 * jnp.where(even, first, rl(second, 1))
-        cy[plane(p), :] = 0.25 * jnp.where(even, rl(first, -1), second)
+        w = jnp.where(even, first, rl(second, 1))
+        cx[plane(p), :] = 0.25 * jnp.where(own, ox[plane(p), :], w)
+        w = jnp.where(even, rl(first, -1), second)
+        cy[plane(p), :] = 0.25 * jnp.where(own, oy[plane(p), :], w)
         first, second = load(1, p - 1), load(1, p + 24)
-        cz[plane(p), :] = 0.25 * jnp.where(even, first, rl(second, 1))
-        diag = jnp.where(even, rl(first, -1), second)
+        w = jnp.where(even, first, rl(second, 1))
+        cz[plane(p), :] = 0.25 * jnp.where(own, oz[plane(p), :], w)
+        diag = jnp.where(own, od[plane(p), :], jnp.where(even, rl(first, -1), second))
         inside = diag > 0.0
         one = jnp.where(inside, 1.0 / jnp.where(inside, diag, 1.0), 0.0)
         mine, other = (jr, jb) if p % 2 == 0 else (jb, jr)
@@ -725,14 +742,16 @@
     xlo, xhi = swap(xlo, xhi, "gx")
     ec, czlo, czhi = call(coef_z_kernel, [coarse] + [(15 * YR, 128)] * 2)(ec, cxlo, cxhi)
     czlo, czhi = swap(czlo, czhi, "gz")
+    owned = call(merge_own_kernel, [(MXN * YR, 128)] * 4)(ec)
     plo, phi = call(smooth_z_kernel, [(7 * YR, 128)] * 2)(vs)
+    plo, *owned = lax.optimization_barrier((plo, *owned))
     rm, zlo, zhi = call(rhs_z_kernel, [(25 * YR, 128)] + [(7 * YR, 128)] * 2, us=1)(
         er, xlo, xhi, plo, phi
     )
     rxlo, rxhi = xlo, xhi
     zlo, zhi = swap(zlo, zhi, "gz")
     merged = (MXN * YR, 128)
-    coefs = call(merge_kernel, [merged] * 5, us=5)(ec, czlo, czhi)
+    coefs = call(merge_kernel, [merged] * 5, us=5)(*owned, czlo, czhi)
     return tuple(
         call(
             finish_kernel,

time: 190 us -> 192 us (1.011)
  Pallas kernels: 33.3 us -> 35.8 us
    pallas_call x15 -> x16, Pallas kernels: 30.4 us -> 32.9 us  [run(): pl.pallas_call(kernel, out_shape=[jax.ShapeDtypeStruct(s, F32) for s in o...]
  transfers between devices with their start and end apart: 18 -> 18, of which waited for: 5 -> 5; matrix products, arithmetic and copies ran while one was open for 0% -> 0% of each run, Pallas kernels for 9% -> 10%
where the time goes in v7:
time: 192 us; the launch traced here: 191 us
  blocking collectives  91.1 us (47%)
  starting transfers between devices  53.2 us (28%)
  Pallas kernels  35.8 us (19%)
  waiting for transfers between devices  10.3 us (5%)
    ppermute x18, starting transfers between devices, swap(): return (lax.ppermute(high, axis, up), lax.ppermute(low, axis, down))  53.2 us
    all_to_all x1, blocking collectives, body(): got = exchange(spread.reshape(32, 1, 97 * 128)).reshape(32 * 97, 128)  48.4 us
    all_to_all x1, blocking collectives, body(): got = exchange(routed)  42.7 us
    pallas_call x16, Pallas kernels, run(): pl.pallas_call(kernel, out_shape=[jax.ShapeDtypeStruct(s, F32) for s in o...  32.9 us
    ppermute x18, waiting for transfers between devices, swap(): return (lax.ppermute(high, axis, up), lax.ppermute(low, axis, down))  10.3 us
  transfers between devices with their start and end apart: 18, of which 5 were waited for; matrix products, arithmetic and copies ran while one was open for 0% of the time, Pallas kernels for 10%

profile of v7, /device:TPU:41, one launch (start us, length us, event | category | flops | bytes accessed | tf_op | source)
XLA Modules:
  0.0 191.4 jit_solution(5030519055547707922)
XLA Ops:
  0.6 1.6 shard_map.59
  2.2 48.4 %all_to_all.10 = f32[32,1,12416]{2,1,0:T(1,128)S(1)} all-to-all(f32[32,1,12416]{2,1,0:T(1,128)S(1)} %bitcast.5), channel_id=1, replica_groups=mesh['gx'=8,'gy'=4,'gz'=8] {'gx','gy'}, dimensions={0} | all-to-all | bytes 3178496 | tf_op jit(solution)/shard_map/all_to_all | solution.py:691
  50.6 1.3 shard_map.60
  51.9 42.7 %all_to_all.11.got = f32[32,12,8,128]{3,2,1,0:T(8,128)S(1)} all-to-all(f32[32,12,8,128]{3,2,1,0:T(8,128)S(1)} %shard_map.60), channel_id=1, replica_groups=mesh['gx'=8,'gy'=4,'gz'=8] {'gx','gy'}, dimensions={0} | all-to-all | bytes 3145728 | tf_op jit(solution)/shard_map/all_to_all | solution.py:705
  94.6 0.3 shard_map.62
  94.9 2.5 %collective-permute-start = (f32[224,128]{1,0:T(8,128)S(1)}, f32[224,128]{1,0:T(8,128)S(1)}, u32[]{:S(2)}, u32[]{:S(2)}) collective-permute-start(f32[224,128]{1,0:T(8,128)S(1)} %get-tuple-element.71), channel_id=1, source_target_pairs={{0,8},{8,16},{16,24},{1,9},{9,17},{17,25},{2,10},{10,18},{18,26},{... | collective-permute-start | bytes 344072 | tf_op jit(solution)/shard_map/ppermute | solution.py:666
  97.4 1.3 collective-permute-start.1
  98.7 2.6 %shard_map.61 = (f32[2800,128]{1,0:T(8,128)S(1)}, f32[2800,128]{1,0:T(8,128)S(1)}, f32[2800,128]{1,0:T(8,128)S(1)}, f32[280,128]{1,0:T(8,128)S(1)}, f32[280,128]{1,0:T(8,128)S(1)}) custom-call(f32[32,12,8,128]{3,2,1,0:T(8,128)S(1)} %all_to_all.11.got), custom_call_target="tpu_custom_call" | custom-call | bytes 12000000 | tf_op jit(solution)/shard_map/pallas_call | solution.py:49
  101.3 1.6 collective-permute-done.1.yhi
  102.9 0.2 shard_map.64
  103.1 2.5 %collective-permute-start.2 = (f32[160,128]{1,0:T(8,128)S(1)}, f32[160,128]{1,0:T(8,128)S(1)}, u32[]{:S(2)}, u32[]{:S(2)}) collective-permute-start(f32[160,128]{1,0:T(8,128)S(1)} %get-tuple-element.78), channel_id=1, source_target_pairs={{0,32},{32,64},{64,96},{96,128},{128,160},{160,192},{192,224},{1,3... | collective-permute-start | bytes 245768 | tf_op jit(solution)/shard_map/ppermute | solution.py:666
  105.6 2.7 %collective-permute-start.3 = (f32[160,128]{1,0:T(8,128)S(1)}, f32[160,128]{1,0:T(8,128)S(1)}, u32[]{:S(2)}, u32[]{:S(2)}) collective-permute-start(f32[160,128]{1,0:T(8,128)S(1)} %get-tuple-element.79), channel_id=1, source_target_pairs={{32,0},{64,32},{96,64},{128,96},{160,128},{192,160},{224,192},{33,... | collective-permute-start | bytes 245768 | tf_op jit(solution)/shard_map/ppermute | solution.py:666
  108.4 2.4 %shard_map.63 = (f32[2800,128]{1,0:T(8,128)S(1)}, f32[2800,128]{1,0:T(8,128)S(1)}, f32[2800,128]{1,0:T(8,128)S(1)}, f32[160,128]{1,0:T(8,128)S(1)}, f32[160,128]{1,0:T(8,128)S(1)}) custom-call(f32[2800,128]{1,0:T(8,128)S(1)} %get-tuple-element.68.rh0, f32[2800,128]{1,0:T(8,128)S(1)} %get-tuple-element.69.aa0, f32[2800,128]{1,0:T(8,128)S(1)} %get-tuple-element.70.bb0, ...), custom_call_target="tpu_custom_call" | custom-call | bytes 6000000 | tf_op jit(solution)/shard_map/pallas_call | solution.py:49
  110.7 0.0 collective-permute-done.3.xhi
  110.8 0.4 shard_map.65
  111.3 9.3 %collective-permute-start.4 = (f32[160,128]{1,0:T(8,128)S(1)}, f32[160,128]{1,0:T(8,128)S(1)}, u32[]{:S(2)}, u32[]{:S(2)}) collective-permute-start(f32[160,128]{1,0:T(8,128)S(1)} %get-tuple-element.82), channel_id=1, source_target_pairs={{0,1},{1,2},{2,3},{3,4},{4,5},{5,6},{6,7},{8,9},{9,10},{10,11},{11... | collective-permute-start | bytes 245768 | tf_op jit(solution)/shard_map/ppermute | solution.py:666
  120.6 1.9 %collective-permute-start.5 = (f32[160,128]{1,0:T(8,128)S(1)}, f32[160,128]{1,0:T(8,128)S(1)}, u32[]{:S(2)}, u32[]{:S(2)}) collective-permute-start(f32[160,128]{1,0:T(8,128)S(1)} %get-tuple-element.83), channel_id=1, source_target_pairs={{1,0},{2,1},{3,2},{4,3},{5,4},{6,5},{7,6},{9,8},{10,9},{11,10},{12... | collective-permute-start | bytes 245768 | tf_op jit(solution)/shard_map/ppermute | solution.py:666
  122.5 1.1 shard_map.66
  123.6 2.7 %collective-permute-done.5.zhi = f32[160,128]{1,0:T(8,128)S(1)} collective-permute-done((f32[160,128]{1,0:T(8,128)S(1)}, f32[160,128]{1,0:T(8,128)S(1)}, u32[]{:S(2)}, u32[]{:S(2)}) %collective-permute-start.5) | collective-permute-done | bytes 81952 | tf_op jit(solution)/shard_map/ppermute | solution.py:666
  126.4 3.5 %shard_map.67 = (f32[2800,128]{1,0:T(8,128)S(1)}, f32[2800,128]{1,0:T(8,128)S(1)}, f32[2800,128]{1,0:T(8,128)S(1)}, f32[2800,128]{1,0:T(8,128)S(1)}, f32[2800,12...) custom-call(f32[2800,128]{1,0:T(8,128)S(1)} %get-tuple-element.73.rh0, ...), custom_call_target="tpu_custom_call" | custom-call | bytes 12000000 | tf_op jit(solution)/shard_map/pallas_call | solution.py:49
  129.9 2.8 %collective-permute-start.6 = (f32[288,128]{1,0:T(8,128)S(1)}, f32[288,128]{1,0:T(8,128)S(1)}, u32[]{:S(2)}, u32[]{:S(2)}) collective-permute-start(f32[288,128]{1,0:T(8,128)S(1)} %get-tuple-element.87), channel_id=1, source_target_pairs={{0,8},{8,16},{16,24},{1,9},{9,17},{17,25},{2,10},{10,18},{18,26},{... | collective-permute-start | bytes 442376 | tf_op jit(solution)/shard_map/ppermute | solution.py:666
  132.7 1.5 collective-permute-start.7
  134.2 4.2 %shard_map.68 = (f32[2800,128]{1,0:T(8,128)S(1)}, f32[2800,128]{1,0:T(8,128)S(1)}, f32[2800,128]{1,0:T(8,128)S(1)}, f32[2800,128]{1,0:T(8,128)S(1)}, f32[640,128...) custom-call(f32[2800,128]{1,0:T(8,128)S(1)} %get-tuple-element.89.f, ...), custom_call_target="tpu_custom_call" | custom-call | bytes 18000000 | tf_op jit(solution)/shard_map/pallas_call | solution.py:49
  138.4 0.0 collective-permute-done.6.ylo
  138.4 1.3 collective-permute-done.7.yhi
  139.7 0.1 shard_map.71
  139.9 2.1 %collective-permute-start.12 = (f32[360,128]{1,0:T(8,128)S(1)}, f32[360,128]{1,0:T(8,128)S(1)}, u32[]{:S(2)}, u32[]{:S(2)}) collective-permute-start(f32[360,128]{1,0:T(8,128)S(1)} %get-tuple-element.108), channel_id=1, source_target_pairs={{0,32},{32,64},{64,96},{96,128},{128,160},{160,192},{192,224},{1,3... | collective-permute-start | bytes 552968 | tf_op jit(solution)/shard_map/ppermute | solution.py:666
  142.0 3.2 %collective-permute-start.13 = (f32[360,128]{1,0:T(8,128)S(1)}, f32[360,128]{1,0:T(8,128)S(1)}, u32[]{:S(2)}, u32[]{:S(2)}) collective-permute-start(f32[360,128]{1,0:T(8,128)S(1)} %get-tuple-element.109), channel_id=1, source_target_pairs={{32,0},{64,32},{96,64},{128,96},{160,128},{192,160},{224,192},{33,... | collective-permute-start | bytes 552968 | tf_op jit(solution)/shard_map/ppermute | solution.py:666
  145.2 2.9 %collective-permute-start.8 = (f32[288,128]{1,0:T(8,128)S(1)}, f32[288,128]{1,0:T(8,128)S(1)}, u32[]{:S(2)}, u32[]{:S(2)}) collective-permute-start(f32[288,128]{1,0:T(8,128)S(1)} %get-tuple-element.97), channel_id=1, source_target_pairs={{0,8},{8,16},{16,24},{1,9},{9,17},{17,25},{2,10},{10,18},{18,26},{... | collective-permute-start | bytes 442376 | tf_op jit(solution)/shard_map/ppermute | solution.py:666
  148.1 1.3 collective-permute-start.9
  149.4 1.0 collective-permute-done.8.ylo
  150.4 3.6 %collective-permute-done.9.yhi = f32[288,128]{1,0:T(8,128)S(1)} collective-permute-done((f32[288,128]{1,0:T(8,128)S(1)}, f32[288,128]{1,0:T(8,128)S(1)}, u32[]{:S(2)}, u32[]{:S(2)}) %collective-permute-start.9) | collective-permute-done | bytes 147488 | tf_op jit(solution)/shard_map/ppermute | solution.py:666
  154.0 0.3 shard_map.69
  154.3 3.4 %collective-permute-start.10 = (f32[360,128]{1,0:T(8,128)S(1)}, f32[360,128]{1,0:T(8,128)S(1)}, u32[]{:S(2)}, u32[]{:S(2)}) collective-permute-start(f32[360,128]{1,0:T(8,128)S(1)} %get-tuple-element.100), channel_id=1, source_target_pairs={{0,32},{32,64},{64,96},{96,128},{128,160},{160,192},{192,224},{1,3... | collective-permute-start | bytes 552968 | tf_op jit(solution)/shard_map/ppermute | solution.py:666
  157.7 1.9 %collective-permute-start.11 = (f32[360,128]{1,0:T(8,128)S(1)}, f32[360,128]{1,0:T(8,128)S(1)}, u32[]{:S(2)}, u32[]{:S(2)}) collective-permute-start(f32[360,128]{1,0:T(8,128)S(1)} %get-tuple-element.101), channel_id=1, source_target_pairs={{32,0},{64,32},{96,64},{128,96},{160,128},{192,160},{224,192},{33,... | collective-permute-start | bytes 552968 | tf_op jit(solution)/shard_map/ppermute | solution.py:666
  159.7 0.0 collective-permute-done.12.xlo
  159.7 0.0 collective-permute-done.13.xhi
  159.7 1.1 shard_map.72
  160.8 6.0 %collective-permute-start.16 = (f32[600,128]{1,0:T(8,128)S(1)}, f32[600,128]{1,0:T(8,128)S(1)}, u32[]{:S(2)}, u32[]{:S(2)}) collective-permute-start(f32[600,128]{1,0:T(8,128)S(1)} %get-tuple-element.124), channel_id=1, source_target_pairs={{0,1},{1,2},{2,3},{3,4},{4,5},{5,6},{6,7},{8,9},{9,10},{10,11},{11... | collective-permute-start | bytes 921608 | tf_op jit(solution)/shard_map/ppermute | solution.py:666
  166.8 1.9 %collective-permute-start.17 = (f32[600,128]{1,0:T(8,128)S(1)}, f32[600,128]{1,0:T(8,128)S(1)}, u32[]{:S(2)}, u32[]{:S(2)}) collective-permute-start(f32[600,128]{1,0:T(8,128)S(1)} %get-tuple-element.125), channel_id=1, source_target_pairs={{1,0},{2,1},{3,2},{4,3},{5,4},{6,5},{7,6},{9,8},{10,9},{11,10},{12... | collective-permute-start | bytes 921608 | tf_op jit(solution)/shard_map/ppermute | solution.py:666
  168.8 0.7 shard_map.70
  169.5 2.3 %shard_map.73 = (f32[1120,128]{1,0:T(8,128)S(1)}, f32[1120,128]{1,0:T(8,128)S(1)}, f32[1120,128]{1,0:T(8,128)S(1)}, f32[1120,128]{1,0:T(8,128)S(1)}) custom-call(f32[2000,128]{1,0:T(8,128)S(1)} %get-tuple-element.110.ec), custom_call_target="tpu_custom_call" | custom-call | bytes 6000000 | tf_op jit(solution)/shard_map/pallas_call | solution.py:49
  171.8 0.0 collective-permute-done.10.xlo
  171.8 0.5 shard_map.74
  172.3 3.6 %collective-permute-start.14 = (f32[280,128]{1,0:T(8,128)S(1)}, f32[280,128]{1,0:T(8,128)S(1)}, u32[]{:S(2)}, u32[]{:S(2)}) collective-permute-start(f32[280,128]{1,0:T(8,128)S(1)} %get-tuple-element.118), channel_id=1, source_target_pairs={{0,1},{1,2},{2,3},{3,4},{4,5},{5,6},{6,7},{8,9},{9,10},{10,11},{11... | collective-permute-start | bytes 430088 | tf_op jit(solution)/shard_map/ppermute | solution.py:666
  176.0 2.1 %collective-permute-start.15 = (f32[280,128]{1,0:T(8,128)S(1)}, f32[280,128]{1,0:T(8,128)S(1)}, u32[]{:S(2)}, u32[]{:S(2)}) collective-permute-start(f32[280,128]{1,0:T(8,128)S(1)} %get-tuple-element.119), channel_id=1, source_target_pairs={{1,0},{2,1},{3,2},{4,3},{5,4},{6,5},{7,6},{9,8},{10,9},{11,10},{12... | collective-permute-start | bytes 430088 | tf_op jit(solution)/shard_map/ppermute | solution.py:666
  178.1 4.8 %shard_map.75 = (f32[1120,128]{1,0:T(8,128)S(1)}, f32[1120,128]{1,0:T(8,128)S(1)}, f32[1120,128]{1,0:T(8,128)S(1)}, f32[1120,128]{1,0:T(8,128)S(1)}, f32[1120,128]{1,0:T(8,128)S(1)}) custom-call(f32[1120,128]{1,0:T(8,128)S(1)} %get-tuple-element.120.ox, f32[1120,128]{1,0:T(8,128)S(1)} %get-tuple-element.121.oy, f32[1120,128]{1,0:T(8,128)S(1)} %get-tuple-element.122.oz, ...), custom_call_target="tpu_custom_call" | custom-call | bytes 15000000 | tf_op jit(solution)/shard_map/pallas_call | solution.py:49
  182.9 8.5 %shard_map.76 = (f32[64,32,64]{2,1,0:T(8,128)}, f32[64,32,64]{2,1,0:T(8,128)}) custom-call(f32[1000,128]{1,0:T(8,128)S(1)} %get-tuple-element.117.rm, f32[2800,128]{1,0:T(8,128)S(1)} %get-tuple-element.102.vs, f32[360,128]{1,0:T(8,128)S(1)} %collective-permute-done.10.xlo, f32[360,128]{1,0:T(8,128)S(1)} %collective-permute-done.11.xhi, ...), custom_call_target="tpu_custom_call" | custom-call | bytes 24000000 | tf_op jit(solution)/shard_map/pallas_call | solution.py:49
  (8 shorter events, 0.0 us)
Async XLA Ops:
  94.9 6.4 %collective-permute-start = (f32[224,128]{1,0:T(8,128)S(1)}, f32[224,128]{1,0:T(8,128)S(1)}, u32[]{:S(2)}, u32[]{:S(2)}) collective-permute-start(f32[224,128]{1,0:T(8,128)S(1)} %get-tuple-element.71), channel_id=1, source_target_pairs={{0,8},{8,16},{16,24},{1,9},{9,17},{17,25},{2,10},{10,18},{18,26},{... | collective-permute-start | bytes 344072 | tf_op jit(solution)/shard_map/ppermute | solution.py:666
  97.4 5.5 %collective-permute-start.1 = (f32[224,128]{1,0:T(8,128)S(1)}, f32[224,128]{1,0:T(8,128)S(1)}, u32[]{:S(2)}, u32[]{:S(2)}) collective-permute-start(f32[224,128]{1,0:T(8,128)S(1)} %get-tuple-element.72), channel_id=1, source_target_pairs={{8,0},{16,8},{24,16},{9,1},{17,9},{25,17},{10,2},{18,10},{26,18},{... | collective-permute-start | bytes 344072 | tf_op jit(solution)/shard_map/ppermute | solution.py:666
  103.1 7.7 %collective-permute-start.2 = (f32[160,128]{1,0:T(8,128)S(1)}, f32[160,128]{1,0:T(8,128)S(1)}, u32[]{:S(2)}, u32[]{:S(2)}) collective-permute-start(f32[160,128]{1,0:T(8,128)S(1)} %get-tuple-element.78), channel_id=1, source_target_pairs={{0,32},{32,64},{64,96},{96,128},{128,160},{160,192},{192,224},{1,3... | collective-permute-start | bytes 245768 | tf_op jit(solution)/shard_map/ppermute | solution.py:666
  105.6 5.2 %collective-permute-start.3 = (f32[160,128]{1,0:T(8,128)S(1)}, f32[160,128]{1,0:T(8,128)S(1)}, u32[]{:S(2)}, u32[]{:S(2)}) collective-permute-start(f32[160,128]{1,0:T(8,128)S(1)} %get-tuple-element.79), channel_id=1, source_target_pairs={{32,0},{64,32},{96,64},{128,96},{160,128},{192,160},{224,192},{33,... | collective-permute-start | bytes 245768 | tf_op jit(solution)/shard_map/ppermute | solution.py:666
  111.3 12.4 %collective-permute-start.4 = (f32[160,128]{1,0:T(8,128)S(1)}, f32[160,128]{1,0:T(8,128)S(1)}, u32[]{:S(2)}, u32[]{:S(2)}) collective-permute-start(f32[160,128]{1,0:T(8,128)S(1)} %get-tuple-element.82), channel_id=1, source_target_pairs={{0,1},{1,2},{2,3},{3,4},{4,5},{5,6},{6,7},{8,9},{9,10},{10,11},{11... | collective-permute-start | bytes 245768 | tf_op jit(solution)/shard_map/ppermute | solution.py:666
  120.6 5.8 %collective-permute-start.5 = (f32[160,128]{1,0:T(8,128)S(1)}, f32[160,128]{1,0:T(8,128)S(1)}, u32[]{:S(2)}, u32[]{:S(2)}) collective-permute-start(f32[160,128]{1,0:T(8,128)S(1)} %get-tuple-element.83), channel_id=1, source_target_pairs={{1,0},{2,1},{3,2},{4,3},{5,4},{6,5},{7,6},{9,8},{10,9},{11,10},{12... | collective-permute-start | bytes 245768 | tf_op jit(solution)/shard_map/ppermute | solution.py:666
  129.9 8.5 %collective-permute-start.6 = (f32[288,128]{1,0:T(8,128)S(1)}, f32[288,128]{1,0:T(8,128)S(1)}, u32[]{:S(2)}, u32[]{:S(2)}) collective-permute-start(f32[288,128]{1,0:T(8,128)S(1)} %get-tuple-element.87), channel_id=1, source_target_pairs={{0,8},{8,16},{16,24},{1,9},{9,17},{17,25},{2,10},{10,18},{18,26},{... | collective-permute-start | bytes 442376 | tf_op jit(solution)/shard_map/ppermute | solution.py:666
  132.7 7.0 %collective-permute-start.7 = (f32[288,128]{1,0:T(8,128)S(1)}, f32[288,128]{1,0:T(8,128)S(1)}, u32[]{:S(2)}, u32[]{:S(2)}) collective-permute-start(f32[288,128]{1,0:T(8,128)S(1)} %get-tuple-element.88), channel_id=1, source_target_pairs={{8,0},{16,8},{24,16},{9,1},{17,9},{25,17},{10,2},{18,10},{26,18},{... | collective-permute-start | bytes 442376 | tf_op jit(solution)/shard_map/ppermute | solution.py:666
  139.9 19.8 %collective-permute-start.12 = (f32[360,128]{1,0:T(8,128)S(1)}, f32[360,128]{1,0:T(8,128)S(1)}, u32[]{:S(2)}, u32[]{:S(2)}) collective-permute-start(f32[360,128]{1,0:T(8,128)S(1)} %get-tuple-element.108), channel_id=1, source_target_pairs={{0,32},{32,64},{64,96},{96,128},{128,160},{160,192},{192,224},{1,3... | collective-permute-start | bytes 552968 | tf_op jit(solution)/shard_map/ppermute | solution.py:666
  142.0 17.7 %collective-permute-start.13 = (f32[360,128]{1,0:T(8,128)S(1)}, f32[360,128]{1,0:T(8,128)S(1)}, u32[]{:S(2)}, u32[]{:S(2)}) collective-permute-start(f32[360,128]{1,0:T(8,128)S(1)} %get-tuple-element.109), channel_id=1, source_target_pairs={{32,0},{64,32},{96,64},{128,96},{160,128},{192,160},{224,192},{33,... | collective-permute-start | bytes 552968 | tf_op jit(solution)/shard_map/ppermute | solution.py:666
  145.2 5.3 %collective-permute-start.8 = (f32[288,128]{1,0:T(8,128)S(1)}, f32[288,128]{1,0:T(8,128)S(1)}, u32[]{:S(2)}, u32[]{:S(2)}) collective-permute-start(f32[288,128]{1,0:T(8,128)S(1)} %get-tuple-element.97), channel_id=1, source_target_pairs={{0,8},{8,16},{16,24},{1,9},{9,17},{17,25},{2,10},{10,18},{18,26},{... | collective-permute-start | bytes 442376 | tf_op jit(solution)/shard_map/ppermute | solution.py:666
  148.1 5.9 %collective-permute-start.9 = (f32[288,128]{1,0:T(8,128)S(1)}, f32[288,128]{1,0:T(8,128)S(1)}, u32[]{:S(2)}, u32[]{:S(2)}) collective-permute-start(f32[288,128]{1,0:T(8,128)S(1)} %get-tuple-element.98), channel_id=1, source_target_pairs={{8,0},{16,8},{24,16},{9,1},{17,9},{25,17},{10,2},{18,10},{26,18},{... | collective-permute-start | bytes 442376 | tf_op jit(solution)/shard_map/ppermute | solution.py:666
  154.3 17.5 %collective-permute-start.10 = (f32[360,128]{1,0:T(8,128)S(1)}, f32[360,128]{1,0:T(8,128)S(1)}, u32[]{:S(2)}, u32[]{:S(2)}) collective-permute-start(f32[360,128]{1,0:T(8,128)S(1)} %get-tuple-element.100), channel_id=1, source_target_pairs={{0,32},{32,64},{64,96},{96,128},{128,160},{160,192},{192,224},{1,3... | collective-permute-start | bytes 552968 | tf_op jit(solution)/shard_map/ppermute | solution.py:666
  157.7 14.1 %collective-permute-start.11 = (f32[360,128]{1,0:T(8,128)S(1)}, f32[360,128]{1,0:T(8,128)S(1)}, u32[]{:S(2)}, u32[]{:S(2)}) collective-permute-start(f32[360,128]{1,0:T(8,128)S(1)} %get-tuple-element.101), channel_id=1, source_target_pairs={{32,0},{64,32},{96,64},{128,96},{160,128},{192,160},{224,192},{33,... | collective-permute-start | bytes 552968 | tf_op jit(solution)/shard_map/ppermute | solution.py:666
  160.8 17.3 %collective-permute-start.16 = (f32[600,128]{1,0:T(8,128)S(1)}, f32[600,128]{1,0:T(8,128)S(1)}, u32[]{:S(2)}, u32[]{:S(2)}) collective-permute-start(f32[600,128]{1,0:T(8,128)S(1)} %get-tuple-element.124), channel_id=1, source_target_pairs={{0,1},{1,2},{2,3},{3,4},{4,5},{5,6},{6,7},{8,9},{9,10},{10,11},{11... | collective-permute-start | bytes 921608 | tf_op jit(solution)/shard_map/ppermute | solution.py:666
  166.8 11.3 %collective-permute-start.17 = (f32[600,128]{1,0:T(8,128)S(1)}, f32[600,128]{1,0:T(8,128)S(1)}, u32[]{:S(2)}, u32[]{:S(2)}) collective-permute-start(f32[600,128]{1,0:T(8,128)S(1)} %get-tuple-element.125), channel_id=1, source_target_pairs={{1,0},{2,1},{3,2},{4,3},{5,4},{6,5},{7,6},{9,8},{10,9},{11,10},{12... | collective-permute-start | bytes 921608 | tf_op jit(solution)/shard_map/ppermute | solution.py:666
  172.3 10.6 %collective-permute-start.14 = (f32[280,128]{1,0:T(8,128)S(1)}, f32[280,128]{1,0:T(8,128)S(1)}, u32[]{:S(2)}, u32[]{:S(2)}) collective-permute-start(f32[280,128]{1,0:T(8,128)S(1)} %get-tuple-element.118), channel_id=1, source_target_pairs={{0,1},{1,2},{2,3},{3,4},{4,5},{5,6},{6,7},{8,9},{9,10},{10,11},{11... | collective-permute-start | bytes 430088 | tf_op jit(solution)/shard_map/ppermute | solution.py:666
  176.0 6.9 %collective-permute-start.15 = (f32[280,128]{1,0:T(8,128)S(1)}, f32[280,128]{1,0:T(8,128)S(1)}, u32[]{:S(2)}, u32[]{:S(2)}) collective-permute-start(f32[280,128]{1,0:T(8,128)S(1)} %get-tuple-element.119), channel_id=1, source_target_pairs={{1,0},{2,1},{3,2},{4,3},{5,4},{6,5},{7,6},{9,8},{10,9},{11,10},{12... | collective-permute-start | bytes 430088 | tf_op jit(solution)/shard_map/ppermute | solution.py:666
